TPU v7x, 128 devices: a whole 4x4x4 slice. The times are simulated.
128 devices in a mesh: row: 16 (over z_hi, y, core), col: 8 (over z_lo, x).
Axes of the slice: x: 4, y: 4, z: 4 (z_hi: 2, z_lo: 2; z = z_hi * 2 + z_lo), core: 2. Of those that a mesh axis runs over, the one named last changes fastest.
Arguments:
- edge_tensor: float32 [1024, 16, 1024], P('row'), may hold values from -0.0234375 to 0.0234375
- site_tensor: float32 [16, 16, 16, 16], replicated, may hold values from -0.375 to 0.375
- left_isometry: float32 [1024, 16, 1024], P('row'), may hold values from -0.0234375 to 0.0234375
- right_isometry: float32 [512, 16, 1024], P('col', None, 'row'), may hold values from -0.03125 to 0.03125
- cotangent: float32 [512, 16, 1024], P('col', None, 'row'), may hold values from -96 to 96
Outputs:
- edge_gradient: float32 [1024, 16, 1024], P('row', 'col')
- site_gradient: float32 [16, 16, 16, 16], replicated
- left_gradient: float32 [1024, 16, 1024], P('row', 'col')
- right_gradient: float32 [512, 16, 1024], P('col', 'row')
All inputs are finite; a program needn't handle non-finite values.
Results may differ from a plain program's by a relative error of at most 0.0003.
Values sent between devices are 32-bit elements; how exact they have to be, the bound alone decides.
No kernel may reach another device: no remote copies, remote signals or barrier semaphores. Data moves between devices by JAX's collectives and lax.ppermute only.
A program may use at most 192 MiB of HBM per device.

v0:
```python
import functools

import jax
import jax.numpy as jnp
import numpy as np
from jax import lax
from jax.experimental import pallas as pl
from jax.experimental.pallas import tpu as pltpu
from jax.sharding import PartitionSpec as P

F32, BF16 = jnp.float32, jnp.bfloat16
NN = (((1,), (0,)), ((), ()))
NT = (((1,), (1,)), ((), ()))
TN = (((0,), (0,)), ((), ()))
PARAMS = pltpu.CompilerParams(vmem_limit_bytes=28 << 20)
ROWS = 256
CHUNKS = 4
WIDTH = 512


def split(value):
    high = value.astype(BF16)
    return high, (value - high.astype(F32)).astype(BF16)


def dot3(left, right, dims):
    dot = functools.partial(lax.dot_general, dimension_numbers=dims, preferred_element_type=F32)
    return dot(left[0], right[0]) + (dot(left[0], right[1]) + dot(left[1], right[0]))


def swap_into(value, high_ref, low_ref):
    lane = lax.broadcasted_iota(jnp.int32, (16, 128), 1)
    for pair in range(8):
        for tile in range(8):
            first = value[32 * pair : 32 * pair + 16, 128 * tile : 128 * tile + 128]
            second = value[32 * pair + 16 : 32 * pair + 32, 128 * tile : 128 * tile + 128]
            even = jnp.where(lane < 64, first, pltpu.roll(second, 64, 1))
            odd = jnp.where(lane < 64, pltpu.roll(first, 64, 1), second)
            columns = slice(128 * pair, 128 * pair + 128)
            for start, part in ((16 * tile, even), (128 + 16 * tile, odd)):
                high, low = split(part)
                high_ref[start : start + 16, columns] = high
                low_ref[start : start + 16, columns] = low


def unswap_into(value, high_ref, low_ref):
    lane = lax.broadcasted_iota(jnp.int32, (16, 128), 1)
    for pair in range(8):
        for tile in range(8):
            columns = slice(128 * pair, 128 * pair + 128)
            even = value[16 * tile : 16 * tile + 16, columns]
            odd = value[128 + 16 * tile : 128 + 16 * tile + 16, columns]
            first = jnp.where(lane < 64, even, pltpu.roll(odd, 64, 1))
            second = jnp.where(lane < 64, pltpu.roll(even, 64, 1), odd)
            columns = slice(128 * tile, 128 * tile + 128)
            for start, part in ((32 * pair, first), (32 * pair + 16, second)):
                high, low = split(part)
                high_ref[start : start + 16, columns] = high
                low_ref[start : start + 16, columns] = low


def assemble(offsets_ref, piece_refs, whole_ref, sems, high_ref, low_ref):
    block = 64
    copies = []
    count = 0
    for piece in piece_refs:
        for part in range(piece.shape[0] // block):
            start = pl.multiple_of(offsets_ref[count], block)
            target = whole_ref.at[pl.ds(start, block)]
            copies.append((pltpu.make_async_copy(piece.at[pl.ds(part * block, block)], target, sems.at[count]), start))
            count += 1
    for copy, _ in copies:
        copy.start()
    for copy, start in copies:
        copy.wait()

        def some(index, carry, start=start):
            rows = pl.ds(pl.multiple_of(start + index * 16, 16), 16)
            high, low = split(whole_ref[rows, :])
            high_ref[rows, :] = high
            low_ref[rows, :] = low
            return carry

        lax.fori_loop(0, block // 16, some, 0)


def chunk_of(ref):
    return ref.at[pl.ds(pl.multiple_of(pl.program_id(0) * ROWS, ROWS), ROWS)]


def back_kernel(pieces, offsets_ref, *refs):
    piece_refs = refs[:pieces]
    rows_ref, site_ref = refs[pieces : pieces + 2]
    whole_high, whole_low, back_high, back_low, swapped_high, swapped_low, whole, sems = refs[pieces + 2 :]

    @pl.when(pl.program_id(0) == 0)
    def _():
        assemble(offsets_ref, piece_refs, whole, sems, whole_high, whole_low)

    section = dot3(split(rows_ref[...]), (whole_high[...], whole_low[...]), NN)
    swapped_high, swapped_low = chunk_of(swapped_high), chunk_of(swapped_low)
    swap_into(section, swapped_high, swapped_low)
    mixed = dot3(split(site_ref[...]), (swapped_high[...], swapped_low[...]), NN)
    unswap_into(mixed, chunk_of(back_high), chunk_of(back_low))


def block_of(ref):
    return ref.at[pl.ds(pl.multiple_of(pl.program_id(1) * WIDTH, WIDTH), WIDTH)]


def place(terms, sources_ref, staged, ahead_ref, behind_ref, kept_ref):
    for a in range(16):
        staged[:, a, :] = terms[16 * a : 16 * a + 16, :]
    slot = 0
    for ref in (ahead_ref, behind_ref, kept_ref):
        for block in range(ref.shape[0]):
            ref[block] = staged[pl.ds(sources_ref[slot] * 2, 2)]
            slot += 1


def edge_kernel(pieces, offsets_ref, sources_ref, *refs):
    piece_refs = refs[:pieces]
    back_high_ref, back_low_ref = refs[pieces : pieces + 2]
    whole_high, whole_low, ahead_ref, behind_ref, kept_ref, whole, staged, sems = refs[pieces + 2 :]

    @pl.when((pl.program_id(0) == 0) & (pl.program_id(1) == 0))
    def _():
        assemble(offsets_ref, piece_refs, whole, sems, whole_high, whole_low)

    rows = chunk_of(back_high_ref)[...], chunk_of(back_low_ref)[...]
    terms = dot3(rows, (block_of(whole_high)[...], block_of(whole_low)[...]), NT)
    place(terms, sources_ref, staged, ahead_ref, behind_ref, kept_ref)


def first_kernel(
    edge_ref,
    right_high_ref,
    right_low_ref,
    site_matrix_ref,
    swapped_high_ref,
    swapped_low_ref,
    second_high_ref,
    second_low_ref,
    site_ref,
    first_high,
    first_low,
):
    first = dot3(split(edge_ref[...]), (right_high_ref[...], right_low_ref[...]), NN)
    swap_into(first, first_high, first_low)
    mixed = dot3(split(site_matrix_ref[...]), (first_high[...], first_low[...]), TN)
    unswap_into(mixed, chunk_of(second_high_ref), chunk_of(second_low_ref))
    swapped = chunk_of(swapped_high_ref)[...], chunk_of(swapped_low_ref)[...]
    site = dot3((first_high[...], first_low[...]), swapped, NT)

    @pl.when(pl.program_id(0) == 0)
    def _():
        site_ref[...] = site

    @pl.when(pl.program_id(0) > 0)
    def _():
        site_ref[...] += site


def left_kernel(
    sources_ref, second_high_ref, second_low_ref, high_ref, low_ref, ahead_ref, behind_ref, kept_ref, staged
):
    rows = chunk_of(second_high_ref)[...], chunk_of(second_low_ref)[...]
    terms = dot3(rows, (block_of(high_ref)[...], block_of(low_ref)[...]), NT)
    place(terms, sources_ref, staged, ahead_ref, behind_ref, kept_ref)


def right_kernel(places_ref, back_high_ref, back_low_ref, edge_ref, own_ref, other_ref, turned_high, turned_low, placed):
    @pl.when(pl.program_id(0) == 0)
    def _():
        def turn(chunk, carry):
            rows = pl.ds(pl.multiple_of(chunk * ROWS, ROWS), ROWS)
            turned_high[:, rows] = back_high_ref[rows, :].T
            turned_low[:, rows] = back_low_ref[rows, :].T
            return carry

        lax.fori_loop(0, CHUNKS, turn, 0)

    terms = dot3((turned_high[...], turned_low[...]), split(edge_ref[...]), NN)
    for block in range(16):
        start = pl.multiple_of(places_ref[block], 64)
        placed[pl.ds(start, 64), :] = terms[64 * block : 64 * block + 64, :]
    own_ref[...] = placed[:512, :]
    other_ref[...] = placed[512:, :]


def resident(shape):
    return pl.BlockSpec(shape, lambda *_: (0,) * len(shape))


OUTSIDE = pl.BlockSpec(memory_space=pltpu.HBM)
HELD = pl.BlockSpec(memory_space=pltpu.VMEM)
SQUARE = jax.ShapeDtypeStruct((1024, 1024), BF16)
CHUNK = pl.BlockSpec((ROWS, 1024), lambda i, *_: (i, 0))


def back_call(offsets, pieces, rows, site_matrix):
    return pl.pallas_call(
        functools.partial(back_kernel, len(pieces)),
        out_shape=(SQUARE,) * 6,
        grid_spec=pltpu.PrefetchScalarGridSpec(
            num_scalar_prefetch=1,
            grid=(CHUNKS,),
            in_specs=[OUTSIDE] * len(pieces) + [CHUNK, resident((256, 256))],
            out_specs=[HELD] * 6,
            scratch_shapes=[pltpu.VMEM((1024, 1024), F32), pltpu.SemaphoreType.DMA((16,))],
        ),
        compiler_params=PARAMS,
        name="back",
    )(offsets, *pieces, rows, site_matrix)


BLOCKS = tuple(jax.ShapeDtypeStruct((count, 2, 64, 1024), F32) for count in (2, 2, 4))
BLOCK_SPECS = [pl.BlockSpec((count, 2, 16, WIDTH), lambda i, j, *_: (0, 0, i, j)) for count in (2, 2, 4)]


def edge_call(offsets, sources, pieces, back_split):
    return pl.pallas_call(
        functools.partial(edge_kernel, len(pieces)),
        out_shape=(SQUARE, SQUARE, *BLOCKS),
        grid_spec=pltpu.PrefetchScalarGridSpec(
            num_scalar_prefetch=2,
            grid=(CHUNKS, 1024 // WIDTH),
            in_specs=[OUTSIDE] * len(pieces) + [HELD, HELD],
            out_specs=[HELD] * 2 + BLOCK_SPECS,
            scratch_shapes=[
                pltpu.VMEM((1024, 1024), F32),
                pltpu.VMEM((16, 16, WIDTH), F32),
                pltpu.SemaphoreType.DMA((16,)),
            ],
        ),
        compiler_params=PARAMS,
        name="edge",
    )(offsets, sources, *pieces, *back_split)


def first_call(edge_rows, right_split, site_matrix, swapped_split):
    return pl.pallas_call(
        first_kernel,
        out_shape=(SQUARE, SQUARE, jax.ShapeDtypeStruct((256, 256), F32)),
        grid=(CHUNKS,),
        in_specs=[CHUNK] + [HELD] * 2 + [resident((256, 256))] + [HELD] * 2,
        out_specs=[HELD, HELD, resident((256, 256))],
        scratch_shapes=[pltpu.VMEM((ROWS, 1024), BF16)] * 2,
        compiler_params=PARAMS,
        name="first",
    )(edge_rows, *right_split, site_matrix, *swapped_split)


def left_call(sources, second_split, cotangent_split):
    return pl.pallas_call(
        left_kernel,
        out_shape=BLOCKS,
        grid_spec=pltpu.PrefetchScalarGridSpec(
            num_scalar_prefetch=1,
            grid=(CHUNKS, 1024 // WIDTH),
            in_specs=[HELD] * 4,
            out_specs=BLOCK_SPECS,
            scratch_shapes=[pltpu.VMEM((16, 16, WIDTH), F32)],
        ),
        compiler_params=PARAMS,
        name="left",
    )(sources, *second_split, *cotangent_split)


def right_call(places, back_split, edge_rows):
    column = lambda rows: pl.BlockSpec((rows, 256), lambda i, *_: (0, i))
    return pl.pallas_call(
        right_kernel,
        out_shape=(jax.ShapeDtypeStruct((512, 1024), F32),) * 2,
        grid_spec=pltpu.PrefetchScalarGridSpec(
            num_scalar_prefetch=1,
            grid=(4,),
            in_specs=[HELD] * 2 + [column(1024)],
            out_specs=[column(512)] * 2,
            scratch_shapes=[pltpu.VMEM((1024, 1024), BF16)] * 2 + [pltpu.VMEM((1024, 256), F32)],
        ),
        compiler_params=PARAMS,
        name="right",
    )(places, *back_split, edge_rows)


def row_permute(value, z, y, core):
    pairs = []
    for source in range(16):
        there = ((source // 8) ^ z) * 8 + ((source // 2 + y) % 4) * 2 + ((source % 2) ^ core)
        pairs.append((source, there))
    return lax.ppermute(value, "row", pairs)


def col_permute(value, z, x):
    return lax.ppermute(value, "col", [(i, ((i // 4) ^ z) * 4 + (i + x) % 4) for i in range(8)])


def col_reduce(ahead, behind, kept):
    from_behind = col_permute(ahead, 0, 1)
    from_ahead = col_permute(behind, 0, 3)
    far_behind = col_permute(kept[0] + from_behind[0], 0, 1)
    far_ahead = col_permute(kept[1] + from_ahead[0], 0, 3)
    other = kept[3] + from_behind[1] + far_ahead
    same = kept[2] + from_ahead[1] + far_behind
    return jnp.transpose(same + col_permute(other, 1, 0), (1, 0, 2))


def dense(value):
    cols, bond, width = value.shape
    return jnp.transpose(value.reshape(cols, 2, 8, width), (3, 2, 1, 0)).reshape(width, bond * cols)


def take(value, index):
    return lax.dynamic_index_in_dim(value, index, 0, keepdims=False, allow_negative_indices=False)


def on_device(edge_tensor, site_tensor, left_isometry, right_isometry, cotangent):
    row = lax.axis_index("row").astype(jnp.int32)
    col = lax.axis_index("col").astype(jnp.int32)
    z, y, core = row >> 3, (row >> 1) & 3, row & 1
    edge_rows = edge_tensor.reshape(1024, 1024)
    left_rows = left_isometry.reshape(1024, 1024)

    def offset_of(other_z, steps, other_core):
        other_z, steps, other_core = (np.array(list(v), np.int32) for v in (other_z, steps, other_core))
        return ((z ^ other_z) * 8 + ((y - steps) & 3) * 2 + (core ^ other_core)) * 64

    site_matrix = jnp.transpose(site_tensor, (2, 1, 3, 0)).reshape(256, 256)
    order = [(j, steps, c) for c in (0, 1) for j in (0, 1) for steps in (0, 1, 3, 2)]
    cotangent_offsets = offset_of(*zip(*order))
    order = [(j, steps, c) for c in (0, 1) for steps in (0, 1, 3, 2) for j in (0, 1)]
    isometry_offsets = offset_of(*zip(*order))
    steps = np.array([2, 1, 2, 3, 1, 3, 0, 0], np.int32)
    others = np.array([0, 1, 1, 0, 0, 1, 0, 1], np.int32)
    sources = ((col >> 2) ^ others) * 4 + ((col + steps) & 3)
    blocks = np.array([(i % 2) * 8 + i // 2 for i in range(16)], np.int32)
    places = (((blocks & 1) ^ core) * 8 + (((blocks >> 1) - y) & 3) * 2 + ((blocks >> 3) ^ z)) * 64
    corners = [(core * 2 + z) ^ k for k in range(4)]
    ahead = [(y + k) & 3 for k in range(4)]
    first_row, at_low_z, at_low_core = ((4 - y) & 3) * 16, z == 0, core == 0

    early = dense(cotangent)
    early, right_isometry = lax.optimization_barrier((early, right_isometry))
    other = row_permute(early, 1, 0, 0)
    nearest = [row_permute(early, 0, steps, 0) for steps in (1, 3, 2)]
    values = (site_matrix, cotangent_offsets, isometry_offsets, sources, places)
    indices = (*corners, *ahead, first_row, at_low_z, at_low_core)
    other, values, indices = lax.optimization_barrier((other, values, indices))
    site_matrix, cotangent_offsets, isometry_offsets, sources, places = values
    corners, ahead, (first_row, at_low_z, at_low_core) = indices[:4], indices[4:8], indices[8:]
    own = dense(right_isometry)
    pair = jnp.concatenate([own, row_permute(own, 1, 0, 0)], 0)
    pieces = [early, *nearest, other, *(row_permute(other, 0, steps, 0) for steps in (1, 3, 2))]
    pairs = [pair] + [row_permute(pair, 0, steps, 0) for steps in (1, 3, 2)]

    pieces += [row_permute(piece, 0, 0, 1) for piece in pieces]
    cotangent_high, cotangent_low, *rest = back_call(cotangent_offsets, pieces, left_rows, site_matrix)
    back_split, swapped_split = rest[:2], rest[2:]

    pairs += [row_permute(piece, 0, 0, 1) for piece in pairs]
    right_high, right_low, *edge_terms = edge_call(isometry_offsets, sources, pairs, back_split)
    edge_gradient = col_reduce(*edge_terms)
    *second_split, site_terms = first_call(edge_rows, (right_high, right_low), site_matrix, swapped_split)
    left_terms = left_call(sources, second_split, (cotangent_high, cotangent_low))
    left_gradient = col_reduce(*left_terms)

    right_own, right_other = right_call(places, back_split, edge_rows)

    part = site_terms.reshape(4, 64, 256)
    sends = [row_permute(take(part, corners[k]), k & 1, 0, k >> 1) for k in (1, 2, 3)]
    part = take(part, corners[0]) + sum(sends)
    part = part.reshape(4, 16, 256)
    part = take(part, ahead[0]) + sum(row_permute(take(part, ahead[k]), 0, k, 0) for k in (1, 2, 3))
    part = part + sum(col_permute(part, 0, k) for k in (1, 2, 3))
    part = part + col_permute(part, 1, 0)
    ring = [part] + [row_permute(part, 0, k, 0) for k in (3, 2, 1)]
    ring = jnp.concatenate(ring + ring, 0)
    part = lax.dynamic_slice(ring, (first_row, 0), (64, 256), allow_negative_indices=False)
    near, across, far = (row_permute(part, k & 1, 0, k >> 1) for k in (1, 2, 3))
    low = jnp.where(at_low_z, jnp.concatenate([part, near], 0), jnp.concatenate([near, part], 0))
    high = jnp.where(at_low_z, jnp.concatenate([across, far], 0), jnp.concatenate([far, across], 0))
    part = jnp.where(at_low_core, jnp.concatenate([low, high], 0), jnp.concatenate([high, low], 0))
    site_gradient = jnp.transpose(part.reshape(16, 16, 16, 16), (3, 1, 0, 2))

    right_own = right_own.reshape(4, 2, 64, 1024)
    received = row_permute(right_other, 0, 0, 1).reshape(4, 2, 64, 1024)
    total = [right_own[k] + received[k] for k in range(4)]
    total = total[0] + sum(row_permute(total[k], 0, k, 0) for k in (1, 3, 2))
    right_gradient = total[0] + row_permute(total[1], 1, 0, 0)

    return (
        edge_gradient,
        site_gradient,
        left_gradient,
        right_gradient.reshape(64, 1, 1024),
    )


def solution(mesh):
    in_specs = (
        P("row", None, None),
        P(),
        P("row", None, None),
        P("col", None, "row"),
        P("col", None, "row"),
    )
    out_specs = (P("row", "col", None), P(), P("row", "col", None), P("col", "row", None))

    return jax.shard_map(on_device, mesh=mesh, in_specs=in_specs, out_specs=out_specs, check_vma=False)
```

profile of v0, /device:TPU:1, one launch (start us, length us, event | category | flops | bytes accessed | tf_op | source)
XLA Modules:
  0.0 249.3 jit_solution(11609751344748397344)
XLA Ops:
  0.7 1.7 copy.25
  2.9 4.5 %collective-permute-start = (f32[64,1024]{1,0:T(8,128)S(1)}, f32[64,1024]{1,0:T(8,128)S(1)}, u32[]{:S(2)}, u32[]{:S(2)}) collective-permute-start(f32[64,1024]{1,0:T(8,128)S(1)} %reshape.74.refs_0_), channel_id=1, source_target_pairs={{0,64},{8,72},{16,80},{24,88},{32,96},{40,104},{48,112},{56,120},{... | collective-permute-start | bytes 786440 | tf_op jit(solution)/shard_map/ppermute | solution.py:292
  7.4 1.3 collective-permute-start.9
  8.7 1.4 collective-permute-start.10
  10.1 1.6 collective-permute-start.11
  11.7 2.1 copy.27
  13.9 2.2 reshape.77
  16.3 2.1 copy.26
  18.4 2.5 reshape.75.refs_17_.site_matrix_ref
  20.9 1.9 collective-permute-start.15
  22.8 1.2 collective-permute-done.1
  24.4 2.3 collective-permute-start.13
  26.9 3.4 %collective-permute-start.16 = (f32[64,1024]{1,0:T(8,128)S(1)}, f32[64,1024]{1,0:T(8,128)S(1)}, u32[]{:S(2)}, u32[]{:S(2)}) collective-permute-start(f32[64,1024]{1,0:T(8,128)S(1)} %collective-permute-done.9.refs_1_), channel_id=1, source_target_pairs={{0,8},{8,0},{16,24},{24,16},{32,40},{40,32},{48,56},{56,48},{64,72... | collective-permute-start | bytes 786440 | tf_op jit(solution)/shard_map/ppermute | solution.py:292
  30.4 1.0 constant_dynamic-update-slice_fusion.refs_0_
  32.3 3.9 %collective-permute-start.3 = (f32[128,1024]{1,0:T(8,128)S(1)}, f32[128,1024]{1,0:T(8,128)S(1)}, u32[]{:S(2)}, u32[]{:S(2)}) collective-permute-start(f32[128,1024]{1,0:T(8,128)S(1)} %constant_dynamic-update-slice_fusion.refs_0_), channel_id=1, source_target_pairs={{0,48},{8,56},{16,0},{24,8},{32,16},{40,24},{48,32},{56,40},{64,11... | collective-permute-start | bytes 1572872 | tf_op jit(solution)/shard_map/ppermute | solution.py:292
  36.6 7.1 %collective-permute-start.18 = (f32[64,1024]{1,0:T(8,128)S(1)}, f32[64,1024]{1,0:T(8,128)S(1)}, u32[]{:S(2)}, u32[]{:S(2)}) collective-permute-start(f32[64,1024]{1,0:T(8,128)S(1)} %collective-permute-done.11.refs_3_), channel_id=1, source_target_pairs={{0,8},{8,0},{16,24},{24,16},{32,40},{40,32},{48,56},{56,48},{64,72... | collective-permute-start | bytes 786440 | tf_op jit(solution)/shard_map/ppermute | solution.py:292
  43.7 1.1 collective-permute-done.18.refs_11_
  46.2 16.0 %collective-permute-start.5 = (f32[128,1024]{1,0:T(8,128)S(1)}, f32[128,1024]{1,0:T(8,128)S(1)}, u32[]{:S(2)}, u32[]{:S(2)}) collective-permute-start(f32[128,1024]{1,0:T(8,128)S(1)} %constant_dynamic-update-slice_fusion.refs_0_), channel_id=1, source_target_pairs={{0,8},{8,0},{16,24},{24,16},{32,40},{40,32},{48,56},{56,48},{64,72... | collective-permute-start | bytes 1572872 | tf_op jit(solution)/shard_map/ppermute | solution.py:292
  63.3 3.1 %collective-permute-done.22.refs_15_ = f32[64,1024]{1,0:T(8,128)S(1)} collective-permute-done((f32[64,1024]{1,0:T(8,128)S(1)}, f32[64,1024]{1,0:T(8,128)S(1)}, u32[]{:S(2)}, u32[]{:S(2)}) %collective-permute-start.22) | collective-permute-done | bytes 262176 | tf_op jit(solution)/shard_map/ppermute | solution.py:292
  66.4 2.2 copy-done.1
  68.6 12.9 %back.1 = (bf16[1024,1024]{1,0:T(8,128)(2,1)S(1)}, bf16[1024,1024]{1,0:T(8,128)(2,1)S(1)}, bf16[1024,1024]{1,0:T(8,128)(2,1)S(1)}, bf16[1024,1024]{1,0:T(8,128)(...) custom-call(s32[16]{0:T(128)S(1)} %get-tuple-element.46.offsets_ref, ...), custom_call_target="tpu_custom_call" | custom-call | tf_op jit(solution)/shard_map/back/pallas_call | solution.py:202
  81.6 11.6 %edge.1 = (bf16[1024,1024]{1,0:T(8,128)(2,1)S(1)}, bf16[1024,1024]{1,0:T(8,128)(2,1)S(1)}, f32[2,2,64,1024]{3,2,1,0:T(8,128)S(1)}, f32[2,2,64,1024]{3,2,1,0:T(8,128)S(1)}, f32[4,2,64,1024]{3,2,1,0:T(8,128)S(1)}) custom-call(s32[16]{0:T(128)S(1)} %get-tuple-element.43.offsets_ref, s32[8]{0:T(128)S(1)} %and_add_fusion.sources_ref, ...), custom_call_target="tpu_custom_call" | custom-call | tf_op jit(solution)/shard_map/edge/pallas_call | solution.py:222
  93.1 15.1 %first.1 = (bf16[1024,1024]{1,0:T(8,128)(2,1)S(1)}, bf16[1024,1024]{1,0:T(8,128)(2,1)S(1)}, f32[256,256]{1,0:T(8,128)S(1)}) custom-call(f32[1024,1024]{1,0:T(8,128)S(1)} %bitcast.74, bf16[1024,1024]{1,0:T(8,128)(2,1)S(1)} %get-tuple-element.56.right_high_ref, bf16[1024,1024]{1,0:T(8,128)(2,1)S(1)} %get-tuple-element.57.right_low_ref, ...), custom_call_target="tpu_custom_call" | custom-call | tf_op jit(solution)/shard_map/first/pallas_call | solution.py:242
  108.3 2.2 collective-permute-start.30
  110.5 1.2 collective-permute-start.28
  112.0 2.1 collective-permute-done.30
  114.1 1.4 collective-permute-done.28
  115.6 2.0 collective-permute-start.33
  117.6 1.3 collective-permute-start.32
  118.8 2.5 %collective-permute-done.31 = f32[16,256]{1,0:T(8,128)S(1)} collective-permute-done((f32[16,256]{1,0:T(8,128)S(1)}, f32[16,256]{1,0:T(8,128)S(1)}, u32[]{:S(2)}, u32[]{:S(2)}) %collective-permute-start.31) | collective-permute-done | bytes 16416 | tf_op jit(solution)/shard_map/ppermute | solution.py:292
  121.7 2.5 collective-permute-start.36
  124.2 1.7 collective-permute-start.35
  125.9 2.1 collective-permute-done.34
  129.0 2.2 collective-permute-done.37
  131.2 2.7 %collective-permute-start.38 = (f32[16,256]{1,0:T(8,128)S(1)}, f32[16,256]{1,0:T(8,128)S(1)}, u32[]{:S(2)}, u32[]{:S(2)}) collective-permute-start(f32[16,256]{1,0:T(8,128)S(1)} %get-tuple-element.89), channel_id=1, source_target_pairs={{0,48},{8,56},{16,0},{24,8},{32,16},{40,24},{48,32},{56,40},{64,11... | collective-permute-start | bytes 49160 | tf_op jit(solution)/shard_map/ppermute | solution.py:292
  133.8 10.8 %right.1 = (f32[512,1024]{1,0:T(8,128)S(1)}, f32[512,1024]{1,0:T(8,128)}) custom-call(s32[16]{0:T(128)S(1)} %get-tuple-element.77.places_ref, bf16[1024,1024]{1,0:T(8,128)(2,1)S(1)} %get-tuple-element.49.refs_8_.back_high_ref, bf16[1024,1024]{1,0:T(8,128)(2,1)S(1)} %get-tuple-element.50.refs_9_.back_low_ref, f32[1024,1024]{1,0:T(8,128)S(1)} %bitcast.75), custom_call_target="tpu_custom_call" | custom-call | tf_op jit(solution)/shard_map/right/pallas_call | solution.py:272
  144.6 5.3 %collective-permute-start.49 = (f32[512,1024]{1,0:T(8,128)}, f32[512,1024]{1,0:T(8,128)}, u32[]{:S(2)}, u32[]{:S(2)}) collective-permute-start(f32[512,1024]{1,0:T(8,128)} %get-tuple-element.79), channel_id=1, source_target_pairs={{0,8},{8,0},{16,24},{24,16},{32,40},{40,32},{48,56},{56,48},{64,72... | collective-permute-start | bytes 6291464 | tf_op jit(solution)/shard_map/ppermute | solution.py:292
  150.5 2.4 collective-permute-start.23
  153.2 3.8 %collective-permute-done.39 = f32[16,256]{1,0:T(8,128)S(1)} collective-permute-done((f32[16,256]{1,0:T(8,128)S(1)}, f32[16,256]{1,0:T(8,128)S(1)}, u32[]{:S(2)}, u32[]{:S(2)}) %collective-permute-start.39) | collective-permute-done | bytes 16416 | tf_op jit(solution)/shard_map/ppermute | solution.py:292
  157.0 1.5 collective-permute-start.41
  158.5 10.5 %left.1 = (f32[2,2,64,1024]{3,2,1,0:T(8,128)}, f32[2,2,64,1024]{3,2,1,0:T(8,128)S(1)}, f32[4,2,64,1024]{3,2,1,0:T(8,128)S(1)}) custom-call(s32[8]{0:T(128)S(1)} %and_add_fusion.sources_ref, bf16[1024,1024]{1,0:T(8,128)(2,1)S(1)} %get-tuple-element.70.second_high_ref, bf16[1024,1024]{1,0:T(8,128)(2,1)S(1)} %get-tuple-element.71.second_low_ref, ...), custom_call_target="tpu_custom_call" | custom-call | tf_op jit(solution)/shard_map/left/pallas_call | solution.py:255
  169.1 2.7 %collective-permute-start.44 = (f32[2,2,64,1024]{3,2,1,0:T(8,128)S(1)}, f32[2,2,64,1024]{3,2,1,0:T(8,128)}, u32[]{:S(2)}, u32[]{:S(2)}) collective-permute-start(f32[2,2,64,1024]{3,2,1,0:T(8,128)S(1)} %get-tuple-element.75), channel_id=1, source_target_pairs={{0,3},{1,0},{2,1},{3,2},{4,7},{5,4},{6,5},{7,6},{8,11},{9,8},{10,9... | collective-permute-start | bytes 3145736 | tf_op jit(solution)/shard_map/ppermute | solution.py:296
  171.8 4.6 %collective-permute-done.24 = f32[2,2,64,1024]{3,2,1,0:T(8,128)S(1)} collective-permute-done((f32[2,2,64,1024]{3,2,1,0:T(8,128)S(1)}, f32[2,2,64,1024]{3,2,1,0:T(8,128)S(1)}, u32[]{:S(2)}, u32[]{:S(2)}) %collective-permute-start.24) | collective-permute-done | bytes 1048608 | tf_op jit(solution)/shard_map/ppermute | solution.py:296
  176.4 2.1 collective-permute-start.43
  178.5 1.3 fusion.11
  179.8 2.8 %collective-permute-done.43 = f32[64,256]{1,0:T(8,128)S(1)} collective-permute-done((f32[64,256]{1,0:T(8,128)S(1)}, f32[64,256]{1,0:T(8,128)S(1)}, u32[]{:S(2)}, u32[]{:S(2)}) %collective-permute-start.43) | collective-permute-done | bytes 65568 | tf_op jit(solution)/shard_map/ppermute | solution.py:292
  183.2 2.0 select_n.29
  185.2 3.7 %copy.29 = f32[16,16,16,16]{3,2,1,0:T(8,128)} copy(f32[16,16,16,16]{0,3,1,2:T(8,128)} %bitcast.79) | data formatting | bytes 524288
  189.7 9.3 %collective-permute-done.45 = f32[2,2,64,1024]{3,2,1,0:T(8,128)} collective-permute-done((f32[2,2,64,1024]{3,2,1,0:T(8,128)}, f32[2,2,64,1024]{3,2,1,0:T(8,128)}, u32[]{:S(2)}, u32[]{:S(2)}) %collective-permute-start.45) | collective-permute-done | bytes 1048608 | tf_op jit(solution)/shard_map/ppermute | solution.py:296
  199.0 1.7 fusion.3
  200.6 2.5 collective-permute-start.47
  203.1 6.1 %collective-permute-done.26 = f32[2,64,1024]{2,1,0:T(8,128)} collective-permute-done((f32[2,64,1024]{2,1,0:T(8,128)}, f32[2,64,1024]{2,1,0:T(8,128)}, u32[]{:S(2)}, u32[]{:S(2)}) %collective-permute-start.26) | collective-permute-done | bytes 524320 | tf_op jit(solution)/shard_map/ppermute | solution.py:296
  209.2 1.1 fusion.10
  211.2 2.1 slice_add_fusion.1
  213.6 6.7 %collective-permute-done.47 = f32[2,64,1024]{2,1,0:T(8,128)S(1)} collective-permute-done((f32[2,64,1024]{2,1,0:T(8,128)S(1)}, f32[2,64,1024]{2,1,0:T(8,128)S(1)}, u32[]{:S(2)}, u32[]{:S(2)}) %collective-permute-start.47) | collective-permute-done | bytes 524320 | tf_op jit(solution)/shard_map/ppermute | solution.py:296
  220.3 1.2 fusion.2
  221.5 1.7 collective-permute-start.46
  224.1 1.2 copy.28
  225.3 1.4 collective-permute-done.52
  226.7 12.8 %collective-permute-done.50 = f32[2,64,1024]{2,1,0:T(8,128)S(1)} collective-permute-done((f32[2,64,1024]{2,1,0:T(8,128)S(1)}, f32[2,64,1024]{2,1,0:T(8,128)S(1)}, u32[]{:S(2)}, u32[]{:S(2)}) %collective-permute-start.50) | collective-permute-done | bytes 524320 | tf_op jit(solution)/shard_map/ppermute | solution.py:292
  239.7 2.1 collective-permute-start.53
  241.8 1.2 fusion.7
  243.0 1.2 copy.30
  244.2 4.2 %collective-permute-done.53 = f32[64,1024]{1,0:T(8,128)S(1)} collective-permute-done((f32[64,1024]{1,0:T(8,128)S(1)}, f32[64,1024]{1,0:T(8,128)S(1)}, u32[]{:S(2)}, u32[]{:S(2)}) %collective-permute-start.53) | collective-permute-done | bytes 262176 | tf_op jit(solution)/shard_map/ppermute | solution.py:292
  (133 shorter events, 12.5 us)
Async XLA Ops:
  0.6 15.6 %copy-start.14 = (s32[16]{0:T(128)S(1)}, s32[16]{0:T(128)}, u32[]{:S(2)}) copy-start(s32[16]{0:T(128)} %constant.60.clone) | copy-start | bytes 196
  0.6 15.6 %copy-start.15 = (s32[16]{0:T(128)S(1)}, s32[16]{0:T(128)}, u32[]{:S(2)}) copy-start(s32[16]{0:T(128)} %constant.65.clone) | copy-start | bytes 196
  0.7 15.5 %copy-start.16 = (s32[16]{0:T(128)S(1)}, s32[16]{0:T(128)}, u32[]{:S(2)}) copy-start(s32[16]{0:T(128)} %constant.64.clone) | copy-start | bytes 196
  0.7 15.5 %copy-start.17 = (s32[16]{0:T(128)S(1)}, s32[16]{0:T(128)}, u32[]{:S(2)}) copy-start(s32[16]{0:T(128)} %constant.59.clone) | copy-start | bytes 196
  0.7 15.5 %copy-start.18 = (s32[16]{0:T(128)S(1)}, s32[16]{0:T(128)}, u32[]{:S(2)}) copy-start(s32[16]{0:T(128)} %constant.67) | copy-start | bytes 196
  0.7 15.5 %copy-start.19 = (s32[16]{0:T(128)S(1)}, s32[16]{0:T(128)}, u32[]{:S(2)}) copy-start(s32[16]{0:T(128)} %constant.66) | copy-start | bytes 196
  0.7 15.5 %copy-start.6 = (f32[16,16,16,16]{3,2,1,0:T(8,128)S(1)}, f32[16,16,16,16]{3,2,1,0:T(8,128)}, u32[]{:S(2)}) copy-start(f32[16,16,16,16]{3,2,1,0:T(8,128)} %param.17) | copy-start | bytes 786436
  2.9 18.0 %collective-permute-start = (f32[64,1024]{1,0:T(8,128)S(1)}, f32[64,1024]{1,0:T(8,128)S(1)}, u32[]{:S(2)}, u32[]{:S(2)}) collective-permute-start(f32[64,1024]{1,0:T(8,128)S(1)} %reshape.74.refs_0_), channel_id=1, source_target_pairs={{0,64},{8,72},{16,80},{24,88},{32,96},{40,104},{48,112},{56,120},{... | collective-permute-start | bytes 786440 | tf_op jit(solution)/shard_map/ppermute | solution.py:292
  7.4 17.0 %collective-permute-start.9 = (f32[64,1024]{1,0:T(8,128)S(1)}, f32[64,1024]{1,0:T(8,128)S(1)}, u32[]{:S(2)}, u32[]{:S(2)}) collective-permute-start(f32[64,1024]{1,0:T(8,128)S(1)} %reshape.74.refs_0_), channel_id=1, source_target_pairs={{0,16},{8,24},{16,32},{24,40},{32,48},{40,56},{48,0},{56,8},{64,80... | collective-permute-start | bytes 786440 | tf_op jit(solution)/shard_map/ppermute | solution.py:292
  8.7 18.0 %collective-permute-start.10 = (f32[64,1024]{1,0:T(8,128)S(1)}, f32[64,1024]{1,0:T(8,128)S(1)}, u32[]{:S(2)}, u32[]{:S(2)}) collective-permute-start(f32[64,1024]{1,0:T(8,128)S(1)} %reshape.74.refs_0_), channel_id=1, source_target_pairs={{0,48},{8,56},{16,0},{24,8},{32,16},{40,24},{48,32},{56,40},{64,11... | collective-permute-start | bytes 786440 | tf_op jit(solution)/shard_map/ppermute | solution.py:292
  10.1 16.8 %collective-permute-start.11 = (f32[64,1024]{1,0:T(8,128)S(1)}, f32[64,1024]{1,0:T(8,128)S(1)}, u32[]{:S(2)}, u32[]{:S(2)}) collective-permute-start(f32[64,1024]{1,0:T(8,128)S(1)} %reshape.74.refs_0_), channel_id=1, source_target_pairs={{0,32},{8,40},{16,48},{24,56},{32,0},{40,8},{48,16},{56,24},{64,96... | collective-permute-start | bytes 786440 | tf_op jit(solution)/shard_map/ppermute | solution.py:292
  16.1 7.9 %collective-permute-start.1 = (f32[64,1024]{1,0:T(8,128)}, f32[64,1024]{1,0:T(8,128)}, u32[]{:S(2)}, u32[]{:S(2)}) collective-permute-start(f32[64,1024]{1,0:T(8,128)} %reshape.77), channel_id=1, source_target_pairs={{0,64},{8,72},{16,80},{24,88},{32,96},{40,104},{48,112},{56,120},{... | collective-permute-start | bytes 786440 | tf_op jit(solution)/shard_map/ppermute | solution.py:292
  20.9 9.4 %collective-permute-start.15 = (f32[64,1024]{1,0:T(8,128)S(1)}, f32[64,1024]{1,0:T(8,128)S(1)}, u32[]{:S(2)}, u32[]{:S(2)}) collective-permute-start(f32[64,1024]{1,0:T(8,128)S(1)} %reshape.74.refs_0_), channel_id=1, source_target_pairs={{0,8},{8,0},{16,24},{24,16},{32,40},{40,32},{48,56},{56,48},{64,72... | collective-permute-start | bytes 786440 | tf_op jit(solution)/shard_map/ppermute | solution.py:292
  24.0 7.4 %collective-permute-start.12 = (f32[64,1024]{1,0:T(8,128)S(1)}, f32[64,1024]{1,0:T(8,128)S(1)}, u32[]{:S(2)}, u32[]{:S(2)}) collective-permute-start(f32[64,1024]{1,0:T(8,128)S(1)} %collective-permute-done.refs_4_), channel_id=1, source_target_pairs={{0,16},{8,24},{16,32},{24,40},{32,48},{40,56},{48,0},{56,8},{64,80... | collective-permute-start | bytes 786440 | tf_op jit(solution)/shard_map/ppermute | solution.py:292
  24.4 7.9 %collective-permute-start.13 = (f32[64,1024]{1,0:T(8,128)S(1)}, f32[64,1024]{1,0:T(8,128)S(1)}, u32[]{:S(2)}, u32[]{:S(2)}) collective-permute-start(f32[64,1024]{1,0:T(8,128)S(1)} %collective-permute-done.refs_4_), channel_id=1, source_target_pairs={{0,48},{8,56},{16,0},{24,8},{32,16},{40,24},{48,32},{56,40},{64,11... | collective-permute-start | bytes 786440 | tf_op jit(solution)/shard_map/ppermute | solution.py:292
  26.7 9.9 %collective-permute-start.14 = (f32[64,1024]{1,0:T(8,128)S(1)}, f32[64,1024]{1,0:T(8,128)S(1)}, u32[]{:S(2)}, u32[]{:S(2)}) collective-permute-start(f32[64,1024]{1,0:T(8,128)S(1)} %collective-permute-done.refs_4_), channel_id=1, source_target_pairs={{0,32},{8,40},{16,48},{24,56},{32,0},{40,8},{48,16},{56,24},{64,96... | collective-permute-start | bytes 786440 | tf_op jit(solution)/shard_map/ppermute | solution.py:292
  26.9 9.7 %collective-permute-start.16 = (f32[64,1024]{1,0:T(8,128)S(1)}, f32[64,1024]{1,0:T(8,128)S(1)}, u32[]{:S(2)}, u32[]{:S(2)}) collective-permute-start(f32[64,1024]{1,0:T(8,128)S(1)} %collective-permute-done.9.refs_1_), channel_id=1, source_target_pairs={{0,8},{8,0},{16,24},{24,16},{32,40},{40,32},{48,56},{56,48},{64,72... | collective-permute-start | bytes 786440 | tf_op jit(solution)/shard_map/ppermute | solution.py:292
  30.3 13.3 %collective-permute-start.17 = (f32[64,1024]{1,0:T(8,128)S(1)}, f32[64,1024]{1,0:T(8,128)S(1)}, u32[]{:S(2)}, u32[]{:S(2)}) collective-permute-start(f32[64,1024]{1,0:T(8,128)S(1)} %collective-permute-done.10.refs_2_), channel_id=1, source_target_pairs={{0,8},{8,0},{16,24},{24,16},{32,40},{40,32},{48,56},{56,48},{64,72... | collective-permute-start | bytes 786440 | tf_op jit(solution)/shard_map/ppermute | solution.py:292
  31.4 14.8 %collective-permute-start.2 = (f32[128,1024]{1,0:T(8,128)S(1)}, f32[128,1024]{1,0:T(8,128)S(1)}, u32[]{:S(2)}, u32[]{:S(2)}) collective-permute-start(f32[128,1024]{1,0:T(8,128)S(1)} %constant_dynamic-update-slice_fusion.refs_0_), channel_id=1, source_target_pairs={{0,16},{8,24},{16,32},{24,40},{32,48},{40,56},{48,0},{56,8},{64,80... | collective-permute-start | bytes 1572872 | tf_op jit(solution)/shard_map/ppermute | solution.py:292
  32.3 30.0 %collective-permute-start.3 = (f32[128,1024]{1,0:T(8,128)S(1)}, f32[128,1024]{1,0:T(8,128)S(1)}, u32[]{:S(2)}, u32[]{:S(2)}) collective-permute-start(f32[128,1024]{1,0:T(8,128)S(1)} %constant_dynamic-update-slice_fusion.refs_0_), channel_id=1, source_target_pairs={{0,48},{8,56},{16,0},{24,8},{32,16},{40,24},{48,32},{56,40},{64,11... | collective-permute-start | bytes 1572872 | tf_op jit(solution)/shard_map/ppermute | solution.py:292
  36.6 25.7 %collective-permute-start.4 = (f32[128,1024]{1,0:T(8,128)S(1)}, f32[128,1024]{1,0:T(8,128)S(1)}, u32[]{:S(2)}, u32[]{:S(2)}) collective-permute-start(f32[128,1024]{1,0:T(8,128)S(1)} %constant_dynamic-update-slice_fusion.refs_0_), channel_id=1, source_target_pairs={{0,32},{8,40},{16,48},{24,56},{32,0},{40,8},{48,16},{56,24},{64,96... | collective-permute-start | bytes 1572872 | tf_op jit(solution)/shard_map/ppermute | solution.py:292
  36.6 8.2 %collective-permute-start.18 = (f32[64,1024]{1,0:T(8,128)S(1)}, f32[64,1024]{1,0:T(8,128)S(1)}, u32[]{:S(2)}, u32[]{:S(2)}) collective-permute-start(f32[64,1024]{1,0:T(8,128)S(1)} %collective-permute-done.11.refs_3_), channel_id=1, source_target_pairs={{0,8},{8,0},{16,24},{24,16},{32,40},{40,32},{48,56},{56,48},{64,72... | collective-permute-start | bytes 786440 | tf_op jit(solution)/shard_map/ppermute | solution.py:292
  43.6 1.5 collective-permute-start.19
  44.8 18.0 %collective-permute-start.20 = (f32[64,1024]{1,0:T(8,128)S(1)}, f32[64,1024]{1,0:T(8,128)S(1)}, u32[]{:S(2)}, u32[]{:S(2)}) collective-permute-start(f32[64,1024]{1,0:T(8,128)S(1)} %collective-permute-done.12.refs_5_), channel_id=1, source_target_pairs={{0,8},{8,0},{16,24},{24,16},{32,40},{40,32},{48,56},{56,48},{64,72... | collective-permute-start | bytes 786440 | tf_op jit(solution)/shard_map/ppermute | solution.py:292
  45.2 17.7 %collective-permute-start.21 = (f32[64,1024]{1,0:T(8,128)S(1)}, f32[64,1024]{1,0:T(8,128)S(1)}, u32[]{:S(2)}, u32[]{:S(2)}) collective-permute-start(f32[64,1024]{1,0:T(8,128)S(1)} %collective-permute-done.13.refs_6_), channel_id=1, source_target_pairs={{0,8},{8,0},{16,24},{24,16},{32,40},{40,32},{48,56},{56,48},{64,72... | collective-permute-start | bytes 786440 | tf_op jit(solution)/shard_map/ppermute | solution.py:292
  46.2 35.3 %collective-permute-start.5 = (f32[128,1024]{1,0:T(8,128)S(1)}, f32[128,1024]{1,0:T(8,128)S(1)}, u32[]{:S(2)}, u32[]{:S(2)}) collective-permute-start(f32[128,1024]{1,0:T(8,128)S(1)} %constant_dynamic-update-slice_fusion.refs_0_), channel_id=1, source_target_pairs={{0,8},{8,0},{16,24},{24,16},{32,40},{40,32},{48,56},{56,48},{64,72... | collective-permute-start | bytes 1572872 | tf_op jit(solution)/shard_map/ppermute | solution.py:292
  62.3 19.3 %collective-permute-start.6 = (f32[128,1024]{1,0:T(8,128)S(1)}, f32[128,1024]{1,0:T(8,128)S(1)}, u32[]{:S(2)}, u32[]{:S(2)}) collective-permute-start(f32[128,1024]{1,0:T(8,128)S(1)} %collective-permute-done.2.refs_1_), channel_id=1, source_target_pairs={{0,8},{8,0},{16,24},{24,16},{32,40},{40,32},{48,56},{56,48},{64,72... | collective-permute-start | bytes 1572872 | tf_op jit(solution)/shard_map/ppermute | solution.py:292
  62.3 19.3 %collective-permute-start.7 = (f32[128,1024]{1,0:T(8,128)S(1)}, f32[128,1024]{1,0:T(8,128)S(1)}, u32[]{:S(2)}, u32[]{:S(2)}) collective-permute-start(f32[128,1024]{1,0:T(8,128)S(1)} %collective-permute-done.3.refs_2_), channel_id=1, source_target_pairs={{0,8},{8,0},{16,24},{24,16},{32,40},{40,32},{48,56},{56,48},{64,72... | collective-permute-start | bytes 1572872 | tf_op jit(solution)/shard_map/ppermute | solution.py:292
  62.8 18.8 %collective-permute-start.8 = (f32[128,1024]{1,0:T(8,128)S(1)}, f32[128,1024]{1,0:T(8,128)S(1)}, u32[]{:S(2)}, u32[]{:S(2)}) collective-permute-start(f32[128,1024]{1,0:T(8,128)S(1)} %collective-permute-done.4.refs_3_), channel_id=1, source_target_pairs={{0,8},{8,0},{16,24},{24,16},{32,40},{40,32},{48,56},{56,48},{64,72... | collective-permute-start | bytes 1572872 | tf_op jit(solution)/shard_map/ppermute | solution.py:292
  62.9 3.6 %collective-permute-start.22 = (f32[64,1024]{1,0:T(8,128)S(1)}, f32[64,1024]{1,0:T(8,128)S(1)}, u32[]{:S(2)}, u32[]{:S(2)}) collective-permute-start(f32[64,1024]{1,0:T(8,128)S(1)} %collective-permute-done.14.refs_7_), channel_id=1, source_target_pairs={{0,8},{8,0},{16,24},{24,16},{32,40},{40,32},{48,56},{56,48},{64,72... | collective-permute-start | bytes 786440 | tf_op jit(solution)/shard_map/ppermute | solution.py:292
  93.1 85.3 %copy-start.2 = (f32[4,2,64,1024]{3,2,1,0:T(8,128)}, f32[4,2,64,1024]{3,2,1,0:T(8,128)S(1)}, u32[]{:S(2)}) copy-start(f32[4,2,64,1024]{3,2,1,0:T(8,128)S(1)} %get-tuple-element.51) | copy-start | bytes 6291460
  108.3 5.8 %collective-permute-start.30 = (f32[64,256]{1,0:T(8,128)S(1)}, f32[64,256]{1,0:T(8,128)S(1)}, u32[]{:S(2)}, u32[]{:S(2)}) collective-permute-start(f32[64,256]{1,0:T(8,128)S(1)} %get-tuple-element.99), channel_id=1, source_target_pairs={{0,72},{8,64},{16,88},{24,80},{32,104},{40,96},{48,120},{56,112},{... | collective-permute-start | bytes 196616 | tf_op jit(solution)/shard_map/ppermute | solution.py:292
  110.5 5.0 %collective-permute-start.28 = (f32[64,256]{1,0:T(8,128)S(1)}, f32[64,256]{1,0:T(8,128)S(1)}, u32[]{:S(2)}, u32[]{:S(2)}) collective-permute-start(f32[64,256]{1,0:T(8,128)S(1)} %get-tuple-element.100), channel_id=1, source_target_pairs={{0,64},{8,72},{16,80},{24,88},{32,96},{40,104},{48,112},{56,120},{... | collective-permute-start | bytes 196616 | tf_op jit(solution)/shard_map/ppermute | solution.py:292
  111.7 3.9 %collective-permute-start.29 = (f32[64,256]{1,0:T(8,128)S(1)}, f32[64,256]{1,0:T(8,128)S(1)}, u32[]{:S(2)}, u32[]{:S(2)}) collective-permute-start(f32[64,256]{1,0:T(8,128)S(1)} %get-tuple-element.98), channel_id=1, source_target_pairs={{0,8},{8,0},{16,24},{24,16},{32,40},{40,32},{48,56},{56,48},{64,72... | collective-permute-start | bytes 196616 | tf_op jit(solution)/shard_map/ppermute | solution.py:292
  115.6 3.3 %collective-permute-start.33 = (f32[16,256]{1,0:T(8,128)S(1)}, f32[16,256]{1,0:T(8,128)S(1)}, u32[]{:S(2)}, u32[]{:S(2)}) collective-permute-start(f32[16,256]{1,0:T(8,128)S(1)} %get-tuple-element.102), channel_id=1, source_target_pairs={{0,48},{8,56},{16,0},{24,8},{32,16},{40,24},{48,32},{56,40},{64,11... | collective-permute-start | bytes 49160 | tf_op jit(solution)/shard_map/ppermute | solution.py:292
  117.6 3.8 %collective-permute-start.31 = (f32[16,256]{1,0:T(8,128)S(1)}, f32[16,256]{1,0:T(8,128)S(1)}, u32[]{:S(2)}, u32[]{:S(2)}) collective-permute-start(f32[16,256]{1,0:T(8,128)S(1)} %get-tuple-element.103), channel_id=1, source_target_pairs={{0,16},{8,24},{16,32},{24,40},{32,48},{40,56},{48,0},{56,8},{64,80... | collective-permute-start | bytes 49160 | tf_op jit(solution)/shard_map/ppermute | solution.py:292
  117.6 4.1 %collective-permute-start.32 = (f32[16,256]{1,0:T(8,128)S(1)}, f32[16,256]{1,0:T(8,128)S(1)}, u32[]{:S(2)}, u32[]{:S(2)}) collective-permute-start(f32[16,256]{1,0:T(8,128)S(1)} %get-tuple-element.101), channel_id=1, source_target_pairs={{0,32},{8,40},{16,48},{24,56},{32,0},{40,8},{48,16},{56,24},{64,96... | collective-permute-start | bytes 49160 | tf_op jit(solution)/shard_map/ppermute | solution.py:292
  121.7 4.2 %collective-permute-start.36 = (f32[16,256]{1,0:T(8,128)S(1)}, f32[16,256]{1,0:T(8,128)S(1)}, u32[]{:S(2)}, u32[]{:S(2)}) collective-permute-start(f32[16,256]{1,0:T(8,128)S(1)} %bitcast_add_fusion.1), channel_id=1, source_target_pairs={{0,3},{1,0},{2,1},{3,2},{4,7},{5,4},{6,5},{7,6},{8,11},{9,8},{10,9... | collective-permute-start | bytes 49160 | tf_op jit(solution)/shard_map/ppermute | solution.py:296
  124.2 3.8 %collective-permute-start.34 = (f32[16,256]{1,0:T(8,128)S(1)}, f32[16,256]{1,0:T(8,128)S(1)}, u32[]{:S(2)}, u32[]{:S(2)}) collective-permute-start(f32[16,256]{1,0:T(8,128)S(1)} %bitcast_add_fusion.1), channel_id=1, source_target_pairs={{0,1},{1,2},{2,3},{3,0},{4,5},{5,6},{6,7},{7,4},{8,9},{9,10},{10,1... | collective-permute-start | bytes 49160 | tf_op jit(solution)/shard_map/ppermute | solution.py:296
  124.2 4.1 %collective-permute-start.35 = (f32[16,256]{1,0:T(8,128)S(1)}, f32[16,256]{1,0:T(8,128)S(1)}, u32[]{:S(2)}, u32[]{:S(2)}) collective-permute-start(f32[16,256]{1,0:T(8,128)S(1)} %bitcast_add_fusion.1), channel_id=1, source_target_pairs={{0,2},{1,3},{2,0},{3,1},{4,6},{5,7},{6,4},{7,5},{8,10},{9,11},{10,... | collective-permute-start | bytes 49160 | tf_op jit(solution)/shard_map/ppermute | solution.py:296
  128.3 2.9 %collective-permute-start.37 = (f32[16,256]{1,0:T(8,128)S(1)}, f32[16,256]{1,0:T(8,128)S(1)}, u32[]{:S(2)}, u32[]{:S(2)}) collective-permute-start(f32[16,256]{1,0:T(8,128)S(1)} %add_add_fusion.1), channel_id=1, source_target_pairs={{0,4},{1,5},{2,6},{3,7},{4,0},{5,1},{6,2},{7,3},{8,12},{9,13},{10,... | collective-permute-start | bytes 49160 | tf_op jit(solution)/shard_map/ppermute | solution.py:296
  131.2 21.7 %collective-permute-start.38 = (f32[16,256]{1,0:T(8,128)S(1)}, f32[16,256]{1,0:T(8,128)S(1)}, u32[]{:S(2)}, u32[]{:S(2)}) collective-permute-start(f32[16,256]{1,0:T(8,128)S(1)} %get-tuple-element.89), channel_id=1, source_target_pairs={{0,48},{8,56},{16,0},{24,8},{32,16},{40,24},{48,32},{56,40},{64,11... | collective-permute-start | bytes 49160 | tf_op jit(solution)/shard_map/ppermute | solution.py:292
  144.6 66.5 %collective-permute-start.49 = (f32[512,1024]{1,0:T(8,128)}, f32[512,1024]{1,0:T(8,128)}, u32[]{:S(2)}, u32[]{:S(2)}) collective-permute-start(f32[512,1024]{1,0:T(8,128)} %get-tuple-element.79), channel_id=1, source_target_pairs={{0,8},{8,0},{16,24},{24,16},{32,40},{40,32},{48,56},{56,48},{64,72... | collective-permute-start | bytes 6291464 | tf_op jit(solution)/shard_map/ppermute | solution.py:292
  149.9 26.5 %collective-permute-start.24 = (f32[2,2,64,1024]{3,2,1,0:T(8,128)S(1)}, f32[2,2,64,1024]{3,2,1,0:T(8,128)S(1)}, u32[]{:S(2)}, u32[]{:S(2)}) collective-permute-start(f32[2,2,64,1024]{3,2,1,0:T(8,128)S(1)} %get-tuple-element.53), channel_id=1, source_target_pairs={{0,1},{1,2},{2,3},{3,0},{4,5},{5,6},{6,7},{7,4},{8,9},{9,10},{10,1... | collective-permute-start | bytes 3145736 | tf_op jit(solution)/shard_map/ppermute | solution.py:296
  150.5 28.0 %collective-permute-start.23 = (f32[2,2,64,1024]{3,2,1,0:T(8,128)S(1)}, f32[2,2,64,1024]{3,2,1,0:T(8,128)S(1)}, u32[]{:S(2)}, u32[]{:S(2)}) collective-permute-start(f32[2,2,64,1024]{3,2,1,0:T(8,128)S(1)} %get-tuple-element.52), channel_id=1, source_target_pairs={{0,3},{1,0},{2,1},{3,2},{4,7},{5,4},{6,5},{7,6},{8,11},{9,8},{10,9... | collective-permute-start | bytes 3145736 | tf_op jit(solution)/shard_map/ppermute | solution.py:296
  152.9 4.1 %collective-permute-start.39 = (f32[16,256]{1,0:T(8,128)S(1)}, f32[16,256]{1,0:T(8,128)S(1)}, u32[]{:S(2)}, u32[]{:S(2)}) collective-permute-start(f32[16,256]{1,0:T(8,128)S(1)} %get-tuple-element.89), channel_id=1, source_target_pairs={{0,32},{8,40},{16,48},{24,56},{32,0},{40,8},{48,16},{56,24},{64,96... | collective-permute-start | bytes 49160 | tf_op jit(solution)/shard_map/ppermute | solution.py:292
  152.9 4.1 %collective-permute-start.40 = (f32[16,256]{1,0:T(8,128)S(1)}, f32[16,256]{1,0:T(8,128)S(1)}, u32[]{:S(2)}, u32[]{:S(2)}) collective-permute-start(f32[16,256]{1,0:T(8,128)S(1)} %get-tuple-element.89), channel_id=1, source_target_pairs={{0,16},{8,24},{16,32},{24,40},{32,48},{40,56},{48,0},{56,8},{64,80... | collective-permute-start | bytes 49160 | tf_op jit(solution)/shard_map/ppermute | solution.py:292
  157.0 12.0 %collective-permute-start.41 = (f32[64,256]{1,0:T(8,128)S(1)}, f32[64,256]{1,0:T(8,128)S(1)}, u32[]{:S(2)}, u32[]{:S(2)}) collective-permute-start(f32[64,256]{1,0:T(8,128)S(1)} %constant_dynamic-slice_fusion), channel_id=1, source_target_pairs={{0,64},{8,72},{16,80},{24,88},{32,96},{40,104},{48,112},{56,120},{... | collective-permute-start | bytes 196616 | tf_op jit(solution)/shard_map/ppermute | solution.py:292
  169.1 29.9 %collective-permute-start.45 = (f32[2,2,64,1024]{3,2,1,0:T(8,128)}, f32[2,2,64,1024]{3,2,1,0:T(8,128)}, u32[]{:S(2)}, u32[]{:S(2)}) collective-permute-start(f32[2,2,64,1024]{3,2,1,0:T(8,128)} %get-tuple-element.76), channel_id=1, source_target_pairs={{0,1},{1,2},{2,3},{3,0},{4,5},{5,6},{6,7},{7,4},{8,9},{9,10},{10,1... | collective-permute-start | bytes 3145736 | tf_op jit(solution)/shard_map/ppermute | solution.py:296
  169.1 29.9 %collective-permute-start.44 = (f32[2,2,64,1024]{3,2,1,0:T(8,128)S(1)}, f32[2,2,64,1024]{3,2,1,0:T(8,128)}, u32[]{:S(2)}, u32[]{:S(2)}) collective-permute-start(f32[2,2,64,1024]{3,2,1,0:T(8,128)S(1)} %get-tuple-element.75), channel_id=1, source_target_pairs={{0,3},{1,0},{2,1},{3,2},{4,7},{5,4},{6,5},{7,6},{8,11},{9,8},{10,9... | collective-permute-start | bytes 3145736 | tf_op jit(solution)/shard_map/ppermute | solution.py:296
  176.4 6.1 %collective-permute-start.43 = (f32[64,256]{1,0:T(8,128)S(1)}, f32[64,256]{1,0:T(8,128)S(1)}, u32[]{:S(2)}, u32[]{:S(2)}) collective-permute-start(f32[64,256]{1,0:T(8,128)S(1)} %constant_dynamic-slice_fusion), channel_id=1, source_target_pairs={{0,72},{8,64},{16,88},{24,80},{32,104},{40,96},{48,120},{56,112},{... | collective-permute-start | bytes 196616 | tf_op jit(solution)/shard_map/ppermute | solution.py:292
  178.5 4.7 %collective-permute-start.42 = (f32[64,256]{1,0:T(8,128)S(1)}, f32[64,256]{1,0:T(8,128)S(1)}, u32[]{:S(2)}, u32[]{:S(2)}) collective-permute-start(f32[64,256]{1,0:T(8,128)S(1)} %constant_dynamic-slice_fusion), channel_id=1, source_target_pairs={{0,8},{8,0},{16,24},{24,16},{32,40},{40,32},{48,56},{56,48},{64,72... | collective-permute-start | bytes 196616 | tf_op jit(solution)/shard_map/ppermute | solution.py:292
  182.5 26.7 %collective-permute-start.26 = (f32[2,64,1024]{2,1,0:T(8,128)}, f32[2,64,1024]{2,1,0:T(8,128)}, u32[]{:S(2)}, u32[]{:S(2)}) collective-permute-start(f32[2,64,1024]{2,1,0:T(8,128)} %get-tuple-element.97), channel_id=1, source_target_pairs={{0,3},{1,0},{2,1},{3,2},{4,7},{5,4},{6,5},{7,6},{8,11},{9,8},{10,9... | collective-permute-start | bytes 1572872 | tf_op jit(solution)/shard_map/ppermute | solution.py:296
  188.9 20.3 %copy-start.3 = (f32[4,2,64,1024]{3,2,1,0:T(8,128)S(1)}, f32[4,2,64,1024]{3,2,1,0:T(8,128)}, u32[]{:S(2)}) copy-start(f32[4,2,64,1024]{3,2,1,0:T(8,128)} %copy-done.2) | copy-start | bytes 6291460
  188.9 20.3 %copy-start.11 = (f32[2,2,64,1024]{3,2,1,0:T(8,128)S(1)}, f32[2,2,64,1024]{3,2,1,0:T(8,128)}, u32[]{:S(2)}) copy-start(f32[2,2,64,1024]{3,2,1,0:T(8,128)} %copy-done.10) | copy-start | bytes 3145732
  188.9 32.6 %collective-permute-start.25 = (f32[2,64,1024]{2,1,0:T(8,128)}, f32[2,64,1024]{2,1,0:T(8,128)S(1)}, u32[]{:S(2)}, u32[]{:S(2)}) collective-permute-start(f32[2,64,1024]{2,1,0:T(8,128)} %get-tuple-element.96), channel_id=1, source_target_pairs={{0,1},{1,2},{2,3},{3,0},{4,5},{5,6},{6,7},{7,4},{8,9},{9,10},{10,1... | collective-permute-start | bytes 1572872 | tf_op jit(solution)/shard_map/ppermute | solution.py:296
  200.6 19.7 %collective-permute-start.47 = (f32[2,64,1024]{2,1,0:T(8,128)S(1)}, f32[2,64,1024]{2,1,0:T(8,128)S(1)}, u32[]{:S(2)}, u32[]{:S(2)}) collective-permute-start(f32[2,64,1024]{2,1,0:T(8,128)S(1)} %get-tuple-element.95), channel_id=1, source_target_pairs={{0,3},{1,0},{2,1},{3,2},{4,7},{5,4},{6,5},{7,6},{8,11},{9,8},{10,9... | collective-permute-start | bytes 1572872 | tf_op jit(solution)/shard_map/ppermute | solution.py:296
  210.3 12.8 %collective-permute-start.27 = (f32[2,64,1024]{2,1,0:T(8,128)S(1)}, f32[2,64,1024]{2,1,0:T(8,128)S(1)}, u32[]{:S(2)}, u32[]{:S(2)}) collective-permute-start(f32[2,64,1024]{2,1,0:T(8,128)S(1)} %fusion.10), channel_id=1, source_target_pairs={{0,4},{1,5},{2,6},{3,7},{4,0},{5,1},{6,2},{7,3},{8,12},{9,13},{10,... | collective-permute-start | bytes 1572872 | tf_op jit(solution)/shard_map/ppermute | solution.py:296
  213.2 13.5 %collective-permute-start.52 = (f32[2,64,1024]{2,1,0:T(8,128)S(1)}, f32[2,64,1024]{2,1,0:T(8,128)S(1)}, u32[]{:S(2)}, u32[]{:S(2)}) collective-permute-start(f32[2,64,1024]{2,1,0:T(8,128)S(1)} %bitcast.86), channel_id=1, source_target_pairs={{0,32},{8,40},{16,48},{24,56},{32,0},{40,8},{48,16},{56,24},{64,96... | collective-permute-start | bytes 1572872 | tf_op jit(solution)/shard_map/ppermute | solution.py:292
  213.3 26.1 %collective-permute-start.50 = (f32[2,64,1024]{2,1,0:T(8,128)S(1)}, f32[2,64,1024]{2,1,0:T(8,128)S(1)}, u32[]{:S(2)}, u32[]{:S(2)}) collective-permute-start(f32[2,64,1024]{2,1,0:T(8,128)S(1)} %bitcast.85), channel_id=1, source_target_pairs={{0,16},{8,24},{16,32},{24,40},{32,48},{40,56},{48,0},{56,8},{64,80... | collective-permute-start | bytes 1572872 | tf_op jit(solution)/shard_map/ppermute | solution.py:292
  220.3 19.2 %collective-permute-start.51 = (f32[2,64,1024]{2,1,0:T(8,128)S(1)}, f32[2,64,1024]{2,1,0:T(8,128)S(1)}, u32[]{:S(2)}, u32[]{:S(2)}) collective-permute-start(f32[2,64,1024]{2,1,0:T(8,128)S(1)} %bitcast.84), channel_id=1, source_target_pairs={{0,48},{8,56},{16,0},{24,8},{32,16},{40,24},{48,32},{56,40},{64,11... | collective-permute-start | bytes 1572872 | tf_op jit(solution)/shard_map/ppermute | solution.py:292
  221.5 20.3 %collective-permute-start.46 = (f32[2,64,1024]{2,1,0:T(8,128)S(1)}, f32[2,64,1024]{2,1,0:T(8,128)S(1)}, u32[]{:S(2)}, u32[]{:S(2)}) collective-permute-start(f32[2,64,1024]{2,1,0:T(8,128)S(1)} %get-tuple-element.94), channel_id=1, source_target_pairs={{0,1},{1,2},{2,3},{3,0},{4,5},{5,6},{6,7},{7,4},{8,9},{9,10},{10,1... | collective-permute-start | bytes 1572872 | tf_op jit(solution)/shard_map/ppermute | solution.py:296
  223.2 18.6 %collective-permute-start.48 = (f32[2,64,1024]{2,1,0:T(8,128)S(1)}, f32[2,64,1024]{2,1,0:T(8,128)S(1)}, u32[]{:S(2)}, u32[]{:S(2)}) collective-permute-start(f32[2,64,1024]{2,1,0:T(8,128)S(1)} %fusion.2), channel_id=1, source_target_pairs={{0,4},{1,5},{2,6},{3,7},{4,0},{5,1},{6,2},{7,3},{8,12},{9,13},{10,... | collective-permute-start | bytes 1572872 | tf_op jit(solution)/shard_map/ppermute | solution.py:296
  239.7 8.7 %collective-permute-start.53 = (f32[64,1024]{1,0:T(8,128)S(1)}, f32[64,1024]{1,0:T(8,128)S(1)}, u32[]{:S(2)}, u32[]{:S(2)}) collective-permute-start(f32[64,1024]{1,0:T(8,128)S(1)} %slice_bitcast_fusion), channel_id=1, source_target_pairs={{0,64},{8,72},{16,80},{24,88},{32,96},{40,104},{48,112},{56,120},{... | collective-permute-start | bytes 786440 | tf_op jit(solution)/shard_map/ppermute | solution.py:292
  (11 other events, 92.0 us)
where the time goes:
time: 251 us; the launch traced here: 249 us
  starting transfers between devices  85.2 us (34%)
  waiting for transfers between devices  69.7 us (28%)
  Pallas kernels  60.9 us (24%)
  local copies, waits for them, and re-layouts  23.4 us (9%)
  other arithmetic  8.94 us (4%)
    ppermute x40, starting transfers between devices, row_permute(): return lax.ppermute(value, 'row', pairs)  67.6 us
    ppermute x40, waiting for transfers between devices, row_permute(): return lax.ppermute(value, 'row', pairs)  38.5 us
    ppermute x14, waiting for transfers between devices, col_permute(): lax.ppermute(value, 'col', [(i, (i // 4 ^ z) * 4 + (i + x) % 4) for i in...  31.3 us
    ppermute x14, starting transfers between devices, col_permute(): lax.ppermute(value, 'col', [(i, (i // 4 ^ z) * 4 + (i + x) % 4) for i in...  17.7 us
    pallas_call x1, Pallas kernels, first_call(): pl.pallas_call(first_kernel, out_shape=(SQUARE, SQUARE, jax.ShapeDtypeStr...  15.1 us
    pallas_call x1, Pallas kernels, back_call(): pl.pallas_call(functools.partial(back_kernel, len(pieces)), out_shape=(SQ...  12.9 us
    pallas_call x1, Pallas kernels, edge_call(): pl.pallas_call(functools.partial(edge_kernel, len(pieces)), out_shape=(SQ...  11.6 us
    pallas_call x1, Pallas kernels, right_call(): pl.pallas_call(right_kernel, out_shape=(jax.ShapeDtypeStruct((512, 1024),...  10.8 us
  transfers between devices with their start and end apart: 54, of which 22 were waited for; matrix products, arithmetic and copies ran while one was open for 11% of the time, Pallas kernels for 14%

commit v1 on v0

--- a/solution.py
+++ b/solution.py
@@ -320,7 +320,7 @@
     col = lax.axis_index("col").astype(jnp.int32)
     z, y, core = row >> 3, (row >> 1) & 3, row & 1
     edge_rows = edge_tensor.reshape(1024, 1024)
-    left_rows = left_isometry.reshape(1024, 1024)
+    left_rows = pltpu.with_memory_space_constraint(left_isometry.reshape(1024, 1024), pltpu.HBM)
 
     def offset_of(other_z, steps, other_core):
         other_z, steps, other_core = (np.array(list(v), np.int32) for v in (other_z, steps, other_core))
@@ -344,16 +344,17 @@
     early, right_isometry = lax.optimization_barrier((early, right_isometry))
     other = row_permute(early, 1, 0, 0)
     nearest = [row_permute(early, 0, steps, 0) for steps in (1, 3, 2)]
-    values = (site_matrix, cotangent_offsets, isometry_offsets, sources, places)
+    values = (cotangent_offsets, isometry_offsets, sources, places)
     indices = (*corners, *ahead, first_row, at_low_z, at_low_core)
     other, values, indices = lax.optimization_barrier((other, values, indices))
-    site_matrix, cotangent_offsets, isometry_offsets, sources, places = values
+    cotangent_offsets, isometry_offsets, sources, places = values
     corners, ahead, (first_row, at_low_z, at_low_core) = indices[:4], indices[4:8], indices[8:]
     own = dense(right_isometry)
     pair = jnp.concatenate([own, row_permute(own, 1, 0, 0)], 0)
     pieces = [early, *nearest, other, *(row_permute(other, 0, steps, 0) for steps in (1, 3, 2))]
     pairs = [pair] + [row_permute(pair, 0, steps, 0) for steps in (1, 3, 2)]
 
+    pieces[3], site_matrix = lax.optimization_barrier((pieces[3], site_matrix))
     pieces += [row_permute(piece, 0, 0, 1) for piece in pieces]
     cotangent_high, cotangent_low, *rest = back_call(cotangent_offsets, pieces, left_rows, site_matrix)
     back_split, swapped_split = rest[:2], rest[2:]

time: 251 us -> 246 us (0.980)
  local copies, waits for them, and re-layouts: 23.4 us -> 17.9 us
  waiting for transfers between devices: 69.7 us -> 75.2 us
  starting transfers between devices: 85.2 us -> 80.2 us
    ppermute x40, waiting for transfers between devices: 38.5 us -> 43.9 us  [row_permute(): return lax.ppermute(value, 'row', pairs)]
    ppermute x40, starting transfers between devices: 67.6 us -> 62.5 us  [row_permute(): return lax.ppermute(value, 'row', pairs)]
    unnamed x52 -> x44, local copies, waits for them, and re-layouts: 8.43 us -> 6.23 us
  transfers between devices with their start and end apart: 54 -> 54, of which waited for: 22 -> 21; matrix products, arithmetic and copies ran while one was open for 11% -> 10% of each run, Pallas kernels for 14% -> 14%
where the time goes in v1:
time: 246 us; the launch traced here: 245 us
  starting transfers between devices  80.2 us (33%)
  waiting for transfers between devices  75.2 us (31%)
  Pallas kernels  61.9 us (25%)
  local copies, waits for them, and re-layouts  17.9 us (7%)
  other arithmetic  8.76 us (4%)
    ppermute x40, starting transfers between devices, row_permute(): return lax.ppermute(value, 'row', pairs)  62.5 us
    ppermute x40, waiting for transfers between devices, row_permute(): return lax.ppermute(value, 'row', pairs)  43.9 us
    ppermute x14, waiting for transfers between devices, col_permute(): lax.ppermute(value, 'col', [(i, (i // 4 ^ z) * 4 + (i + x) % 4) for i in...  31.3 us
    ppermute x14, starting transfers between devices, col_permute(): lax.ppermute(value, 'col', [(i, (i // 4 ^ z) * 4 + (i + x) % 4) for i in...  17.6 us
    pallas_call x1, Pallas kernels, first_call(): pl.pallas_call(first_kernel, out_shape=(SQUARE, SQUARE, jax.ShapeDtypeStr...  14.9 us
    pallas_call x1, Pallas kernels, back_call(): pl.pallas_call(functools.partial(back_kernel, len(pieces)), out_shape=(SQ...  14.1 us
    pallas_call x1, Pallas kernels, edge_call(): pl.pallas_call(functools.partial(edge_kernel, len(pieces)), out_shape=(SQ...  11.6 us
    pallas_call x1, Pallas kernels, right_call(): pl.pallas_call(right_kernel, out_shape=(jax.ShapeDtypeStruct((512, 1024),...  10.8 us
  transfers between devices with their start and end apart: 54, of which 21 were waited for; matrix products, arithmetic and copies ran while one was open for 10% of the time, Pallas kernels for 14%

profile of v1, /device:TPU:1, one launch (start us, length us, event | category | flops | bytes accessed | tf_op | source)
XLA Modules:
  0.0 245.1 jit_solution(17719838118800637605)
XLA Ops:
  0.8 1.6 copy.25
  2.8 4.5 %collective-permute-start = (f32[64,1024]{1,0:T(8,128)S(1)}, f32[64,1024]{1,0:T(8,128)S(1)}, u32[]{:S(2)}, u32[]{:S(2)}) collective-permute-start(f32[64,1024]{1,0:T(8,128)S(1)} %reshape.74.refs_0_), channel_id=1, source_target_pairs={{0,64},{8,72},{16,80},{24,88},{32,96},{40,104},{48,112},{56,120},{... | collective-permute-start | bytes 786440 | tf_op jit(solution)/shard_map/ppermute | solution.py:292
  7.3 1.3 collective-permute-start.9
  8.6 1.4 collective-permute-start.10
  10.0 1.6 collective-permute-start.11
  13.3 1.5 collective-permute-start.15
  14.8 5.5 %collective-permute-done.1 = f32[64,1024]{1,0:T(8,128)S(1)} collective-permute-done((f32[64,1024]{1,0:T(8,128)S(1)}, f32[64,1024]{1,0:T(8,128)S(1)}, u32[]{:S(2)}, u32[]{:S(2)}) %collective-permute-start.1) | collective-permute-done | bytes 262176 | tf_op jit(solution)/shard_map/ppermute | solution.py:292
  20.7 2.3 collective-permute-start.13
  23.2 3.4 %collective-permute-start.16 = (f32[64,1024]{1,0:T(8,128)S(1)}, f32[64,1024]{1,0:T(8,128)S(1)}, u32[]{:S(2)}, u32[]{:S(2)}) collective-permute-start(f32[64,1024]{1,0:T(8,128)S(1)} %collective-permute-done.9.refs_1_), channel_id=1, source_target_pairs={{0,8},{8,0},{16,24},{24,16},{32,40},{40,32},{48,56},{56,48},{64,72... | collective-permute-start | bytes 786440 | tf_op jit(solution)/shard_map/ppermute | solution.py:292
  26.6 3.2 %copy.27 = f32[16,16,16,16]{3,2,1,0:T(8,128)} copy(f32[16,16,16,16]{2,0,1,3:T(8,128)} %bitcast.81) | data formatting | bytes 524288 | tf_op jit(solution)/shard_map/transpose | solution.py:329
  29.8 2.4 reshape.77.refs_17_.site_matrix_ref
  32.7 2.4 collective-permute-start.3
  35.2 1.6 collective-permute-start.4
  36.8 2.6 %collective-permute-start.18 = (f32[64,1024]{1,0:T(8,128)S(1)}, f32[64,1024]{1,0:T(8,128)S(1)}, u32[]{:S(2)}, u32[]{:S(2)}) collective-permute-start(f32[64,1024]{1,0:T(8,128)S(1)} %collective-permute-done.11.refs_3_), channel_id=1, source_target_pairs={{0,8},{8,0},{16,24},{24,16},{32,40},{40,32},{48,56},{56,48},{64,72... | collective-permute-start | bytes 786440 | tf_op jit(solution)/shard_map/ppermute | solution.py:292
  39.5 1.1 collective-permute-done.18.refs_11_
  41.3 2.2 collective-permute-done.2.refs_1_
  43.5 6.0 %collective-permute-start.5 = (f32[128,1024]{1,0:T(8,128)S(1)}, f32[128,1024]{1,0:T(8,128)S(1)}, u32[]{:S(2)}, u32[]{:S(2)}) collective-permute-start(f32[128,1024]{1,0:T(8,128)S(1)} %constant_dynamic-update-slice_fusion.refs_0_), channel_id=1, source_target_pairs={{0,8},{8,0},{16,24},{24,16},{32,40},{40,32},{48,56},{56,48},{64,72... | collective-permute-start | bytes 1572872 | tf_op jit(solution)/shard_map/ppermute | solution.py:292
  49.5 9.0 %collective-permute-start.6 = (f32[128,1024]{1,0:T(8,128)S(1)}, f32[128,1024]{1,0:T(8,128)S(1)}, u32[]{:S(2)}, u32[]{:S(2)}) collective-permute-start(f32[128,1024]{1,0:T(8,128)S(1)} %collective-permute-done.2.refs_1_), channel_id=1, source_target_pairs={{0,8},{8,0},{16,24},{24,16},{32,40},{40,32},{48,56},{56,48},{64,72... | collective-permute-start | bytes 1572872 | tf_op jit(solution)/shard_map/ppermute | solution.py:292
  58.6 0.9 collective-permute-start.7
  60.0 2.1 collective-permute-done.22.refs_15_
  62.1 14.1 %back.1 = (bf16[1024,1024]{1,0:T(8,128)(2,1)S(1)}, bf16[1024,1024]{1,0:T(8,128)(2,1)S(1)}, bf16[1024,1024]{1,0:T(8,128)(2,1)S(1)}, bf16[1024,1024]{1,0:T(8,128)(...) custom-call(s32[16]{0:T(128)S(1)} %get-tuple-element.47.offsets_ref, ...), custom_call_target="tpu_custom_call" | custom-call | tf_op jit(solution)/shard_map/back/pallas_call | solution.py:202
  76.2 11.6 %edge.1 = (bf16[1024,1024]{1,0:T(8,128)(2,1)S(1)}, bf16[1024,1024]{1,0:T(8,128)(2,1)S(1)}, f32[2,2,64,1024]{3,2,1,0:T(8,128)S(1)}, f32[2,2,64,1024]{3,2,1,0:T(8,128)S(1)}, f32[4,2,64,1024]{3,2,1,0:T(8,128)S(1)}) custom-call(s32[16]{0:T(128)S(1)} %get-tuple-element.44.offsets_ref, s32[8]{0:T(128)S(1)} %and_add_fusion.sources_ref, ...), custom_call_target="tpu_custom_call" | custom-call | tf_op jit(solution)/shard_map/edge/pallas_call | solution.py:222
  87.8 14.9 %first.1 = (bf16[1024,1024]{1,0:T(8,128)(2,1)S(1)}, bf16[1024,1024]{1,0:T(8,128)(2,1)S(1)}, f32[256,256]{1,0:T(8,128)S(1)}) custom-call(f32[1024,1024]{1,0:T(8,128)S(1)} %bitcast.74, bf16[1024,1024]{1,0:T(8,128)(2,1)S(1)} %get-tuple-element.58.right_high_ref, bf16[1024,1024]{1,0:T(8,128)(2,1)S(1)} %get-tuple-element.59.right_low_ref, ...), custom_call_target="tpu_custom_call" | custom-call | tf_op jit(solution)/shard_map/first/pallas_call | solution.py:242
  102.8 3.6 %collective-permute-start.30 = (f32[64,256]{1,0:T(8,128)S(1)}, f32[64,256]{1,0:T(8,128)S(1)}, u32[]{:S(2)}, u32[]{:S(2)}) collective-permute-start(f32[64,256]{1,0:T(8,128)S(1)} %get-tuple-element.101), channel_id=1, source_target_pairs={{0,72},{8,64},{16,88},{24,80},{32,104},{40,96},{48,120},{56,112},{... | collective-permute-start | bytes 196616 | tf_op jit(solution)/shard_map/ppermute | solution.py:292
  106.9 1.6 collective-permute-done.30
  108.5 3.0 %collective-permute-done.28 = f32[64,256]{1,0:T(8,128)S(1)} collective-permute-done((f32[64,256]{1,0:T(8,128)S(1)}, f32[64,256]{1,0:T(8,128)S(1)}, u32[]{:S(2)}, u32[]{:S(2)}) %collective-permute-start.28) | collective-permute-done | bytes 65568 | tf_op jit(solution)/shard_map/ppermute | solution.py:292
  111.5 1.7 collective-permute-start.33
  113.2 1.3 collective-permute-start.32
  114.5 2.5 %collective-permute-done.31 = f32[16,256]{1,0:T(8,128)S(1)} collective-permute-done((f32[16,256]{1,0:T(8,128)S(1)}, f32[16,256]{1,0:T(8,128)S(1)}, u32[]{:S(2)}, u32[]{:S(2)}) %collective-permute-start.31) | collective-permute-done | bytes 16416 | tf_op jit(solution)/shard_map/ppermute | solution.py:292
  117.3 2.6 %collective-permute-start.36 = (f32[16,256]{1,0:T(8,128)S(1)}, f32[16,256]{1,0:T(8,128)S(1)}, u32[]{:S(2)}, u32[]{:S(2)}) collective-permute-start(f32[16,256]{1,0:T(8,128)S(1)} %bitcast_add_fusion.1), channel_id=1, source_target_pairs={{0,3},{1,0},{2,1},{3,2},{4,7},{5,4},{6,5},{7,6},{8,11},{9,8},{10,9... | collective-permute-start | bytes 49160 | tf_op jit(solution)/shard_map/ppermute | solution.py:296
  120.0 1.7 collective-permute-start.35
  121.6 2.1 collective-permute-done.34
  124.7 2.2 collective-permute-done.37
  127.0 2.7 %collective-permute-start.38 = (f32[16,256]{1,0:T(8,128)S(1)}, f32[16,256]{1,0:T(8,128)S(1)}, u32[]{:S(2)}, u32[]{:S(2)}) collective-permute-start(f32[16,256]{1,0:T(8,128)S(1)} %get-tuple-element.91), channel_id=1, source_target_pairs={{0,48},{8,56},{16,0},{24,8},{32,16},{40,24},{48,32},{56,40},{64,11... | collective-permute-start | bytes 49160 | tf_op jit(solution)/shard_map/ppermute | solution.py:292
  129.6 10.8 %right.1 = (f32[512,1024]{1,0:T(8,128)S(1)}, f32[512,1024]{1,0:T(8,128)}) custom-call(s32[16]{0:T(128)S(1)} %get-tuple-element.79.places_ref, bf16[1024,1024]{1,0:T(8,128)(2,1)S(1)} %get-tuple-element.51.refs_8_.back_high_ref, bf16[1024,1024]{1,0:T(8,128)(2,1)S(1)} %get-tuple-element.52.refs_9_.back_low_ref, f32[1024,1024]{1,0:T(8,128)S(1)} %bitcast.75), custom_call_target="tpu_custom_call" | custom-call | tf_op jit(solution)/shard_map/right/pallas_call | solution.py:272
  140.4 5.3 %collective-permute-start.49 = (f32[512,1024]{1,0:T(8,128)}, f32[512,1024]{1,0:T(8,128)}, u32[]{:S(2)}, u32[]{:S(2)}) collective-permute-start(f32[512,1024]{1,0:T(8,128)} %get-tuple-element.81), channel_id=1, source_target_pairs={{0,8},{8,0},{16,24},{24,16},{32,40},{40,32},{48,56},{56,48},{64,72... | collective-permute-start | bytes 6291464 | tf_op jit(solution)/shard_map/ppermute | solution.py:292
  146.1 2.5 %collective-permute-start.23 = (f32[2,2,64,1024]{3,2,1,0:T(8,128)S(1)}, f32[2,2,64,1024]{3,2,1,0:T(8,128)S(1)}, u32[]{:S(2)}, u32[]{:S(2)}) collective-permute-start(f32[2,2,64,1024]{3,2,1,0:T(8,128)S(1)} %get-tuple-element.54), channel_id=1, source_target_pairs={{0,3},{1,0},{2,1},{3,2},{4,7},{5,4},{6,5},{7,6},{8,11},{9,8},{10,9... | collective-permute-start | bytes 3145736 | tf_op jit(solution)/shard_map/ppermute | solution.py:296
  149.0 3.8 %collective-permute-done.39 = f32[16,256]{1,0:T(8,128)S(1)} collective-permute-done((f32[16,256]{1,0:T(8,128)S(1)}, f32[16,256]{1,0:T(8,128)S(1)}, u32[]{:S(2)}, u32[]{:S(2)}) %collective-permute-start.39) | collective-permute-done | bytes 16416 | tf_op jit(solution)/shard_map/ppermute | solution.py:292
  152.8 1.5 collective-permute-start.41
  154.3 10.6 %left.1 = (f32[2,2,64,1024]{3,2,1,0:T(8,128)}, f32[2,2,64,1024]{3,2,1,0:T(8,128)}, f32[4,2,64,1024]{3,2,1,0:T(8,128)S(1)}) custom-call(s32[8]{0:T(128)S(1)} %and_add_fusion.sources_ref, bf16[1024,1024]{1,0:T(8,128)(2,1)S(1)} %get-tuple-element.72.second_high_ref, bf16[1024,1024]{1,0:T(8,128)(2,1)S(1)} %get-tuple-element.73.second_low_ref, ...), custom_call_target="tpu_custom_call" | custom-call | tf_op jit(solution)/shard_map/left/pallas_call | solution.py:255
  164.9 2.7 %collective-permute-start.44 = (f32[2,2,64,1024]{3,2,1,0:T(8,128)}, f32[2,2,64,1024]{3,2,1,0:T(8,128)}, u32[]{:S(2)}, u32[]{:S(2)}) collective-permute-start(f32[2,2,64,1024]{3,2,1,0:T(8,128)} %get-tuple-element.77), channel_id=1, source_target_pairs={{0,3},{1,0},{2,1},{3,2},{4,7},{5,4},{6,5},{7,6},{8,11},{9,8},{10,9... | collective-permute-start | bytes 3145736 | tf_op jit(solution)/shard_map/ppermute | solution.py:296
  167.6 4.6 %collective-permute-done.24 = f32[2,2,64,1024]{3,2,1,0:T(8,128)S(1)} collective-permute-done((f32[2,2,64,1024]{3,2,1,0:T(8,128)S(1)}, f32[2,2,64,1024]{3,2,1,0:T(8,128)S(1)}, u32[]{:S(2)}, u32[]{:S(2)}) %collective-permute-start.24) | collective-permute-done | bytes 1048608 | tf_op jit(solution)/shard_map/ppermute | solution.py:296
  172.2 2.1 collective-permute-start.43
  174.3 1.1 fusion.11
  175.4 2.9 %collective-permute-done.43 = f32[64,256]{1,0:T(8,128)S(1)} collective-permute-done((f32[64,256]{1,0:T(8,128)S(1)}, f32[64,256]{1,0:T(8,128)S(1)}, u32[]{:S(2)}, u32[]{:S(2)}) %collective-permute-start.43) | collective-permute-done | bytes 65568 | tf_op jit(solution)/shard_map/ppermute | solution.py:292
  179.0 2.0 select_n.29
  181.0 3.7 %copy.29 = f32[16,16,16,16]{3,2,1,0:T(8,128)} copy(f32[16,16,16,16]{0,3,1,2:T(8,128)} %bitcast.78) | data formatting | bytes 524288
  185.5 9.2 %collective-permute-done.45 = f32[2,2,64,1024]{3,2,1,0:T(8,128)} collective-permute-done((f32[2,2,64,1024]{3,2,1,0:T(8,128)}, f32[2,2,64,1024]{3,2,1,0:T(8,128)}, u32[]{:S(2)}, u32[]{:S(2)}) %collective-permute-start.45) | collective-permute-done | bytes 1048608 | tf_op jit(solution)/shard_map/ppermute | solution.py:296
  194.8 1.7 fusion.3
  196.4 2.5 %collective-permute-start.47 = (f32[2,64,1024]{2,1,0:T(8,128)S(1)}, f32[2,64,1024]{2,1,0:T(8,128)S(1)}, u32[]{:S(2)}, u32[]{:S(2)}) collective-permute-start(f32[2,64,1024]{2,1,0:T(8,128)S(1)} %get-tuple-element.97), channel_id=1, source_target_pairs={{0,3},{1,0},{2,1},{3,2},{4,7},{5,4},{6,5},{7,6},{8,11},{9,8},{10,9... | collective-permute-start | bytes 1572872 | tf_op jit(solution)/shard_map/ppermute | solution.py:296
  198.9 6.1 %collective-permute-done.26 = f32[2,64,1024]{2,1,0:T(8,128)} collective-permute-done((f32[2,64,1024]{2,1,0:T(8,128)}, f32[2,64,1024]{2,1,0:T(8,128)}, u32[]{:S(2)}, u32[]{:S(2)}) %collective-permute-start.26) | collective-permute-done | bytes 524320 | tf_op jit(solution)/shard_map/ppermute | solution.py:296
  205.0 1.1 fusion.10
  206.9 2.1 slice_add_fusion.1
  209.4 6.7 %collective-permute-done.47 = f32[2,64,1024]{2,1,0:T(8,128)S(1)} collective-permute-done((f32[2,64,1024]{2,1,0:T(8,128)S(1)}, f32[2,64,1024]{2,1,0:T(8,128)S(1)}, u32[]{:S(2)}, u32[]{:S(2)}) %collective-permute-start.47) | collective-permute-done | bytes 524320 | tf_op jit(solution)/shard_map/ppermute | solution.py:296
  216.1 1.2 fusion.2
  217.3 1.7 collective-permute-start.46
  219.8 1.2 copy.28
  221.0 1.5 collective-permute-done.52
  222.5 12.7 %collective-permute-done.50 = f32[2,64,1024]{2,1,0:T(8,128)S(1)} collective-permute-done((f32[2,64,1024]{2,1,0:T(8,128)S(1)}, f32[2,64,1024]{2,1,0:T(8,128)S(1)}, u32[]{:S(2)}, u32[]{:S(2)}) %collective-permute-start.50) | collective-permute-done | bytes 524320 | tf_op jit(solution)/shard_map/ppermute | solution.py:292
  235.4 2.1 collective-permute-start.53
  237.5 1.2 fusion.7
  238.7 1.2 copy.30
  239.9 4.2 %collective-permute-done.53 = f32[64,1024]{1,0:T(8,128)S(1)} collective-permute-done((f32[64,1024]{1,0:T(8,128)S(1)}, f32[64,1024]{1,0:T(8,128)S(1)}, u32[]{:S(2)}, u32[]{:S(2)}) %collective-permute-start.53) | collective-permute-done | bytes 262176 | tf_op jit(solution)/shard_map/ppermute | solution.py:292
  244.2 0.9 reshape.82
  (125 shorter events, 10.9 us)
Async XLA Ops:
  0.6 12.2 %copy-start.8 = (s32[8]{0:T(128)S(1)}, s32[8]{0:T(128)}, u32[]{:S(2)}) copy-start(s32[8]{0:T(128)} %constant.63.clone) | copy-start | bytes 100
  0.7 12.2 %copy-start.10 = (s32[16]{0:T(128)S(1)}, s32[16]{0:T(128)}, u32[]{:S(2)}) copy-start(s32[16]{0:T(128)} %constant.60.clone) | copy-start | bytes 196
  0.7 12.2 %copy-start.11 = (s32[16]{0:T(128)S(1)}, s32[16]{0:T(128)}, u32[]{:S(2)}) copy-start(s32[16]{0:T(128)} %constant.65.clone) | copy-start | bytes 196
  0.7 12.2 %copy-start.12 = (s32[16]{0:T(128)S(1)}, s32[16]{0:T(128)}, u32[]{:S(2)}) copy-start(s32[16]{0:T(128)} %constant.64.clone) | copy-start | bytes 196
  0.7 12.2 %copy-start.13 = (s32[16]{0:T(128)S(1)}, s32[16]{0:T(128)}, u32[]{:S(2)}) copy-start(s32[16]{0:T(128)} %constant.59.clone) | copy-start | bytes 196
  0.7 12.2 %copy-start.14 = (s32[16]{0:T(128)S(1)}, s32[16]{0:T(128)}, u32[]{:S(2)}) copy-start(s32[16]{0:T(128)} %constant.67) | copy-start | bytes 196
  0.7 12.2 %copy-start.15 = (s32[16]{0:T(128)S(1)}, s32[16]{0:T(128)}, u32[]{:S(2)}) copy-start(s32[16]{0:T(128)} %constant.66) | copy-start | bytes 196
  2.8 10.5 %collective-permute-start = (f32[64,1024]{1,0:T(8,128)S(1)}, f32[64,1024]{1,0:T(8,128)S(1)}, u32[]{:S(2)}, u32[]{:S(2)}) collective-permute-start(f32[64,1024]{1,0:T(8,128)S(1)} %reshape.74.refs_0_), channel_id=1, source_target_pairs={{0,64},{8,72},{16,80},{24,88},{32,96},{40,104},{48,112},{56,120},{... | collective-permute-start | bytes 786440 | tf_op jit(solution)/shard_map/ppermute | solution.py:292
  7.3 13.4 %collective-permute-start.9 = (f32[64,1024]{1,0:T(8,128)S(1)}, f32[64,1024]{1,0:T(8,128)S(1)}, u32[]{:S(2)}, u32[]{:S(2)}) collective-permute-start(f32[64,1024]{1,0:T(8,128)S(1)} %reshape.74.refs_0_), channel_id=1, source_target_pairs={{0,16},{8,24},{16,32},{24,40},{32,48},{40,56},{48,0},{56,8},{64,80... | collective-permute-start | bytes 786440 | tf_op jit(solution)/shard_map/ppermute | solution.py:292
  8.6 14.4 %collective-permute-start.10 = (f32[64,1024]{1,0:T(8,128)S(1)}, f32[64,1024]{1,0:T(8,128)S(1)}, u32[]{:S(2)}, u32[]{:S(2)}) collective-permute-start(f32[64,1024]{1,0:T(8,128)S(1)} %reshape.74.refs_0_), channel_id=1, source_target_pairs={{0,48},{8,56},{16,0},{24,8},{32,16},{40,24},{48,32},{56,40},{64,11... | collective-permute-start | bytes 786440 | tf_op jit(solution)/shard_map/ppermute | solution.py:292
  10.0 13.1 %collective-permute-start.11 = (f32[64,1024]{1,0:T(8,128)S(1)}, f32[64,1024]{1,0:T(8,128)S(1)}, u32[]{:S(2)}, u32[]{:S(2)}) collective-permute-start(f32[64,1024]{1,0:T(8,128)S(1)} %reshape.74.refs_0_), channel_id=1, source_target_pairs={{0,32},{8,40},{16,48},{24,56},{32,0},{40,8},{48,16},{56,24},{64,96... | collective-permute-start | bytes 786440 | tf_op jit(solution)/shard_map/ppermute | solution.py:292
  12.7 7.6 %collective-permute-start.1 = (f32[64,1024]{1,0:T(8,128)S(1)}, f32[64,1024]{1,0:T(8,128)S(1)}, u32[]{:S(2)}, u32[]{:S(2)}) collective-permute-start(f32[64,1024]{1,0:T(8,128)S(1)} %reshape.76), channel_id=1, source_target_pairs={{0,64},{8,72},{16,80},{24,88},{32,96},{40,104},{48,112},{56,120},{... | collective-permute-start | bytes 786440 | tf_op jit(solution)/shard_map/ppermute | solution.py:292
  13.3 19.0 %collective-permute-start.15 = (f32[64,1024]{1,0:T(8,128)S(1)}, f32[64,1024]{1,0:T(8,128)S(1)}, u32[]{:S(2)}, u32[]{:S(2)}) collective-permute-start(f32[64,1024]{1,0:T(8,128)S(1)} %reshape.74.refs_0_), channel_id=1, source_target_pairs={{0,8},{8,0},{16,24},{24,16},{32,40},{40,32},{48,56},{56,48},{64,72... | collective-permute-start | bytes 786440 | tf_op jit(solution)/shard_map/ppermute | solution.py:292
  20.3 12.1 %collective-permute-start.12 = (f32[64,1024]{1,0:T(8,128)S(1)}, f32[64,1024]{1,0:T(8,128)S(1)}, u32[]{:S(2)}, u32[]{:S(2)}) collective-permute-start(f32[64,1024]{1,0:T(8,128)S(1)} %collective-permute-done.refs_4_), channel_id=1, source_target_pairs={{0,16},{8,24},{16,32},{24,40},{32,48},{40,56},{48,0},{56,8},{64,80... | collective-permute-start | bytes 786440 | tf_op jit(solution)/shard_map/ppermute | solution.py:292
  20.7 12.0 %collective-permute-start.13 = (f32[64,1024]{1,0:T(8,128)S(1)}, f32[64,1024]{1,0:T(8,128)S(1)}, u32[]{:S(2)}, u32[]{:S(2)}) collective-permute-start(f32[64,1024]{1,0:T(8,128)S(1)} %collective-permute-done.refs_4_), channel_id=1, source_target_pairs={{0,48},{8,56},{16,0},{24,8},{32,16},{40,24},{48,32},{56,40},{64,11... | collective-permute-start | bytes 786440 | tf_op jit(solution)/shard_map/ppermute | solution.py:292
  23.0 12.2 %collective-permute-start.14 = (f32[64,1024]{1,0:T(8,128)S(1)}, f32[64,1024]{1,0:T(8,128)S(1)}, u32[]{:S(2)}, u32[]{:S(2)}) collective-permute-start(f32[64,1024]{1,0:T(8,128)S(1)} %collective-permute-done.refs_4_), channel_id=1, source_target_pairs={{0,32},{8,40},{16,48},{24,56},{32,0},{40,8},{48,16},{56,24},{64,96... | collective-permute-start | bytes 786440 | tf_op jit(solution)/shard_map/ppermute | solution.py:292
  23.2 13.6 %collective-permute-start.16 = (f32[64,1024]{1,0:T(8,128)S(1)}, f32[64,1024]{1,0:T(8,128)S(1)}, u32[]{:S(2)}, u32[]{:S(2)}) collective-permute-start(f32[64,1024]{1,0:T(8,128)S(1)} %collective-permute-done.9.refs_1_), channel_id=1, source_target_pairs={{0,8},{8,0},{16,24},{24,16},{32,40},{40,32},{48,56},{56,48},{64,72... | collective-permute-start | bytes 786440 | tf_op jit(solution)/shard_map/ppermute | solution.py:292
  32.3 7.1 %collective-permute-start.17 = (f32[64,1024]{1,0:T(8,128)S(1)}, f32[64,1024]{1,0:T(8,128)S(1)}, u32[]{:S(2)}, u32[]{:S(2)}) collective-permute-start(f32[64,1024]{1,0:T(8,128)S(1)} %collective-permute-done.10.refs_2_), channel_id=1, source_target_pairs={{0,8},{8,0},{16,24},{24,16},{32,40},{40,32},{48,56},{56,48},{64,72... | collective-permute-start | bytes 786440 | tf_op jit(solution)/shard_map/ppermute | solution.py:292
  32.4 11.1 %collective-permute-start.2 = (f32[128,1024]{1,0:T(8,128)S(1)}, f32[128,1024]{1,0:T(8,128)S(1)}, u32[]{:S(2)}, u32[]{:S(2)}) collective-permute-start(f32[128,1024]{1,0:T(8,128)S(1)} %constant_dynamic-update-slice_fusion.refs_0_), channel_id=1, source_target_pairs={{0,16},{8,24},{16,32},{24,40},{32,48},{40,56},{48,0},{56,8},{64,80... | collective-permute-start | bytes 1572872 | tf_op jit(solution)/shard_map/ppermute | solution.py:292
  32.7 16.8 %collective-permute-start.3 = (f32[128,1024]{1,0:T(8,128)S(1)}, f32[128,1024]{1,0:T(8,128)S(1)}, u32[]{:S(2)}, u32[]{:S(2)}) collective-permute-start(f32[128,1024]{1,0:T(8,128)S(1)} %constant_dynamic-update-slice_fusion.refs_0_), channel_id=1, source_target_pairs={{0,48},{8,56},{16,0},{24,8},{32,16},{40,24},{48,32},{56,40},{64,11... | collective-permute-start | bytes 1572872 | tf_op jit(solution)/shard_map/ppermute | solution.py:292
  35.2 23.4 %collective-permute-start.4 = (f32[128,1024]{1,0:T(8,128)S(1)}, f32[128,1024]{1,0:T(8,128)S(1)}, u32[]{:S(2)}, u32[]{:S(2)}) collective-permute-start(f32[128,1024]{1,0:T(8,128)S(1)} %constant_dynamic-update-slice_fusion.refs_0_), channel_id=1, source_target_pairs={{0,32},{8,40},{16,48},{24,56},{32,0},{40,8},{48,16},{56,24},{64,96... | collective-permute-start | bytes 1572872 | tf_op jit(solution)/shard_map/ppermute | solution.py:292
  36.8 3.8 %collective-permute-start.18 = (f32[64,1024]{1,0:T(8,128)S(1)}, f32[64,1024]{1,0:T(8,128)S(1)}, u32[]{:S(2)}, u32[]{:S(2)}) collective-permute-start(f32[64,1024]{1,0:T(8,128)S(1)} %collective-permute-done.11.refs_3_), channel_id=1, source_target_pairs={{0,8},{8,0},{16,24},{24,16},{32,40},{40,32},{48,56},{56,48},{64,72... | collective-permute-start | bytes 786440 | tf_op jit(solution)/shard_map/ppermute | solution.py:292
  39.4 1.5 collective-permute-start.19
  40.6 18.8 %collective-permute-start.20 = (f32[64,1024]{1,0:T(8,128)S(1)}, f32[64,1024]{1,0:T(8,128)S(1)}, u32[]{:S(2)}, u32[]{:S(2)}) collective-permute-start(f32[64,1024]{1,0:T(8,128)S(1)} %collective-permute-done.12.refs_5_), channel_id=1, source_target_pairs={{0,8},{8,0},{16,24},{24,16},{32,40},{40,32},{48,56},{56,48},{64,72... | collective-permute-start | bytes 786440 | tf_op jit(solution)/shard_map/ppermute | solution.py:292
  41.0 18.5 %collective-permute-start.21 = (f32[64,1024]{1,0:T(8,128)S(1)}, f32[64,1024]{1,0:T(8,128)S(1)}, u32[]{:S(2)}, u32[]{:S(2)}) collective-permute-start(f32[64,1024]{1,0:T(8,128)S(1)} %collective-permute-done.13.refs_6_), channel_id=1, source_target_pairs={{0,8},{8,0},{16,24},{24,16},{32,40},{40,32},{48,56},{56,48},{64,72... | collective-permute-start | bytes 786440 | tf_op jit(solution)/shard_map/ppermute | solution.py:292
  43.5 32.6 %collective-permute-start.5 = (f32[128,1024]{1,0:T(8,128)S(1)}, f32[128,1024]{1,0:T(8,128)S(1)}, u32[]{:S(2)}, u32[]{:S(2)}) collective-permute-start(f32[128,1024]{1,0:T(8,128)S(1)} %constant_dynamic-update-slice_fusion.refs_0_), channel_id=1, source_target_pairs={{0,8},{8,0},{16,24},{24,16},{32,40},{40,32},{48,56},{56,48},{64,72... | collective-permute-start | bytes 1572872 | tf_op jit(solution)/shard_map/ppermute | solution.py:292
  49.5 26.7 %collective-permute-start.6 = (f32[128,1024]{1,0:T(8,128)S(1)}, f32[128,1024]{1,0:T(8,128)S(1)}, u32[]{:S(2)}, u32[]{:S(2)}) collective-permute-start(f32[128,1024]{1,0:T(8,128)S(1)} %collective-permute-done.2.refs_1_), channel_id=1, source_target_pairs={{0,8},{8,0},{16,24},{24,16},{32,40},{40,32},{48,56},{56,48},{64,72... | collective-permute-start | bytes 1572872 | tf_op jit(solution)/shard_map/ppermute | solution.py:292
  58.6 17.6 %collective-permute-start.7 = (f32[128,1024]{1,0:T(8,128)S(1)}, f32[128,1024]{1,0:T(8,128)S(1)}, u32[]{:S(2)}, u32[]{:S(2)}) collective-permute-start(f32[128,1024]{1,0:T(8,128)S(1)} %collective-permute-done.3.refs_2_), channel_id=1, source_target_pairs={{0,8},{8,0},{16,24},{24,16},{32,40},{40,32},{48,56},{56,48},{64,72... | collective-permute-start | bytes 1572872 | tf_op jit(solution)/shard_map/ppermute | solution.py:292
  59.4 16.8 %collective-permute-start.8 = (f32[128,1024]{1,0:T(8,128)S(1)}, f32[128,1024]{1,0:T(8,128)S(1)}, u32[]{:S(2)}, u32[]{:S(2)}) collective-permute-start(f32[128,1024]{1,0:T(8,128)S(1)} %collective-permute-done.4.refs_3_), channel_id=1, source_target_pairs={{0,8},{8,0},{16,24},{24,16},{32,40},{40,32},{48,56},{56,48},{64,72... | collective-permute-start | bytes 1572872 | tf_op jit(solution)/shard_map/ppermute | solution.py:292
  59.4 2.6 %collective-permute-start.22 = (f32[64,1024]{1,0:T(8,128)S(1)}, f32[64,1024]{1,0:T(8,128)S(1)}, u32[]{:S(2)}, u32[]{:S(2)}) collective-permute-start(f32[64,1024]{1,0:T(8,128)S(1)} %collective-permute-done.14.refs_7_), channel_id=1, source_target_pairs={{0,8},{8,0},{16,24},{24,16},{32,40},{40,32},{48,56},{56,48},{64,72... | collective-permute-start | bytes 786440 | tf_op jit(solution)/shard_map/ppermute | solution.py:292
  87.8 86.5 %copy-start.1 = (f32[4,2,64,1024]{3,2,1,0:T(8,128)}, f32[4,2,64,1024]{3,2,1,0:T(8,128)S(1)}, u32[]{:S(2)}) copy-start(f32[4,2,64,1024]{3,2,1,0:T(8,128)S(1)} %get-tuple-element.53) | copy-start | bytes 6291460
  102.8 5.7 %collective-permute-start.30 = (f32[64,256]{1,0:T(8,128)S(1)}, f32[64,256]{1,0:T(8,128)S(1)}, u32[]{:S(2)}, u32[]{:S(2)}) collective-permute-start(f32[64,256]{1,0:T(8,128)S(1)} %get-tuple-element.101), channel_id=1, source_target_pairs={{0,72},{8,64},{16,88},{24,80},{32,104},{40,96},{48,120},{56,112},{... | collective-permute-start | bytes 196616 | tf_op jit(solution)/shard_map/ppermute | solution.py:292
  106.4 5.0 %collective-permute-start.28 = (f32[64,256]{1,0:T(8,128)S(1)}, f32[64,256]{1,0:T(8,128)S(1)}, u32[]{:S(2)}, u32[]{:S(2)}) collective-permute-start(f32[64,256]{1,0:T(8,128)S(1)} %get-tuple-element.102), channel_id=1, source_target_pairs={{0,64},{8,72},{16,80},{24,88},{32,96},{40,104},{48,112},{56,120},{... | collective-permute-start | bytes 196616 | tf_op jit(solution)/shard_map/ppermute | solution.py:292
  106.4 5.0 %collective-permute-start.29 = (f32[64,256]{1,0:T(8,128)S(1)}, f32[64,256]{1,0:T(8,128)S(1)}, u32[]{:S(2)}, u32[]{:S(2)}) collective-permute-start(f32[64,256]{1,0:T(8,128)S(1)} %get-tuple-element.100), channel_id=1, source_target_pairs={{0,8},{8,0},{16,24},{24,16},{32,40},{40,32},{48,56},{56,48},{64,72... | collective-permute-start | bytes 196616 | tf_op jit(solution)/shard_map/ppermute | solution.py:292
  111.5 3.0 %collective-permute-start.33 = (f32[16,256]{1,0:T(8,128)S(1)}, f32[16,256]{1,0:T(8,128)S(1)}, u32[]{:S(2)}, u32[]{:S(2)}) collective-permute-start(f32[16,256]{1,0:T(8,128)S(1)} %get-tuple-element.104), channel_id=1, source_target_pairs={{0,48},{8,56},{16,0},{24,8},{32,16},{40,24},{48,32},{56,40},{64,11... | collective-permute-start | bytes 49160 | tf_op jit(solution)/shard_map/ppermute | solution.py:292
  113.2 3.8 %collective-permute-start.31 = (f32[16,256]{1,0:T(8,128)S(1)}, f32[16,256]{1,0:T(8,128)S(1)}, u32[]{:S(2)}, u32[]{:S(2)}) collective-permute-start(f32[16,256]{1,0:T(8,128)S(1)} %get-tuple-element.105), channel_id=1, source_target_pairs={{0,16},{8,24},{16,32},{24,40},{32,48},{40,56},{48,0},{56,8},{64,80... | collective-permute-start | bytes 49160 | tf_op jit(solution)/shard_map/ppermute | solution.py:292
  113.2 4.1 %collective-permute-start.32 = (f32[16,256]{1,0:T(8,128)S(1)}, f32[16,256]{1,0:T(8,128)S(1)}, u32[]{:S(2)}, u32[]{:S(2)}) collective-permute-start(f32[16,256]{1,0:T(8,128)S(1)} %get-tuple-element.103), channel_id=1, source_target_pairs={{0,32},{8,40},{16,48},{24,56},{32,0},{40,8},{48,16},{56,24},{64,96... | collective-permute-start | bytes 49160 | tf_op jit(solution)/shard_map/ppermute | solution.py:292
  117.3 4.3 %collective-permute-start.36 = (f32[16,256]{1,0:T(8,128)S(1)}, f32[16,256]{1,0:T(8,128)S(1)}, u32[]{:S(2)}, u32[]{:S(2)}) collective-permute-start(f32[16,256]{1,0:T(8,128)S(1)} %bitcast_add_fusion.1), channel_id=1, source_target_pairs={{0,3},{1,0},{2,1},{3,2},{4,7},{5,4},{6,5},{7,6},{8,11},{9,8},{10,9... | collective-permute-start | bytes 49160 | tf_op jit(solution)/shard_map/ppermute | solution.py:296
  120.0 3.8 %collective-permute-start.34 = (f32[16,256]{1,0:T(8,128)S(1)}, f32[16,256]{1,0:T(8,128)S(1)}, u32[]{:S(2)}, u32[]{:S(2)}) collective-permute-start(f32[16,256]{1,0:T(8,128)S(1)} %bitcast_add_fusion.1), channel_id=1, source_target_pairs={{0,1},{1,2},{2,3},{3,0},{4,5},{5,6},{6,7},{7,4},{8,9},{9,10},{10,1... | collective-permute-start | bytes 49160 | tf_op jit(solution)/shard_map/ppermute | solution.py:296
  120.0 4.1 %collective-permute-start.35 = (f32[16,256]{1,0:T(8,128)S(1)}, f32[16,256]{1,0:T(8,128)S(1)}, u32[]{:S(2)}, u32[]{:S(2)}) collective-permute-start(f32[16,256]{1,0:T(8,128)S(1)} %bitcast_add_fusion.1), channel_id=1, source_target_pairs={{0,2},{1,3},{2,0},{3,1},{4,6},{5,7},{6,4},{7,5},{8,10},{9,11},{10,... | collective-permute-start | bytes 49160 | tf_op jit(solution)/shard_map/ppermute | solution.py:296
  124.1 2.9 %collective-permute-start.37 = (f32[16,256]{1,0:T(8,128)S(1)}, f32[16,256]{1,0:T(8,128)S(1)}, u32[]{:S(2)}, u32[]{:S(2)}) collective-permute-start(f32[16,256]{1,0:T(8,128)S(1)} %add_add_fusion.1), channel_id=1, source_target_pairs={{0,4},{1,5},{2,6},{3,7},{4,0},{5,1},{6,2},{7,3},{8,12},{9,13},{10,... | collective-permute-start | bytes 49160 | tf_op jit(solution)/shard_map/ppermute | solution.py:296
  127.0 21.7 %collective-permute-start.38 = (f32[16,256]{1,0:T(8,128)S(1)}, f32[16,256]{1,0:T(8,128)S(1)}, u32[]{:S(2)}, u32[]{:S(2)}) collective-permute-start(f32[16,256]{1,0:T(8,128)S(1)} %get-tuple-element.91), channel_id=1, source_target_pairs={{0,48},{8,56},{16,0},{24,8},{32,16},{40,24},{48,32},{56,40},{64,11... | collective-permute-start | bytes 49160 | tf_op jit(solution)/shard_map/ppermute | solution.py:292
  140.4 66.5 %collective-permute-start.49 = (f32[512,1024]{1,0:T(8,128)}, f32[512,1024]{1,0:T(8,128)}, u32[]{:S(2)}, u32[]{:S(2)}) collective-permute-start(f32[512,1024]{1,0:T(8,128)} %get-tuple-element.81), channel_id=1, source_target_pairs={{0,8},{8,0},{16,24},{24,16},{32,40},{40,32},{48,56},{56,48},{64,72... | collective-permute-start | bytes 6291464 | tf_op jit(solution)/shard_map/ppermute | solution.py:292
  145.7 26.5 %collective-permute-start.24 = (f32[2,2,64,1024]{3,2,1,0:T(8,128)S(1)}, f32[2,2,64,1024]{3,2,1,0:T(8,128)S(1)}, u32[]{:S(2)}, u32[]{:S(2)}) collective-permute-start(f32[2,2,64,1024]{3,2,1,0:T(8,128)S(1)} %get-tuple-element.55), channel_id=1, source_target_pairs={{0,1},{1,2},{2,3},{3,0},{4,5},{5,6},{6,7},{7,4},{8,9},{9,10},{10,1... | collective-permute-start | bytes 3145736 | tf_op jit(solution)/shard_map/ppermute | solution.py:296
  146.1 28.1 %collective-permute-start.23 = (f32[2,2,64,1024]{3,2,1,0:T(8,128)S(1)}, f32[2,2,64,1024]{3,2,1,0:T(8,128)S(1)}, u32[]{:S(2)}, u32[]{:S(2)}) collective-permute-start(f32[2,2,64,1024]{3,2,1,0:T(8,128)S(1)} %get-tuple-element.54), channel_id=1, source_target_pairs={{0,3},{1,0},{2,1},{3,2},{4,7},{5,4},{6,5},{7,6},{8,11},{9,8},{10,9... | collective-permute-start | bytes 3145736 | tf_op jit(solution)/shard_map/ppermute | solution.py:296
  148.7 4.1 %collective-permute-start.39 = (f32[16,256]{1,0:T(8,128)S(1)}, f32[16,256]{1,0:T(8,128)S(1)}, u32[]{:S(2)}, u32[]{:S(2)}) collective-permute-start(f32[16,256]{1,0:T(8,128)S(1)} %get-tuple-element.91), channel_id=1, source_target_pairs={{0,32},{8,40},{16,48},{24,56},{32,0},{40,8},{48,16},{56,24},{64,96... | collective-permute-start | bytes 49160 | tf_op jit(solution)/shard_map/ppermute | solution.py:292
  148.7 4.1 %collective-permute-start.40 = (f32[16,256]{1,0:T(8,128)S(1)}, f32[16,256]{1,0:T(8,128)S(1)}, u32[]{:S(2)}, u32[]{:S(2)}) collective-permute-start(f32[16,256]{1,0:T(8,128)S(1)} %get-tuple-element.91), channel_id=1, source_target_pairs={{0,16},{8,24},{16,32},{24,40},{32,48},{40,56},{48,0},{56,8},{64,80... | collective-permute-start | bytes 49160 | tf_op jit(solution)/shard_map/ppermute | solution.py:292
  152.8 12.1 %collective-permute-start.41 = (f32[64,256]{1,0:T(8,128)S(1)}, f32[64,256]{1,0:T(8,128)S(1)}, u32[]{:S(2)}, u32[]{:S(2)}) collective-permute-start(f32[64,256]{1,0:T(8,128)S(1)} %constant_dynamic-slice_fusion), channel_id=1, source_target_pairs={{0,64},{8,72},{16,80},{24,88},{32,96},{40,104},{48,112},{56,120},{... | collective-permute-start | bytes 196616 | tf_op jit(solution)/shard_map/ppermute | solution.py:292
  164.9 29.8 %collective-permute-start.45 = (f32[2,2,64,1024]{3,2,1,0:T(8,128)}, f32[2,2,64,1024]{3,2,1,0:T(8,128)}, u32[]{:S(2)}, u32[]{:S(2)}) collective-permute-start(f32[2,2,64,1024]{3,2,1,0:T(8,128)} %get-tuple-element.78), channel_id=1, source_target_pairs={{0,1},{1,2},{2,3},{3,0},{4,5},{5,6},{6,7},{7,4},{8,9},{9,10},{10,1... | collective-permute-start | bytes 3145736 | tf_op jit(solution)/shard_map/ppermute | solution.py:296
  164.9 29.8 %collective-permute-start.44 = (f32[2,2,64,1024]{3,2,1,0:T(8,128)}, f32[2,2,64,1024]{3,2,1,0:T(8,128)}, u32[]{:S(2)}, u32[]{:S(2)}) collective-permute-start(f32[2,2,64,1024]{3,2,1,0:T(8,128)} %get-tuple-element.77), channel_id=1, source_target_pairs={{0,3},{1,0},{2,1},{3,2},{4,7},{5,4},{6,5},{7,6},{8,11},{9,8},{10,9... | collective-permute-start | bytes 3145736 | tf_op jit(solution)/shard_map/ppermute | solution.py:296
  172.2 6.1 %collective-permute-start.43 = (f32[64,256]{1,0:T(8,128)S(1)}, f32[64,256]{1,0:T(8,128)S(1)}, u32[]{:S(2)}, u32[]{:S(2)}) collective-permute-start(f32[64,256]{1,0:T(8,128)S(1)} %constant_dynamic-slice_fusion), channel_id=1, source_target_pairs={{0,72},{8,64},{16,88},{24,80},{32,104},{40,96},{48,120},{56,112},{... | collective-permute-start | bytes 196616 | tf_op jit(solution)/shard_map/ppermute | solution.py:292
  174.3 4.7 %collective-permute-start.42 = (f32[64,256]{1,0:T(8,128)S(1)}, f32[64,256]{1,0:T(8,128)S(1)}, u32[]{:S(2)}, u32[]{:S(2)}) collective-permute-start(f32[64,256]{1,0:T(8,128)S(1)} %constant_dynamic-slice_fusion), channel_id=1, source_target_pairs={{0,8},{8,0},{16,24},{24,16},{32,40},{40,32},{48,56},{56,48},{64,72... | collective-permute-start | bytes 196616 | tf_op jit(solution)/shard_map/ppermute | solution.py:292
  178.3 26.7 %collective-permute-start.26 = (f32[2,64,1024]{2,1,0:T(8,128)}, f32[2,64,1024]{2,1,0:T(8,128)}, u32[]{:S(2)}, u32[]{:S(2)}) collective-permute-start(f32[2,64,1024]{2,1,0:T(8,128)} %get-tuple-element.99), channel_id=1, source_target_pairs={{0,3},{1,0},{2,1},{3,2},{4,7},{5,4},{6,5},{7,6},{8,11},{9,8},{10,9... | collective-permute-start | bytes 1572872 | tf_op jit(solution)/shard_map/ppermute | solution.py:296
  184.7 20.3 %copy-start.2 = (f32[4,2,64,1024]{3,2,1,0:T(8,128)S(1)}, f32[4,2,64,1024]{3,2,1,0:T(8,128)}, u32[]{:S(2)}) copy-start(f32[4,2,64,1024]{3,2,1,0:T(8,128)} %copy-done.1) | copy-start | bytes 6291460
  184.7 20.3 %copy-start.6 = (f32[2,2,64,1024]{3,2,1,0:T(8,128)S(1)}, f32[2,2,64,1024]{3,2,1,0:T(8,128)}, u32[]{:S(2)}) copy-start(f32[2,2,64,1024]{3,2,1,0:T(8,128)} %copy-done.5) | copy-start | bytes 3145732
  184.7 32.6 %collective-permute-start.25 = (f32[2,64,1024]{2,1,0:T(8,128)}, f32[2,64,1024]{2,1,0:T(8,128)S(1)}, u32[]{:S(2)}, u32[]{:S(2)}) collective-permute-start(f32[2,64,1024]{2,1,0:T(8,128)} %get-tuple-element.98), channel_id=1, source_target_pairs={{0,1},{1,2},{2,3},{3,0},{4,5},{5,6},{6,7},{7,4},{8,9},{9,10},{10,1... | collective-permute-start | bytes 1572872 | tf_op jit(solution)/shard_map/ppermute | solution.py:296
  196.4 19.7 %collective-permute-start.47 = (f32[2,64,1024]{2,1,0:T(8,128)S(1)}, f32[2,64,1024]{2,1,0:T(8,128)S(1)}, u32[]{:S(2)}, u32[]{:S(2)}) collective-permute-start(f32[2,64,1024]{2,1,0:T(8,128)S(1)} %get-tuple-element.97), channel_id=1, source_target_pairs={{0,3},{1,0},{2,1},{3,2},{4,7},{5,4},{6,5},{7,6},{8,11},{9,8},{10,9... | collective-permute-start | bytes 1572872 | tf_op jit(solution)/shard_map/ppermute | solution.py:296
  206.1 12.8 %collective-permute-start.27 = (f32[2,64,1024]{2,1,0:T(8,128)S(1)}, f32[2,64,1024]{2,1,0:T(8,128)S(1)}, u32[]{:S(2)}, u32[]{:S(2)}) collective-permute-start(f32[2,64,1024]{2,1,0:T(8,128)S(1)} %fusion.10), channel_id=1, source_target_pairs={{0,4},{1,5},{2,6},{3,7},{4,0},{5,1},{6,2},{7,3},{8,12},{9,13},{10,... | collective-permute-start | bytes 1572872 | tf_op jit(solution)/shard_map/ppermute | solution.py:296
  209.0 13.6 %collective-permute-start.52 = (f32[2,64,1024]{2,1,0:T(8,128)S(1)}, f32[2,64,1024]{2,1,0:T(8,128)S(1)}, u32[]{:S(2)}, u32[]{:S(2)}) collective-permute-start(f32[2,64,1024]{2,1,0:T(8,128)S(1)} %bitcast.86), channel_id=1, source_target_pairs={{0,32},{8,40},{16,48},{24,56},{32,0},{40,8},{48,16},{56,24},{64,96... | collective-permute-start | bytes 1572872 | tf_op jit(solution)/shard_map/ppermute | solution.py:292
  209.1 26.1 %collective-permute-start.50 = (f32[2,64,1024]{2,1,0:T(8,128)S(1)}, f32[2,64,1024]{2,1,0:T(8,128)S(1)}, u32[]{:S(2)}, u32[]{:S(2)}) collective-permute-start(f32[2,64,1024]{2,1,0:T(8,128)S(1)} %bitcast.85), channel_id=1, source_target_pairs={{0,16},{8,24},{16,32},{24,40},{32,48},{40,56},{48,0},{56,8},{64,80... | collective-permute-start | bytes 1572872 | tf_op jit(solution)/shard_map/ppermute | solution.py:292
  216.1 19.1 %collective-permute-start.51 = (f32[2,64,1024]{2,1,0:T(8,128)S(1)}, f32[2,64,1024]{2,1,0:T(8,128)S(1)}, u32[]{:S(2)}, u32[]{:S(2)}) collective-permute-start(f32[2,64,1024]{2,1,0:T(8,128)S(1)} %bitcast.84), channel_id=1, source_target_pairs={{0,48},{8,56},{16,0},{24,8},{32,16},{40,24},{48,32},{56,40},{64,11... | collective-permute-start | bytes 1572872 | tf_op jit(solution)/shard_map/ppermute | solution.py:292
  217.3 20.2 %collective-permute-start.46 = (f32[2,64,1024]{2,1,0:T(8,128)S(1)}, f32[2,64,1024]{2,1,0:T(8,128)S(1)}, u32[]{:S(2)}, u32[]{:S(2)}) collective-permute-start(f32[2,64,1024]{2,1,0:T(8,128)S(1)} %get-tuple-element.96), channel_id=1, source_target_pairs={{0,1},{1,2},{2,3},{3,0},{4,5},{5,6},{6,7},{7,4},{8,9},{9,10},{10,1... | collective-permute-start | bytes 1572872 | tf_op jit(solution)/shard_map/ppermute | solution.py:296
  219.0 18.5 %collective-permute-start.48 = (f32[2,64,1024]{2,1,0:T(8,128)S(1)}, f32[2,64,1024]{2,1,0:T(8,128)S(1)}, u32[]{:S(2)}, u32[]{:S(2)}) collective-permute-start(f32[2,64,1024]{2,1,0:T(8,128)S(1)} %fusion.2), channel_id=1, source_target_pairs={{0,4},{1,5},{2,6},{3,7},{4,0},{5,1},{6,2},{7,3},{8,12},{9,13},{10,... | collective-permute-start | bytes 1572872 | tf_op jit(solution)/shard_map/ppermute | solution.py:296
  235.4 8.7 %collective-permute-start.53 = (f32[64,1024]{1,0:T(8,128)S(1)}, f32[64,1024]{1,0:T(8,128)S(1)}, u32[]{:S(2)}, u32[]{:S(2)}) collective-permute-start(f32[64,1024]{1,0:T(8,128)S(1)} %slice_bitcast_fusion), channel_id=1, source_target_pairs={{0,64},{8,72},{16,80},{24,88},{32,96},{40,104},{48,112},{56,120},{... | collective-permute-start | bytes 786440 | tf_op jit(solution)/shard_map/ppermute | solution.py:292
  (7 other events, 73.3 us)

commit v2 on v1

--- a/solution.py
+++ b/solution.py
@@ -12,7 +12,7 @@
 NN = (((1,), (0,)), ((), ()))
 NT = (((1,), (1,)), ((), ()))
 TN = (((0,), (0,)), ((), ()))
-PARAMS = pltpu.CompilerParams(vmem_limit_bytes=28 << 20)
+PARAMS = pltpu.CompilerParams(vmem_limit_bytes=16 << 20)
 ROWS = 256
 CHUNKS = 4
 WIDTH = 512
@@ -299,8 +299,9 @@
 def col_reduce(ahead, behind, kept):
     from_behind = col_permute(ahead, 0, 1)
     from_ahead = col_permute(behind, 0, 3)
-    far_behind = col_permute(kept[0] + from_behind[0], 0, 1)
-    far_ahead = col_permute(kept[1] + from_ahead[0], 0, 3)
+    sums = kept[0] + from_behind[0], kept[1] + from_ahead[0]
+    far_behind = col_permute(sums[0], 0, 1)
+    far_ahead = col_permute(sums[1], 0, 3)
     other = kept[3] + from_behind[1] + far_ahead
     same = kept[2] + from_ahead[1] + far_behind
     return jnp.transpose(same + col_permute(other, 1, 0), (1, 0, 2))
@@ -336,19 +337,19 @@
     sources = ((col >> 2) ^ others) * 4 + ((col + steps) & 3)
     blocks = np.array([(i % 2) * 8 + i // 2 for i in range(16)], np.int32)
     places = (((blocks & 1) ^ core) * 8 + (((blocks >> 1) - y) & 3) * 2 + ((blocks >> 3) ^ z)) * 64
-    corners = [(core * 2 + z) ^ k for k in range(4)]
+    cores, sides = [core, core ^ 1], [z, z ^ 1]
     ahead = [(y + k) & 3 for k in range(4)]
-    first_row, at_low_z, at_low_core = ((4 - y) & 3) * 16, z == 0, core == 0
+    first_row, at_low_z, at_low_core = ((4 - y) & 3) * 32, z == 0, core == 0
 
     early = dense(cotangent)
     early, right_isometry = lax.optimization_barrier((early, right_isometry))
     other = row_permute(early, 1, 0, 0)
     nearest = [row_permute(early, 0, steps, 0) for steps in (1, 3, 2)]
     values = (cotangent_offsets, isometry_offsets, sources, places)
-    indices = (*corners, *ahead, first_row, at_low_z, at_low_core)
+    indices = (*cores, *sides, *ahead, first_row, at_low_z, at_low_core)
     other, values, indices = lax.optimization_barrier((other, values, indices))
     cotangent_offsets, isometry_offsets, sources, places = values
-    corners, ahead, (first_row, at_low_z, at_low_core) = indices[:4], indices[4:8], indices[8:]
+    cores, sides, ahead, (first_row, at_low_z, at_low_core) = indices[:2], indices[2:4], indices[4:8], indices[8:]
     own = dense(right_isometry)
     pair = jnp.concatenate([own, row_permute(own, 1, 0, 0)], 0)
     pieces = [early, *nearest, other, *(row_permute(other, 0, steps, 0) for steps in (1, 3, 2))]
@@ -368,20 +369,24 @@
 
     right_own, right_other = right_call(places, back_split, edge_rows)
 
-    part = site_terms.reshape(4, 64, 256)
-    sends = [row_permute(take(part, corners[k]), k & 1, 0, k >> 1) for k in (1, 2, 3)]
-    part = take(part, corners[0]) + sum(sends)
+    part = site_terms.reshape(2, 4, 2, 16, 256)
+
+    def corner(k):
+        start = (cores[k >> 1], 0, sides[k & 1], 0, 0)
+        return lax.dynamic_slice(part, start, (1, 4, 1, 16, 256), allow_negative_indices=False).reshape(64, 256)
+
+    part = corner(0) + sum(row_permute(corner(k), k & 1, 0, k >> 1) for k in (1, 2, 3))
     part = part.reshape(4, 16, 256)
     part = take(part, ahead[0]) + sum(row_permute(take(part, ahead[k]), 0, k, 0) for k in (1, 2, 3))
+    part = part + col_permute(part, 1, 0)
     part = part + sum(col_permute(part, 0, k) for k in (1, 2, 3))
-    part = part + col_permute(part, 1, 0)
+    other = row_permute(part, 1, 0, 0)
+    part = jnp.where(at_low_z, jnp.concatenate([part, other], 0), jnp.concatenate([other, part], 0))
     ring = [part] + [row_permute(part, 0, k, 0) for k in (3, 2, 1)]
     ring = jnp.concatenate(ring + ring, 0)
-    part = lax.dynamic_slice(ring, (first_row, 0), (64, 256), allow_negative_indices=False)
-    near, across, far = (row_permute(part, k & 1, 0, k >> 1) for k in (1, 2, 3))
-    low = jnp.where(at_low_z, jnp.concatenate([part, near], 0), jnp.concatenate([near, part], 0))
-    high = jnp.where(at_low_z, jnp.concatenate([across, far], 0), jnp.concatenate([far, across], 0))
-    part = jnp.where(at_low_core, jnp.concatenate([low, high], 0), jnp.concatenate([high, low], 0))
+    part = lax.dynamic_slice(ring, (first_row, 0), (128, 256), allow_negative_indices=False)
+    other = row_permute(part, 0, 0, 1)
+    part = jnp.where(at_low_core, jnp.concatenate([part, other], 0), jnp.concatenate([other, part], 0))
     site_gradient = jnp.transpose(part.reshape(16, 16, 16, 16), (3, 1, 0, 2))
 
     right_own = right_own.reshape(4, 2, 64, 1024)

time: 246 us -> 244 us (level)
  the two profiles are of different devices: /device:TPU:1 before, /device:TPU:26 now
where the time goes in v2:
time: 244 us
  waiting for transfers between devices  96.3 us (39%)
  Pallas kernels  62.2 us (25%)
  starting transfers between devices  57.5 us (24%)
  local copies, waits for them, and re-layouts  17.9 us (7%)
  other arithmetic  8.66 us (4%)
    ppermute x39, waiting for transfers between devices, row_permute(): return lax.ppermute(value, 'row', pairs)  65.3 us
    ppermute x39, starting transfers between devices, row_permute(): return lax.ppermute(value, 'row', pairs)  38.6 us
    ppermute x14, waiting for transfers between devices, col_permute(): lax.ppermute(value, 'col', [(i, (i // 4 ^ z) * 4 + (i + x) % 4) for i in...  31 us
    ppermute x14, starting transfers between devices, col_permute(): lax.ppermute(value, 'col', [(i, (i // 4 ^ z) * 4 + (i + x) % 4) for i in...  19 us
    pallas_call x1, Pallas kernels, first_call(): pl.pallas_call(first_kernel, out_shape=(SQUARE, SQUARE, jax.ShapeDtypeStr...  15.1 us
    pallas_call x1, Pallas kernels, back_call(): pl.pallas_call(functools.partial(back_kernel, len(pieces)), out_shape=(SQ...  14.2 us
    pallas_call x1, Pallas kernels, edge_call(): pl.pallas_call(functools.partial(edge_kernel, len(pieces)), out_shape=(SQ...  11.6 us
    pallas_call x1, Pallas kernels, right_call(): pl.pallas_call(right_kernel, out_shape=(jax.ShapeDtypeStruct((512, 1024),...  10.8 us
  transfers between devices with their start and end apart: 53, of which 26 were waited for; matrix products, arithmetic and copies ran while one was open for 10% of the time, Pallas kernels for 15%

profile of v2, /device:TPU:26, one launch (start us, length us, event | category | flops | bytes accessed | tf_op | source)
XLA Modules:
  0.0 243.7 jit_solution(8193111440179025720)
XLA Ops:
  0.8 1.6 copy.25
  2.8 3.9 %collective-permute-start = (f32[64,1024]{1,0:T(8,128)S(1)}, f32[64,1024]{1,0:T(8,128)S(1)}, u32[]{:S(2)}, u32[]{:S(2)}) collective-permute-start(f32[64,1024]{1,0:T(8,128)S(1)} %reshape.86.refs_0_), channel_id=1, source_target_pairs={{0,64},{8,72},{16,80},{24,88},{32,96},{40,104},{48,112},{56,120},{... | collective-permute-start | bytes 786440 | tf_op jit(solution)/shard_map/ppermute | solution.py:292
  7.0 1.8 collective-permute-start.10
  8.8 1.2 collective-permute-start.11
  11.3 2.2 collective-permute-done.refs_4_
  13.5 6.0 %collective-permute-done.1 = f32[64,1024]{1,0:T(8,128)S(1)} collective-permute-done((f32[64,1024]{1,0:T(8,128)S(1)}, f32[64,1024]{1,0:T(8,128)S(1)}, u32[]{:S(2)}, u32[]{:S(2)}) %collective-permute-start.1) | collective-permute-done | bytes 262176 | tf_op jit(solution)/shard_map/ppermute | solution.py:292
  19.5 2.2 collective-permute-start.12
  21.7 2.1 collective-permute-start.14
  23.8 3.2 %copy.27 = f32[16,16,16,16]{3,2,1,0:T(8,128)} copy(f32[16,16,16,16]{2,0,1,3:T(8,128)} %bitcast.77) | data formatting | bytes 524288 | tf_op jit(solution)/shard_map/transpose | solution.py:330
  27.0 2.4 %reshape.89.refs_17_.site_matrix_ref = f32[256,256]{1,0:T(8,128)S(1)} reshape(f32[16,16,16,16]{3,2,1,0:T(8,128)} %copy.27) | data formatting | bytes 524288 | tf_op jit(solution)/shard_map/reshape | solution.py:330
  31.2 3.7 %collective-permute-start.2 = (f32[128,1024]{1,0:T(8,128)S(1)}, f32[128,1024]{1,0:T(8,128)S(1)}, u32[]{:S(2)}, u32[]{:S(2)}) collective-permute-start(f32[128,1024]{1,0:T(8,128)S(1)} %constant_dynamic-update-slice_fusion.refs_0_), channel_id=1, source_target_pairs={{0,16},{8,24},{16,32},{24,40},{32,48},{40,56},{48,0},{56,8},{64,80... | collective-permute-start | bytes 1572872 | tf_op jit(solution)/shard_map/ppermute | solution.py:292
  34.8 1.5 collective-permute-start.4
  38.3 7.6 %collective-permute-done.2.refs_1_ = f32[128,1024]{1,0:T(8,128)S(1)} collective-permute-done((f32[128,1024]{1,0:T(8,128)S(1)}, f32[128,1024]{1,0:T(8,128)S(1)}, u32[]{:S(2)}, u32[]{:S(2)}) %collective-permute-start.2) | collective-permute-done | bytes 524320 | tf_op jit(solution)/shard_map/ppermute | solution.py:292
  46.0 11.7 %collective-permute-done.3.refs_2_ = f32[128,1024]{1,0:T(8,128)S(1)} collective-permute-done((f32[128,1024]{1,0:T(8,128)S(1)}, f32[128,1024]{1,0:T(8,128)S(1)}, u32[]{:S(2)}, u32[]{:S(2)}) %collective-permute-start.3) | collective-permute-done | bytes 524320 | tf_op jit(solution)/shard_map/ppermute | solution.py:292
  58.7 2.8 %collective-permute-done.22.refs_15_ = f32[64,1024]{1,0:T(8,128)S(1)} collective-permute-done((f32[64,1024]{1,0:T(8,128)S(1)}, f32[64,1024]{1,0:T(8,128)S(1)}, u32[]{:S(2)}, u32[]{:S(2)}) %collective-permute-start.22) | collective-permute-done | bytes 262176 | tf_op jit(solution)/shard_map/ppermute | solution.py:292
  61.5 14.2 %back.1 = (bf16[1024,1024]{1,0:T(8,128)(2,1)S(1)}, bf16[1024,1024]{1,0:T(8,128)(2,1)S(1)}, bf16[1024,1024]{1,0:T(8,128)(2,1)S(1)}, bf16[1024,1024]{1,0:T(8,128)(...) custom-call(s32[16]{0:T(128)S(1)} %get-tuple-element.47.offsets_ref, ...), custom_call_target="tpu_custom_call" | custom-call | tf_op jit(solution)/shard_map/back/pallas_call | solution.py:202
  75.7 11.6 %edge.1 = (bf16[1024,1024]{1,0:T(8,128)(2,1)S(1)}, bf16[1024,1024]{1,0:T(8,128)(2,1)S(1)}, f32[2,2,64,1024]{3,2,1,0:T(8,128)S(1)}, f32[2,2,64,1024]{3,2,1,0:T(8,128)S(1)}, f32[4,2,64,1024]{3,2,1,0:T(8,128)S(1)}) custom-call(s32[16]{0:T(128)S(1)} %get-tuple-element.44.offsets_ref, s32[8]{0:T(128)S(1)} %and_add_fusion.sources_ref, ...), custom_call_target="tpu_custom_call" | custom-call | tf_op jit(solution)/shard_map/edge/pallas_call | solution.py:222
  87.3 15.1 %first.1 = (bf16[1024,1024]{1,0:T(8,128)(2,1)S(1)}, bf16[1024,1024]{1,0:T(8,128)(2,1)S(1)}, f32[256,256]{1,0:T(8,128)S(1)}) custom-call(f32[1024,1024]{1,0:T(8,128)S(1)} %bitcast.71, bf16[1024,1024]{1,0:T(8,128)(2,1)S(1)} %get-tuple-element.58.right_high_ref, bf16[1024,1024]{1,0:T(8,128)(2,1)S(1)} %get-tuple-element.59.right_low_ref, ...), custom_call_target="tpu_custom_call" | custom-call | tf_op jit(solution)/shard_map/first/pallas_call | solution.py:242
  102.4 1.9 collective-permute-start.30
  104.3 1.5 collective-permute-start.28
  105.9 2.2 collective-permute-done.30
  108.1 2.2 collective-permute-done.28
  110.4 3.2 %collective-permute-start.31 = (f32[16,256]{1,0:T(8,128)S(1)}, f32[16,256]{1,0:T(8,128)S(1)}, u32[]{:S(2)}, u32[]{:S(2)}) collective-permute-start(f32[16,256]{1,0:T(8,128)S(1)} %get-tuple-element.106), channel_id=1, source_target_pairs={{0,16},{8,24},{16,32},{24,40},{32,48},{40,56},{48,0},{56,8},{64,80... | collective-permute-start | bytes 49160 | tf_op jit(solution)/shard_map/ppermute | solution.py:292
  113.6 1.7 collective-permute-done.33
  115.3 3.5 %collective-permute-done.32 = f32[16,256]{1,0:T(8,128)S(1)} collective-permute-done((f32[16,256]{1,0:T(8,128)S(1)}, f32[16,256]{1,0:T(8,128)S(1)}, u32[]{:S(2)}, u32[]{:S(2)}) %collective-permute-start.32) | collective-permute-done | bytes 16416 | tf_op jit(solution)/shard_map/ppermute | solution.py:292
  118.8 1.1 collective-permute-start.34
  120.0 2.7 %collective-permute-done.34 = f32[16,256]{1,0:T(8,128)S(1)} collective-permute-done((f32[16,256]{1,0:T(8,128)S(1)}, f32[16,256]{1,0:T(8,128)S(1)}, u32[]{:S(2)}, u32[]{:S(2)}) %collective-permute-start.34) | collective-permute-done | bytes 16416 | tf_op jit(solution)/shard_map/ppermute | solution.py:296
  123.2 1.5 collective-permute-start.35
  124.7 3.3 %collective-permute-start.36 = (f32[16,256]{1,0:T(8,128)S(1)}, f32[16,256]{1,0:T(8,128)S(1)}, u32[]{:S(2)}, u32[]{:S(2)}) collective-permute-start(f32[16,256]{1,0:T(8,128)S(1)} %add.197), channel_id=1, source_target_pairs={{0,2},{1,3},{2,0},{3,1},{4,6},{5,7},{6,4},{7,5},{8,10},{9,11},{10,... | collective-permute-start | bytes 49160 | tf_op jit(solution)/shard_map/ppermute | solution.py:296
  128.0 1.9 collective-permute-done.36
  129.9 1.7 collective-permute-start.38
  131.6 10.8 %right.1 = (f32[512,1024]{1,0:T(8,128)S(1)}, f32[512,1024]{1,0:T(8,128)}) custom-call(s32[16]{0:T(128)S(1)} %get-tuple-element.79.places_ref, bf16[1024,1024]{1,0:T(8,128)(2,1)S(1)} %get-tuple-element.51.refs_8_.back_high_ref, bf16[1024,1024]{1,0:T(8,128)(2,1)S(1)} %get-tuple-element.52.refs_9_.back_low_ref, f32[1024,1024]{1,0:T(8,128)S(1)} %bitcast.72), custom_call_target="tpu_custom_call" | custom-call | tf_op jit(solution)/shard_map/right/pallas_call | solution.py:272
  142.4 1.5 collective-permute-start.24
  144.5 10.6 %left.1 = (f32[2,2,64,1024]{3,2,1,0:T(8,128)}, f32[2,2,64,1024]{3,2,1,0:T(8,128)}, f32[4,2,64,1024]{3,2,1,0:T(8,128)S(1)}) custom-call(s32[8]{0:T(128)S(1)} %and_add_fusion.sources_ref, bf16[1024,1024]{1,0:T(8,128)(2,1)S(1)} %get-tuple-element.72.second_high_ref, bf16[1024,1024]{1,0:T(8,128)(2,1)S(1)} %get-tuple-element.73.second_low_ref, ...), custom_call_target="tpu_custom_call" | custom-call | tf_op jit(solution)/shard_map/left/pallas_call | solution.py:255
  155.1 1.9 collective-permute-start.44
  157.0 1.5 collective-permute-start.40
  158.4 4.0 %collective-permute-done.40 = f32[32,256]{1,0:T(8,128)S(1)} collective-permute-done((f32[32,256]{1,0:T(8,128)S(1)}, f32[32,256]{1,0:T(8,128)S(1)}, u32[]{:S(2)}, u32[]{:S(2)}) %collective-permute-start.40) | collective-permute-done | bytes 32800 | tf_op jit(solution)/shard_map/ppermute | solution.py:292
  162.4 3.2 %collective-permute-start.41 = (f32[32,256]{1,0:T(8,128)S(1)}, f32[32,256]{1,0:T(8,128)S(1)}, u32[]{:S(2)}, u32[]{:S(2)}) collective-permute-start(f32[32,256]{1,0:T(8,128)S(1)} %get-tuple-element.91), channel_id=1, source_target_pairs={{0,16},{8,24},{16,32},{24,40},{32,48},{40,56},{48,0},{56,8},{64,80... | collective-permute-start | bytes 98312 | tf_op jit(solution)/shard_map/ppermute | solution.py:292
  165.6 1.6 collective-permute-done.41
  168.4 1.9 collective-permute-done.23
  170.3 1.1 fusion.11
  171.4 1.2 collective-permute-start.26
  172.7 2.0 select_n.24
  174.7 3.7 %copy.29 = f32[16,16,16,16]{3,2,1,0:T(8,128)} copy(f32[16,16,16,16]{0,3,1,2:T(8,128)} %bitcast.74) | data formatting | bytes 524288
  179.2 11.8 %collective-permute-done.44 = f32[2,2,64,1024]{3,2,1,0:T(8,128)} collective-permute-done((f32[2,2,64,1024]{3,2,1,0:T(8,128)}, f32[2,2,64,1024]{3,2,1,0:T(8,128)}, u32[]{:S(2)}, u32[]{:S(2)}) %collective-permute-start.44) | collective-permute-done | bytes 1048608 | tf_op jit(solution)/shard_map/ppermute | solution.py:296
  191.0 2.6 %collective-permute-done.43 = f32[2,2,64,1024]{3,2,1,0:T(8,128)} collective-permute-done((f32[2,2,64,1024]{3,2,1,0:T(8,128)}, f32[2,2,64,1024]{3,2,1,0:T(8,128)}, u32[]{:S(2)}, u32[]{:S(2)}) %collective-permute-start.43) | collective-permute-done | bytes 1048608 | tf_op jit(solution)/shard_map/ppermute | solution.py:296
  193.6 1.7 fusion.3
  195.2 1.6 collective-permute-start.46
  196.9 7.9 %collective-permute-done.26 = f32[2,64,1024]{2,1,0:T(8,128)} collective-permute-done((f32[2,64,1024]{2,1,0:T(8,128)}, f32[2,64,1024]{2,1,0:T(8,128)}, u32[]{:S(2)}, u32[]{:S(2)}) %collective-permute-start.26) | collective-permute-done | bytes 524320 | tf_op jit(solution)/shard_map/ppermute | solution.py:296
  204.8 1.2 fusion.10
  206.0 1.1 collective-permute-start.27
  207.1 2.0 slice_add_fusion.1
  209.1 1.8 collective-permute-start.51
  210.9 1.9 collective-permute-start.49
  212.8 2.0 collective-permute-done.46
  215.9 1.8 collective-permute-start.45
  218.9 1.2 copy.28
  220.1 5.3 %collective-permute-done.51 = f32[2,64,1024]{2,1,0:T(8,128)S(1)} collective-permute-done((f32[2,64,1024]{2,1,0:T(8,128)S(1)}, f32[2,64,1024]{2,1,0:T(8,128)S(1)}, u32[]{:S(2)}, u32[]{:S(2)}) %collective-permute-start.51) | collective-permute-done | bytes 524320 | tf_op jit(solution)/shard_map/ppermute | solution.py:292
  225.5 3.8 %collective-permute-done.49 = f32[2,64,1024]{2,1,0:T(8,128)S(1)} collective-permute-done((f32[2,64,1024]{2,1,0:T(8,128)S(1)}, f32[2,64,1024]{2,1,0:T(8,128)S(1)}, u32[]{:S(2)}, u32[]{:S(2)}) %collective-permute-start.49) | collective-permute-done | bytes 524320 | tf_op jit(solution)/shard_map/ppermute | solution.py:292
  229.3 3.9 %collective-permute-done.50 = f32[2,64,1024]{2,1,0:T(8,128)S(1)} collective-permute-done((f32[2,64,1024]{2,1,0:T(8,128)S(1)}, f32[2,64,1024]{2,1,0:T(8,128)S(1)}, u32[]{:S(2)}, u32[]{:S(2)}) %collective-permute-start.50) | collective-permute-done | bytes 524320 | tf_op jit(solution)/shard_map/ppermute | solution.py:292
  233.4 2.5 %collective-permute-start.52 = (f32[64,1024]{1,0:T(8,128)S(1)}, f32[64,1024]{1,0:T(8,128)S(1)}, u32[]{:S(2)}, u32[]{:S(2)}) collective-permute-start(f32[64,1024]{1,0:T(8,128)S(1)} %slice_bitcast_fusion), channel_id=1, source_target_pairs={{0,64},{8,72},{16,80},{24,88},{32,96},{40,104},{48,112},{56,120},{... | collective-permute-start | bytes 786440 | tf_op jit(solution)/shard_map/ppermute | solution.py:292
  235.9 1.2 fusion.7
  237.1 1.2 copy.30
  238.3 4.4 %collective-permute-done.52 = f32[64,1024]{1,0:T(8,128)S(1)} collective-permute-done((f32[64,1024]{1,0:T(8,128)S(1)}, f32[64,1024]{1,0:T(8,128)S(1)}, u32[]{:S(2)}, u32[]{:S(2)}) %collective-permute-start.52) | collective-permute-done | bytes 262176 | tf_op jit(solution)/shard_map/ppermute | solution.py:292
  (122 shorter events, 13.5 us)
Async XLA Ops:
  0.6 10.5 %copy-start.8 = (s32[8]{0:T(128)S(1)}, s32[8]{0:T(128)}, u32[]{:S(2)}) copy-start(s32[8]{0:T(128)} %constant.58.clone) | copy-start | bytes 100
  0.7 10.5 %copy-start.10 = (s32[16]{0:T(128)S(1)}, s32[16]{0:T(128)}, u32[]{:S(2)}) copy-start(s32[16]{0:T(128)} %constant.55.clone) | copy-start | bytes 196
  0.7 10.5 %copy-start.11 = (s32[16]{0:T(128)S(1)}, s32[16]{0:T(128)}, u32[]{:S(2)}) copy-start(s32[16]{0:T(128)} %constant.60.clone) | copy-start | bytes 196
  0.7 10.5 %copy-start.12 = (s32[16]{0:T(128)S(1)}, s32[16]{0:T(128)}, u32[]{:S(2)}) copy-start(s32[16]{0:T(128)} %constant.59.clone) | copy-start | bytes 196
  0.7 10.5 %copy-start.13 = (s32[16]{0:T(128)S(1)}, s32[16]{0:T(128)}, u32[]{:S(2)}) copy-start(s32[16]{0:T(128)} %constant.54.clone) | copy-start | bytes 196
  0.7 10.5 %copy-start.14 = (s32[16]{0:T(128)S(1)}, s32[16]{0:T(128)}, u32[]{:S(2)}) copy-start(s32[16]{0:T(128)} %constant.62) | copy-start | bytes 196
  2.8 10.6 %collective-permute-start = (f32[64,1024]{1,0:T(8,128)S(1)}, f32[64,1024]{1,0:T(8,128)S(1)}, u32[]{:S(2)}, u32[]{:S(2)}) collective-permute-start(f32[64,1024]{1,0:T(8,128)S(1)} %reshape.86.refs_0_), channel_id=1, source_target_pairs={{0,64},{8,72},{16,80},{24,88},{32,96},{40,104},{48,112},{56,120},{... | collective-permute-start | bytes 786440 | tf_op jit(solution)/shard_map/ppermute | solution.py:292
  6.8 14.9 %collective-permute-start.9 = (f32[64,1024]{1,0:T(8,128)S(1)}, f32[64,1024]{1,0:T(8,128)S(1)}, u32[]{:S(2)}, u32[]{:S(2)}) collective-permute-start(f32[64,1024]{1,0:T(8,128)S(1)} %reshape.86.refs_0_), channel_id=1, source_target_pairs={{0,16},{8,24},{16,32},{24,40},{32,48},{40,56},{48,0},{56,8},{64,80... | collective-permute-start | bytes 786440 | tf_op jit(solution)/shard_map/ppermute | solution.py:292
  7.0 14.7 %collective-permute-start.10 = (f32[64,1024]{1,0:T(8,128)S(1)}, f32[64,1024]{1,0:T(8,128)S(1)}, u32[]{:S(2)}, u32[]{:S(2)}) collective-permute-start(f32[64,1024]{1,0:T(8,128)S(1)} %reshape.86.refs_0_), channel_id=1, source_target_pairs={{0,48},{8,56},{16,0},{24,8},{32,16},{40,24},{48,32},{56,40},{64,11... | collective-permute-start | bytes 786440 | tf_op jit(solution)/shard_map/ppermute | solution.py:292
  8.8 15.0 %collective-permute-start.11 = (f32[64,1024]{1,0:T(8,128)S(1)}, f32[64,1024]{1,0:T(8,128)S(1)}, u32[]{:S(2)}, u32[]{:S(2)}) collective-permute-start(f32[64,1024]{1,0:T(8,128)S(1)} %reshape.86.refs_0_), channel_id=1, source_target_pairs={{0,32},{8,40},{16,48},{24,56},{32,0},{40,8},{48,16},{56,24},{64,96... | collective-permute-start | bytes 786440 | tf_op jit(solution)/shard_map/ppermute | solution.py:292
  11.0 8.5 %collective-permute-start.1 = (f32[64,1024]{1,0:T(8,128)S(1)}, f32[64,1024]{1,0:T(8,128)S(1)}, u32[]{:S(2)}, u32[]{:S(2)}) collective-permute-start(f32[64,1024]{1,0:T(8,128)S(1)} %reshape.88), channel_id=1, source_target_pairs={{0,64},{8,72},{16,80},{24,88},{32,96},{40,104},{48,112},{56,120},{... | collective-permute-start | bytes 786440 | tf_op jit(solution)/shard_map/ppermute | solution.py:292
  13.4 16.1 %collective-permute-start.15 = (f32[64,1024]{1,0:T(8,128)S(1)}, f32[64,1024]{1,0:T(8,128)S(1)}, u32[]{:S(2)}, u32[]{:S(2)}) collective-permute-start(f32[64,1024]{1,0:T(8,128)S(1)} %reshape.86.refs_0_), channel_id=1, source_target_pairs={{0,8},{8,0},{16,24},{24,16},{32,40},{40,32},{48,56},{56,48},{64,72... | collective-permute-start | bytes 786440 | tf_op jit(solution)/shard_map/ppermute | solution.py:292
  19.5 11.7 %collective-permute-start.12 = (f32[64,1024]{1,0:T(8,128)S(1)}, f32[64,1024]{1,0:T(8,128)S(1)}, u32[]{:S(2)}, u32[]{:S(2)}) collective-permute-start(f32[64,1024]{1,0:T(8,128)S(1)} %collective-permute-done.refs_4_), channel_id=1, source_target_pairs={{0,16},{8,24},{16,32},{24,40},{32,48},{40,56},{48,0},{56,8},{64,80... | collective-permute-start | bytes 786440 | tf_op jit(solution)/shard_map/ppermute | solution.py:292
  21.7 13.1 %collective-permute-start.13 = (f32[64,1024]{1,0:T(8,128)S(1)}, f32[64,1024]{1,0:T(8,128)S(1)}, u32[]{:S(2)}, u32[]{:S(2)}) collective-permute-start(f32[64,1024]{1,0:T(8,128)S(1)} %collective-permute-done.refs_4_), channel_id=1, source_target_pairs={{0,48},{8,56},{16,0},{24,8},{32,16},{40,24},{48,32},{56,40},{64,11... | collective-permute-start | bytes 786440 | tf_op jit(solution)/shard_map/ppermute | solution.py:292
  21.7 13.1 %collective-permute-start.14 = (f32[64,1024]{1,0:T(8,128)S(1)}, f32[64,1024]{1,0:T(8,128)S(1)}, u32[]{:S(2)}, u32[]{:S(2)}) collective-permute-start(f32[64,1024]{1,0:T(8,128)S(1)} %collective-permute-done.refs_4_), channel_id=1, source_target_pairs={{0,32},{8,40},{16,48},{24,56},{32,0},{40,8},{48,16},{56,24},{64,96... | collective-permute-start | bytes 786440 | tf_op jit(solution)/shard_map/ppermute | solution.py:292
  23.8 12.5 %collective-permute-start.16 = (f32[64,1024]{1,0:T(8,128)S(1)}, f32[64,1024]{1,0:T(8,128)S(1)}, u32[]{:S(2)}, u32[]{:S(2)}) collective-permute-start(f32[64,1024]{1,0:T(8,128)S(1)} %collective-permute-done.9.refs_1_), channel_id=1, source_target_pairs={{0,8},{8,0},{16,24},{24,16},{32,40},{40,32},{48,56},{56,48},{64,72... | collective-permute-start | bytes 786440 | tf_op jit(solution)/shard_map/ppermute | solution.py:292
  29.5 6.8 %collective-permute-start.17 = (f32[64,1024]{1,0:T(8,128)S(1)}, f32[64,1024]{1,0:T(8,128)S(1)}, u32[]{:S(2)}, u32[]{:S(2)}) collective-permute-start(f32[64,1024]{1,0:T(8,128)S(1)} %collective-permute-done.10.refs_2_), channel_id=1, source_target_pairs={{0,8},{8,0},{16,24},{24,16},{32,40},{40,32},{48,56},{56,48},{64,72... | collective-permute-start | bytes 786440 | tf_op jit(solution)/shard_map/ppermute | solution.py:292
  31.2 14.8 %collective-permute-start.2 = (f32[128,1024]{1,0:T(8,128)S(1)}, f32[128,1024]{1,0:T(8,128)S(1)}, u32[]{:S(2)}, u32[]{:S(2)}) collective-permute-start(f32[128,1024]{1,0:T(8,128)S(1)} %constant_dynamic-update-slice_fusion.refs_0_), channel_id=1, source_target_pairs={{0,16},{8,24},{16,32},{24,40},{32,48},{40,56},{48,0},{56,8},{64,80... | collective-permute-start | bytes 1572872 | tf_op jit(solution)/shard_map/ppermute | solution.py:292
  34.8 22.9 %collective-permute-start.3 = (f32[128,1024]{1,0:T(8,128)S(1)}, f32[128,1024]{1,0:T(8,128)S(1)}, u32[]{:S(2)}, u32[]{:S(2)}) collective-permute-start(f32[128,1024]{1,0:T(8,128)S(1)} %constant_dynamic-update-slice_fusion.refs_0_), channel_id=1, source_target_pairs={{0,48},{8,56},{16,0},{24,8},{32,16},{40,24},{48,32},{56,40},{64,11... | collective-permute-start | bytes 1572872 | tf_op jit(solution)/shard_map/ppermute | solution.py:292
  34.8 22.9 %collective-permute-start.4 = (f32[128,1024]{1,0:T(8,128)S(1)}, f32[128,1024]{1,0:T(8,128)S(1)}, u32[]{:S(2)}, u32[]{:S(2)}) collective-permute-start(f32[128,1024]{1,0:T(8,128)S(1)} %constant_dynamic-update-slice_fusion.refs_0_), channel_id=1, source_target_pairs={{0,32},{8,40},{16,48},{24,56},{32,0},{40,8},{48,16},{56,24},{64,96... | collective-permute-start | bytes 1572872 | tf_op jit(solution)/shard_map/ppermute | solution.py:292
  36.3 1.5 collective-permute-start.18
  36.3 1.9 collective-permute-start.19
  37.8 20.4 %collective-permute-start.20 = (f32[64,1024]{1,0:T(8,128)S(1)}, f32[64,1024]{1,0:T(8,128)S(1)}, u32[]{:S(2)}, u32[]{:S(2)}) collective-permute-start(f32[64,1024]{1,0:T(8,128)S(1)} %collective-permute-done.12.refs_5_), channel_id=1, source_target_pairs={{0,8},{8,0},{16,24},{24,16},{32,40},{40,32},{48,56},{56,48},{64,72... | collective-permute-start | bytes 786440 | tf_op jit(solution)/shard_map/ppermute | solution.py:292
  38.2 20.1 %collective-permute-start.21 = (f32[64,1024]{1,0:T(8,128)S(1)}, f32[64,1024]{1,0:T(8,128)S(1)}, u32[]{:S(2)}, u32[]{:S(2)}) collective-permute-start(f32[64,1024]{1,0:T(8,128)S(1)} %collective-permute-done.13.refs_6_), channel_id=1, source_target_pairs={{0,8},{8,0},{16,24},{24,16},{32,40},{40,32},{48,56},{56,48},{64,72... | collective-permute-start | bytes 786440 | tf_op jit(solution)/shard_map/ppermute | solution.py:292
  46.0 29.7 %collective-permute-start.5 = (f32[128,1024]{1,0:T(8,128)S(1)}, f32[128,1024]{1,0:T(8,128)S(1)}, u32[]{:S(2)}, u32[]{:S(2)}) collective-permute-start(f32[128,1024]{1,0:T(8,128)S(1)} %constant_dynamic-update-slice_fusion.refs_0_), channel_id=1, source_target_pairs={{0,8},{8,0},{16,24},{24,16},{32,40},{40,32},{48,56},{56,48},{64,72... | collective-permute-start | bytes 1572872 | tf_op jit(solution)/shard_map/ppermute | solution.py:292
  57.7 18.0 %collective-permute-start.6 = (f32[128,1024]{1,0:T(8,128)S(1)}, f32[128,1024]{1,0:T(8,128)S(1)}, u32[]{:S(2)}, u32[]{:S(2)}) collective-permute-start(f32[128,1024]{1,0:T(8,128)S(1)} %collective-permute-done.2.refs_1_), channel_id=1, source_target_pairs={{0,8},{8,0},{16,24},{24,16},{32,40},{40,32},{48,56},{56,48},{64,72... | collective-permute-start | bytes 1572872 | tf_op jit(solution)/shard_map/ppermute | solution.py:292
  57.7 18.0 %collective-permute-start.7 = (f32[128,1024]{1,0:T(8,128)S(1)}, f32[128,1024]{1,0:T(8,128)S(1)}, u32[]{:S(2)}, u32[]{:S(2)}) collective-permute-start(f32[128,1024]{1,0:T(8,128)S(1)} %collective-permute-done.3.refs_2_), channel_id=1, source_target_pairs={{0,8},{8,0},{16,24},{24,16},{32,40},{40,32},{48,56},{56,48},{64,72... | collective-permute-start | bytes 1572872 | tf_op jit(solution)/shard_map/ppermute | solution.py:292
  58.2 17.5 %collective-permute-start.8 = (f32[128,1024]{1,0:T(8,128)S(1)}, f32[128,1024]{1,0:T(8,128)S(1)}, u32[]{:S(2)}, u32[]{:S(2)}) collective-permute-start(f32[128,1024]{1,0:T(8,128)S(1)} %collective-permute-done.4.refs_3_), channel_id=1, source_target_pairs={{0,8},{8,0},{16,24},{24,16},{32,40},{40,32},{48,56},{56,48},{64,72... | collective-permute-start | bytes 1572872 | tf_op jit(solution)/shard_map/ppermute | solution.py:292
  58.3 3.2 %collective-permute-start.22 = (f32[64,1024]{1,0:T(8,128)S(1)}, f32[64,1024]{1,0:T(8,128)S(1)}, u32[]{:S(2)}, u32[]{:S(2)}) collective-permute-start(f32[64,1024]{1,0:T(8,128)S(1)} %collective-permute-done.14.refs_7_), channel_id=1, source_target_pairs={{0,8},{8,0},{16,24},{24,16},{32,40},{40,32},{48,56},{56,48},{64,72... | collective-permute-start | bytes 786440 | tf_op jit(solution)/shard_map/ppermute | solution.py:292
  75.7 11.6 %copy-start = (f32[64,16,1024]{2,1,0:T(8,128)S(1)}, f32[64,16,1024]{2,1,0:T(8,128)}, u32[]{:S(2)}) copy-start(f32[64,16,1024]{2,1,0:T(8,128)} %param.16) | copy-start | bytes 12582916
  87.3 83.0 %copy-start.1 = (f32[4,2,64,1024]{3,2,1,0:T(8,128)}, f32[4,2,64,1024]{3,2,1,0:T(8,128)S(1)}, u32[]{:S(2)}) copy-start(f32[4,2,64,1024]{3,2,1,0:T(8,128)S(1)} %get-tuple-element.53) | copy-start | bytes 6291460
  102.4 5.6 %collective-permute-start.30 = (f32[64,256]{1,0:T(8,128)S(1)}, f32[64,256]{1,0:T(8,128)S(1)}, u32[]{:S(2)}, u32[]{:S(2)}) collective-permute-start(f32[64,256]{1,0:T(8,128)S(1)} %bitcast.89), channel_id=1, source_target_pairs={{0,72},{8,64},{16,88},{24,80},{32,104},{40,96},{48,120},{56,112},{... | collective-permute-start | bytes 196616 | tf_op jit(solution)/shard_map/ppermute | solution.py:292
  104.3 5.9 %collective-permute-start.28 = (f32[64,256]{1,0:T(8,128)S(1)}, f32[64,256]{1,0:T(8,128)S(1)}, u32[]{:S(2)}, u32[]{:S(2)}) collective-permute-start(f32[64,256]{1,0:T(8,128)S(1)} %bitcast.88), channel_id=1, source_target_pairs={{0,64},{8,72},{16,80},{24,88},{32,96},{40,104},{48,112},{56,120},{... | collective-permute-start | bytes 196616 | tf_op jit(solution)/shard_map/ppermute | solution.py:292
  105.8 4.4 %collective-permute-start.29 = (f32[64,256]{1,0:T(8,128)S(1)}, f32[64,256]{1,0:T(8,128)S(1)}, u32[]{:S(2)}, u32[]{:S(2)}) collective-permute-start(f32[64,256]{1,0:T(8,128)S(1)} %bitcast.87), channel_id=1, source_target_pairs={{0,8},{8,0},{16,24},{24,16},{32,40},{40,32},{48,56},{56,48},{64,72... | collective-permute-start | bytes 196616 | tf_op jit(solution)/shard_map/ppermute | solution.py:292
  110.3 5.0 %collective-permute-start.33 = (f32[16,256]{1,0:T(8,128)S(1)}, f32[16,256]{1,0:T(8,128)S(1)}, u32[]{:S(2)}, u32[]{:S(2)}) collective-permute-start(f32[16,256]{1,0:T(8,128)S(1)} %get-tuple-element.105), channel_id=1, source_target_pairs={{0,48},{8,56},{16,0},{24,8},{32,16},{40,24},{48,32},{56,40},{64,11... | collective-permute-start | bytes 49160 | tf_op jit(solution)/shard_map/ppermute | solution.py:292
  110.4 4.9 %collective-permute-start.31 = (f32[16,256]{1,0:T(8,128)S(1)}, f32[16,256]{1,0:T(8,128)S(1)}, u32[]{:S(2)}, u32[]{:S(2)}) collective-permute-start(f32[16,256]{1,0:T(8,128)S(1)} %get-tuple-element.106), channel_id=1, source_target_pairs={{0,16},{8,24},{16,32},{24,40},{32,48},{40,56},{48,0},{56,8},{64,80... | collective-permute-start | bytes 49160 | tf_op jit(solution)/shard_map/ppermute | solution.py:292
  113.6 5.2 %collective-permute-start.32 = (f32[16,256]{1,0:T(8,128)S(1)}, f32[16,256]{1,0:T(8,128)S(1)}, u32[]{:S(2)}, u32[]{:S(2)}) collective-permute-start(f32[16,256]{1,0:T(8,128)S(1)} %get-tuple-element.104), channel_id=1, source_target_pairs={{0,32},{8,40},{16,48},{24,56},{32,0},{40,8},{48,16},{56,24},{64,96... | collective-permute-start | bytes 49160 | tf_op jit(solution)/shard_map/ppermute | solution.py:292
  118.8 3.8 %collective-permute-start.34 = (f32[16,256]{1,0:T(8,128)S(1)}, f32[16,256]{1,0:T(8,128)S(1)}, u32[]{:S(2)}, u32[]{:S(2)}) collective-permute-start(f32[16,256]{1,0:T(8,128)S(1)} %bitcast_add_fusion.1), channel_id=1, source_target_pairs={{0,4},{1,5},{2,6},{3,7},{4,0},{5,1},{6,2},{7,3},{8,12},{9,13},{10,... | collective-permute-start | bytes 49160 | tf_op jit(solution)/shard_map/ppermute | solution.py:296
  122.7 5.4 %collective-permute-start.37 = (f32[16,256]{1,0:T(8,128)S(1)}, f32[16,256]{1,0:T(8,128)S(1)}, u32[]{:S(2)}, u32[]{:S(2)}) collective-permute-start(f32[16,256]{1,0:T(8,128)S(1)} %add.197), channel_id=1, source_target_pairs={{0,3},{1,0},{2,1},{3,2},{4,7},{5,4},{6,5},{7,6},{8,11},{9,8},{10,9... | collective-permute-start | bytes 49160 | tf_op jit(solution)/shard_map/ppermute | solution.py:296
  123.2 4.9 %collective-permute-start.35 = (f32[16,256]{1,0:T(8,128)S(1)}, f32[16,256]{1,0:T(8,128)S(1)}, u32[]{:S(2)}, u32[]{:S(2)}) collective-permute-start(f32[16,256]{1,0:T(8,128)S(1)} %add.197), channel_id=1, source_target_pairs={{0,1},{1,2},{2,3},{3,0},{4,5},{5,6},{6,7},{7,4},{8,9},{9,10},{10,1... | collective-permute-start | bytes 49160 | tf_op jit(solution)/shard_map/ppermute | solution.py:296
  124.7 5.2 %collective-permute-start.36 = (f32[16,256]{1,0:T(8,128)S(1)}, f32[16,256]{1,0:T(8,128)S(1)}, u32[]{:S(2)}, u32[]{:S(2)}) collective-permute-start(f32[16,256]{1,0:T(8,128)S(1)} %add.197), channel_id=1, source_target_pairs={{0,2},{1,3},{2,0},{3,1},{4,6},{5,7},{6,4},{7,5},{8,10},{9,11},{10,... | collective-permute-start | bytes 49160 | tf_op jit(solution)/shard_map/ppermute | solution.py:296
  129.9 14.5 %collective-permute-start.38 = (f32[16,256]{1,0:T(8,128)S(1)}, f32[16,256]{1,0:T(8,128)S(1)}, u32[]{:S(2)}, u32[]{:S(2)}) collective-permute-start(f32[16,256]{1,0:T(8,128)S(1)} %add_add_fusion.1), channel_id=1, source_target_pairs={{0,64},{8,72},{16,80},{24,88},{32,96},{40,104},{48,112},{56,120},{... | collective-permute-start | bytes 49160 | tf_op jit(solution)/shard_map/ppermute | solution.py:292
  142.4 64.7 %collective-permute-start.48 = (f32[512,1024]{1,0:T(8,128)}, f32[512,1024]{1,0:T(8,128)}, u32[]{:S(2)}, u32[]{:S(2)}) collective-permute-start(f32[512,1024]{1,0:T(8,128)} %get-tuple-element.81), channel_id=1, source_target_pairs={{0,8},{8,0},{16,24},{24,16},{32,40},{40,32},{48,56},{56,48},{64,72... | collective-permute-start | bytes 6291464 | tf_op jit(solution)/shard_map/ppermute | solution.py:292
  142.4 26.0 %collective-permute-start.24 = (f32[2,2,64,1024]{3,2,1,0:T(8,128)S(1)}, f32[2,2,64,1024]{3,2,1,0:T(8,128)S(1)}, u32[]{:S(2)}, u32[]{:S(2)}) collective-permute-start(f32[2,2,64,1024]{3,2,1,0:T(8,128)S(1)} %get-tuple-element.55), channel_id=1, source_target_pairs={{0,1},{1,2},{2,3},{3,0},{4,5},{5,6},{6,7},{7,4},{8,9},{9,10},{10,1... | collective-permute-start | bytes 3145736 | tf_op jit(solution)/shard_map/ppermute | solution.py:296
  143.9 26.4 %collective-permute-start.23 = (f32[2,2,64,1024]{3,2,1,0:T(8,128)S(1)}, f32[2,2,64,1024]{3,2,1,0:T(8,128)S(1)}, u32[]{:S(2)}, u32[]{:S(2)}) collective-permute-start(f32[2,2,64,1024]{3,2,1,0:T(8,128)S(1)} %get-tuple-element.54), channel_id=1, source_target_pairs={{0,3},{1,0},{2,1},{3,2},{4,7},{5,4},{6,5},{7,6},{8,11},{9,8},{10,9... | collective-permute-start | bytes 3145736 | tf_op jit(solution)/shard_map/ppermute | solution.py:296
  144.4 12.6 %collective-permute-start.39 = (f32[32,256]{1,0:T(8,128)S(1)}, f32[32,256]{1,0:T(8,128)S(1)}, u32[]{:S(2)}, u32[]{:S(2)}) collective-permute-start(f32[32,256]{1,0:T(8,128)S(1)} %get-tuple-element.91), channel_id=1, source_target_pairs={{0,48},{8,56},{16,0},{24,8},{32,16},{40,24},{48,32},{56,40},{64,11... | collective-permute-start | bytes 98312 | tf_op jit(solution)/shard_map/ppermute | solution.py:292
  155.1 16.3 %copy-start.3 = (f32[4,2,64,1024]{3,2,1,0:T(8,128)}, f32[4,2,64,1024]{3,2,1,0:T(8,128)S(1)}, u32[]{:S(2)}) copy-start(f32[4,2,64,1024]{3,2,1,0:T(8,128)S(1)} %get-tuple-element.76) | copy-start | bytes 6291460
  155.1 35.9 %collective-permute-start.44 = (f32[2,2,64,1024]{3,2,1,0:T(8,128)}, f32[2,2,64,1024]{3,2,1,0:T(8,128)}, u32[]{:S(2)}, u32[]{:S(2)}) collective-permute-start(f32[2,2,64,1024]{3,2,1,0:T(8,128)} %get-tuple-element.78), channel_id=1, source_target_pairs={{0,1},{1,2},{2,3},{3,0},{4,5},{5,6},{6,7},{7,4},{8,9},{9,10},{10,1... | collective-permute-start | bytes 3145736 | tf_op jit(solution)/shard_map/ppermute | solution.py:296
  157.0 5.4 %collective-permute-start.40 = (f32[32,256]{1,0:T(8,128)S(1)}, f32[32,256]{1,0:T(8,128)S(1)}, u32[]{:S(2)}, u32[]{:S(2)}) collective-permute-start(f32[32,256]{1,0:T(8,128)S(1)} %get-tuple-element.91), channel_id=1, source_target_pairs={{0,32},{8,40},{16,48},{24,56},{32,0},{40,8},{48,16},{56,24},{64,96... | collective-permute-start | bytes 98312 | tf_op jit(solution)/shard_map/ppermute | solution.py:292
  162.4 4.8 %collective-permute-start.41 = (f32[32,256]{1,0:T(8,128)S(1)}, f32[32,256]{1,0:T(8,128)S(1)}, u32[]{:S(2)}, u32[]{:S(2)}) collective-permute-start(f32[32,256]{1,0:T(8,128)S(1)} %get-tuple-element.91), channel_id=1, source_target_pairs={{0,16},{8,24},{16,32},{24,40},{32,48},{40,56},{48,0},{56,8},{64,80... | collective-permute-start | bytes 98312 | tf_op jit(solution)/shard_map/ppermute | solution.py:292
  167.2 26.3 %collective-permute-start.43 = (f32[2,2,64,1024]{3,2,1,0:T(8,128)}, f32[2,2,64,1024]{3,2,1,0:T(8,128)}, u32[]{:S(2)}, u32[]{:S(2)}) collective-permute-start(f32[2,2,64,1024]{3,2,1,0:T(8,128)} %get-tuple-element.77), channel_id=1, source_target_pairs={{0,3},{1,0},{2,1},{3,2},{4,7},{5,4},{6,5},{7,6},{8,11},{9,8},{10,9... | collective-permute-start | bytes 3145736 | tf_op jit(solution)/shard_map/ppermute | solution.py:296
  168.4 4.3 %collective-permute-start.42 = (f32[128,256]{1,0:T(8,128)S(1)}, f32[128,256]{1,0:T(8,128)S(1)}, u32[]{:S(2)}, u32[]{:S(2)}) collective-permute-start(f32[128,256]{1,0:T(8,128)S(1)} %constant_dynamic-slice_fusion), channel_id=1, source_target_pairs={{0,8},{8,0},{16,24},{24,16},{32,40},{40,32},{48,56},{56,48},{64,72... | collective-permute-start | bytes 393224 | tf_op jit(solution)/shard_map/ppermute | solution.py:292
  171.4 33.4 %collective-permute-start.26 = (f32[2,64,1024]{2,1,0:T(8,128)}, f32[2,64,1024]{2,1,0:T(8,128)}, u32[]{:S(2)}, u32[]{:S(2)}) collective-permute-start(f32[2,64,1024]{2,1,0:T(8,128)} %get-tuple-element.99), channel_id=1, source_target_pairs={{0,3},{1,0},{2,1},{3,2},{4,7},{5,4},{6,5},{7,6},{8,11},{9,8},{10,9... | collective-permute-start | bytes 1572872 | tf_op jit(solution)/shard_map/ppermute | solution.py:296
  178.4 26.4 %copy-start.2 = (f32[4,2,64,1024]{3,2,1,0:T(8,128)S(1)}, f32[4,2,64,1024]{3,2,1,0:T(8,128)}, u32[]{:S(2)}) copy-start(f32[4,2,64,1024]{3,2,1,0:T(8,128)} %copy-done.1) | copy-start | bytes 6291460
  178.4 26.4 %copy-start.6 = (f32[2,2,64,1024]{3,2,1,0:T(8,128)S(1)}, f32[2,2,64,1024]{3,2,1,0:T(8,128)}, u32[]{:S(2)}) copy-start(f32[2,2,64,1024]{3,2,1,0:T(8,128)} %copy-done.5) | copy-start | bytes 3145732
  178.4 37.5 %collective-permute-start.25 = (f32[2,64,1024]{2,1,0:T(8,128)}, f32[2,64,1024]{2,1,0:T(8,128)S(1)}, u32[]{:S(2)}, u32[]{:S(2)}) collective-permute-start(f32[2,64,1024]{2,1,0:T(8,128)} %get-tuple-element.98), channel_id=1, source_target_pairs={{0,1},{1,2},{2,3},{3,0},{4,5},{5,6},{6,7},{7,4},{8,9},{9,10},{10,1... | collective-permute-start | bytes 1572872 | tf_op jit(solution)/shard_map/ppermute | solution.py:296
  195.2 19.5 %collective-permute-start.46 = (f32[2,64,1024]{2,1,0:T(8,128)S(1)}, f32[2,64,1024]{2,1,0:T(8,128)S(1)}, u32[]{:S(2)}, u32[]{:S(2)}) collective-permute-start(f32[2,64,1024]{2,1,0:T(8,128)S(1)} %get-tuple-element.97), channel_id=1, source_target_pairs={{0,3},{1,0},{2,1},{3,2},{4,7},{5,4},{6,5},{7,6},{8,11},{9,8},{10,9... | collective-permute-start | bytes 1572872 | tf_op jit(solution)/shard_map/ppermute | solution.py:296
  206.0 11.8 %collective-permute-start.27 = (f32[2,64,1024]{2,1,0:T(8,128)S(1)}, f32[2,64,1024]{2,1,0:T(8,128)S(1)}, u32[]{:S(2)}, u32[]{:S(2)}) collective-permute-start(f32[2,64,1024]{2,1,0:T(8,128)S(1)} %fusion.10), channel_id=1, source_target_pairs={{0,4},{1,5},{2,6},{3,7},{4,0},{5,1},{6,2},{7,3},{8,12},{9,13},{10,... | collective-permute-start | bytes 1572872 | tf_op jit(solution)/shard_map/ppermute | solution.py:296
  209.1 16.4 %collective-permute-start.51 = (f32[2,64,1024]{2,1,0:T(8,128)S(1)}, f32[2,64,1024]{2,1,0:T(8,128)S(1)}, u32[]{:S(2)}, u32[]{:S(2)}) collective-permute-start(f32[2,64,1024]{2,1,0:T(8,128)S(1)} %bitcast.82), channel_id=1, source_target_pairs={{0,32},{8,40},{16,48},{24,56},{32,0},{40,8},{48,16},{56,24},{64,96... | collective-permute-start | bytes 1572872 | tf_op jit(solution)/shard_map/ppermute | solution.py:292
  210.9 18.4 %collective-permute-start.49 = (f32[2,64,1024]{2,1,0:T(8,128)S(1)}, f32[2,64,1024]{2,1,0:T(8,128)S(1)}, u32[]{:S(2)}, u32[]{:S(2)}) collective-permute-start(f32[2,64,1024]{2,1,0:T(8,128)S(1)} %bitcast.81), channel_id=1, source_target_pairs={{0,16},{8,24},{16,32},{24,40},{32,48},{40,56},{48,0},{56,8},{64,80... | collective-permute-start | bytes 1572872 | tf_op jit(solution)/shard_map/ppermute | solution.py:292
  214.8 18.4 %collective-permute-start.50 = (f32[2,64,1024]{2,1,0:T(8,128)S(1)}, f32[2,64,1024]{2,1,0:T(8,128)S(1)}, u32[]{:S(2)}, u32[]{:S(2)}) collective-permute-start(f32[2,64,1024]{2,1,0:T(8,128)S(1)} %bitcast.80), channel_id=1, source_target_pairs={{0,48},{8,56},{16,0},{24,8},{32,16},{40,24},{48,32},{56,40},{64,11... | collective-permute-start | bytes 1572872 | tf_op jit(solution)/shard_map/ppermute | solution.py:292
  215.9 20.0 %collective-permute-start.45 = (f32[2,64,1024]{2,1,0:T(8,128)S(1)}, f32[2,64,1024]{2,1,0:T(8,128)S(1)}, u32[]{:S(2)}, u32[]{:S(2)}) collective-permute-start(f32[2,64,1024]{2,1,0:T(8,128)S(1)} %get-tuple-element.96), channel_id=1, source_target_pairs={{0,1},{1,2},{2,3},{3,0},{4,5},{5,6},{6,7},{7,4},{8,9},{9,10},{10,1... | collective-permute-start | bytes 1572872 | tf_op jit(solution)/shard_map/ppermute | solution.py:296
  217.7 18.2 %collective-permute-start.47 = (f32[2,64,1024]{2,1,0:T(8,128)S(1)}, f32[2,64,1024]{2,1,0:T(8,128)S(1)}, u32[]{:S(2)}, u32[]{:S(2)}) collective-permute-start(f32[2,64,1024]{2,1,0:T(8,128)S(1)} %fusion.2), channel_id=1, source_target_pairs={{0,4},{1,5},{2,6},{3,7},{4,0},{5,1},{6,2},{7,3},{8,12},{9,13},{10,... | collective-permute-start | bytes 1572872 | tf_op jit(solution)/shard_map/ppermute | solution.py:296
  233.4 9.4 %collective-permute-start.52 = (f32[64,1024]{1,0:T(8,128)S(1)}, f32[64,1024]{1,0:T(8,128)S(1)}, u32[]{:S(2)}, u32[]{:S(2)}) collective-permute-start(f32[64,1024]{1,0:T(8,128)S(1)} %slice_bitcast_fusion), channel_id=1, source_target_pairs={{0,64},{8,72},{16,80},{24,88},{32,96},{40,104},{48,112},{56,120},{... | collective-permute-start | bytes 786440 | tf_op jit(solution)/shard_map/ppermute | solution.py:292
  (6 other events, 52.8 us)

commit v3 on v2

--- a/solution.py
+++ b/solution.py
@@ -15,7 +15,7 @@
 PARAMS = pltpu.CompilerParams(vmem_limit_bytes=16 << 20)
 ROWS = 256
 CHUNKS = 4
-WIDTH = 512
+WIDTH = 256
 
 
 def split(value):
@@ -67,21 +67,23 @@
         for part in range(piece.shape[0] // block):
             start = pl.multiple_of(offsets_ref[count], block)
             target = whole_ref.at[pl.ds(start, block)]
-            copies.append((pltpu.make_async_copy(piece.at[pl.ds(part * block, block)], target, sems.at[count]), start))
+            copies.append(pltpu.make_async_copy(piece.at[pl.ds(part * block, block)], target, sems.at[count]))
             count += 1
-    for copy, _ in copies:
+    for copy in copies:
         copy.start()
-    for copy, start in copies:
-        copy.wait()
-
-        def some(index, carry, start=start):
-            rows = pl.ds(pl.multiple_of(start + index * 16, 16), 16)
+    for group in range(4):
+        for copy in copies[4 * group : 4 * group + 4]:
+            copy.wait()
+
+        def some(index, carry, group=group):
+            start = offsets_ref[4 * group + (index >> 2)] + (index & 3) * 16
+            rows = pl.ds(pl.multiple_of(start, 16), 16)
             high, low = split(whole_ref[rows, :])
             high_ref[rows, :] = high
             low_ref[rows, :] = low
             return carry
 
-        lax.fori_loop(0, block // 16, some, 0)
+        lax.fori_loop(0, 16, some, 0)
 
 
 def chunk_of(ref):
@@ -108,20 +110,20 @@
     return ref.at[pl.ds(pl.multiple_of(pl.program_id(1) * WIDTH, WIDTH), WIDTH)]
 
 
-def place(terms, sources_ref, staged, ahead_ref, behind_ref, kept_ref):
+def place(terms, sources_ref, staged, out_refs):
     for a in range(16):
         staged[:, a, :] = terms[16 * a : 16 * a + 16, :]
     slot = 0
-    for ref in (ahead_ref, behind_ref, kept_ref):
-        for block in range(ref.shape[0]):
-            ref[block] = staged[pl.ds(sources_ref[slot] * 2, 2)]
+    for ref in out_refs:
+        for unit in range(ref.shape[0]):
+            ref[unit] = staged[sources_ref[slot]]
             slot += 1
 
 
 def edge_kernel(pieces, offsets_ref, sources_ref, *refs):
     piece_refs = refs[:pieces]
     back_high_ref, back_low_ref = refs[pieces : pieces + 2]
-    whole_high, whole_low, ahead_ref, behind_ref, kept_ref, whole, staged, sems = refs[pieces + 2 :]
+    whole_high, whole_low, *out_refs, whole, staged, sems = refs[pieces + 2 :]
 
     @pl.when((pl.program_id(0) == 0) & (pl.program_id(1) == 0))
     def _():
@@ -129,7 +131,7 @@
 
     rows = chunk_of(back_high_ref)[...], chunk_of(back_low_ref)[...]
     terms = dot3(rows, (block_of(whole_high)[...], block_of(whole_low)[...]), NT)
-    place(terms, sources_ref, staged, ahead_ref, behind_ref, kept_ref)
+    place(terms, sources_ref, staged, out_refs)
 
 
 def first_kernel(
@@ -161,16 +163,17 @@
         site_ref[...] += site
 
 
-def left_kernel(
-    sources_ref, second_high_ref, second_low_ref, high_ref, low_ref, ahead_ref, behind_ref, kept_ref, staged
-):
+def left_kernel(sources_ref, second_high_ref, second_low_ref, high_ref, low_ref, *refs):
+    *out_refs, staged = refs
     rows = chunk_of(second_high_ref)[...], chunk_of(second_low_ref)[...]
     terms = dot3(rows, (block_of(high_ref)[...], block_of(low_ref)[...]), NT)
-    place(terms, sources_ref, staged, ahead_ref, behind_ref, kept_ref)
+    place(terms, sources_ref, staged, out_refs)
 
 
 def right_kernel(places_ref, back_high_ref, back_low_ref, edge_ref, own_ref, other_ref, turned_high, turned_low, placed):
-    @pl.when(pl.program_id(0) == 0)
+    half = pl.program_id(1)
+
+    @pl.when((pl.program_id(0) == 0) & (half == 0))
     def _():
         def turn(chunk, carry):
             rows = pl.ds(pl.multiple_of(chunk * ROWS, ROWS), ROWS)
@@ -180,12 +183,16 @@
 
         lax.fori_loop(0, CHUNKS, turn, 0)
 
-    terms = dot3((turned_high[...], turned_low[...]), split(edge_ref[...]), NN)
-    for block in range(16):
-        start = pl.multiple_of(places_ref[block], 64)
+    rows = pl.ds(pl.multiple_of(half * 512, 512), 512)
+    terms = dot3((turned_high[rows, :], turned_low[rows, :]), split(edge_ref[...]), NN)
+    for block in range(8):
+        start = pl.multiple_of(places_ref[half * 8 + block], 64)
         placed[pl.ds(start, 64), :] = terms[64 * block : 64 * block + 64, :]
-    own_ref[...] = placed[:512, :]
-    other_ref[...] = placed[512:, :]
+
+    @pl.when(half == 1)
+    def _():
+        own_ref[...] = placed[:512, :]
+        other_ref[...] = placed[512:, :]
 
 
 def resident(shape):
@@ -214,19 +221,24 @@
     )(offsets, *pieces, rows, site_matrix)
 
 
-BLOCKS = tuple(jax.ShapeDtypeStruct((count, 2, 64, 1024), F32) for count in (2, 2, 4))
-BLOCK_SPECS = [pl.BlockSpec((count, 2, 16, WIDTH), lambda i, j, *_: (0, 0, i, j)) for count in (2, 2, 4)]
+def units(*counts):
+    shapes = tuple(jax.ShapeDtypeStruct((count, 64, 1024), F32) for count in counts)
+    return shapes, [pl.BlockSpec((count, 16, WIDTH), lambda i, j, *_: (0, i, j)) for count in counts]
+
+
+EDGE_SHAPES, EDGE_SPECS = units(4, 4, 8)
+LEFT_SHAPES, LEFT_SPECS = units(2, 2, 4, 2, 2, 4)
 
 
 def edge_call(offsets, sources, pieces, back_split):
     return pl.pallas_call(
         functools.partial(edge_kernel, len(pieces)),
-        out_shape=(SQUARE, SQUARE, *BLOCKS),
+        out_shape=(SQUARE, SQUARE, *EDGE_SHAPES),
         grid_spec=pltpu.PrefetchScalarGridSpec(
             num_scalar_prefetch=2,
             grid=(CHUNKS, 1024 // WIDTH),
             in_specs=[OUTSIDE] * len(pieces) + [HELD, HELD],
-            out_specs=[HELD] * 2 + BLOCK_SPECS,
+            out_specs=[HELD] * 2 + EDGE_SPECS,
             scratch_shapes=[
                 pltpu.VMEM((1024, 1024), F32),
                 pltpu.VMEM((16, 16, WIDTH), F32),
@@ -251,30 +263,30 @@
     )(edge_rows, *right_split, site_matrix, *swapped_split)
 
 
-def left_call(sources, second_split, cotangent_split):
+def left_call(left_sources, second_split, cotangent_split):
     return pl.pallas_call(
         left_kernel,
-        out_shape=BLOCKS,
+        out_shape=LEFT_SHAPES,
         grid_spec=pltpu.PrefetchScalarGridSpec(
             num_scalar_prefetch=1,
             grid=(CHUNKS, 1024 // WIDTH),
             in_specs=[HELD] * 4,
-            out_specs=BLOCK_SPECS,
+            out_specs=LEFT_SPECS,
             scratch_shapes=[pltpu.VMEM((16, 16, WIDTH), F32)],
         ),
         compiler_params=PARAMS,
         name="left",
-    )(sources, *second_split, *cotangent_split)
+    )(left_sources, *second_split, *cotangent_split)
 
 
 def right_call(places, back_split, edge_rows):
-    column = lambda rows: pl.BlockSpec((rows, 256), lambda i, *_: (0, i))
+    column = lambda rows: pl.BlockSpec((rows, 256), lambda i, j, *_: (0, i))
     return pl.pallas_call(
         right_kernel,
         out_shape=(jax.ShapeDtypeStruct((512, 1024), F32),) * 2,
         grid_spec=pltpu.PrefetchScalarGridSpec(
             num_scalar_prefetch=1,
-            grid=(4,),
+            grid=(4, 2),
             in_specs=[HELD] * 2 + [column(1024)],
             out_specs=[column(512)] * 2,
             scratch_shapes=[pltpu.VMEM((1024, 1024), BF16)] * 2 + [pltpu.VMEM((1024, 256), F32)],
@@ -296,15 +308,18 @@
     return lax.ppermute(value, "col", [(i, ((i // 4) ^ z) * 4 + (i + x) % 4) for i in range(8)])
 
 
-def col_reduce(ahead, behind, kept):
+def ring_sum(ahead, behind, kept):
     from_behind = col_permute(ahead, 0, 1)
     from_ahead = col_permute(behind, 0, 3)
-    sums = kept[0] + from_behind[0], kept[1] + from_ahead[0]
+    sums = lax.optimization_barrier((kept[0] + from_behind[0], kept[1] + from_ahead[0]))
     far_behind = col_permute(sums[0], 0, 1)
     far_ahead = col_permute(sums[1], 0, 3)
-    other = kept[3] + from_behind[1] + far_ahead
-    same = kept[2] + from_ahead[1] + far_behind
-    return jnp.transpose(same + col_permute(other, 1, 0), (1, 0, 2))
+    return kept[2] + from_ahead[1] + far_behind, kept[3] + from_behind[1] + far_ahead
+
+
+def col_sources(col, steps, others, halves):
+    steps, others, halves = (np.array(v, np.int32) for v in (steps, others, halves))
+    return (((col >> 2) ^ others) * 4 + ((col + steps) & 3)) * 2 + halves
 
 
 def dense(value):
@@ -332,9 +347,10 @@
     cotangent_offsets = offset_of(*zip(*order))
     order = [(j, steps, c) for c in (0, 1) for steps in (0, 1, 3, 2) for j in (0, 1)]
     isometry_offsets = offset_of(*zip(*order))
-    steps = np.array([2, 1, 2, 3, 1, 3, 0, 0], np.int32)
-    others = np.array([0, 1, 1, 0, 0, 1, 0, 1], np.int32)
-    sources = ((col >> 2) ^ others) * 4 + ((col + steps) & 3)
+    order = (2, 1, 2, 3, 1, 3, 0, 0)
+    halves = (0, 1, 1, 0, 0, 1, 0, 1)
+    edge_sources = col_sources(col, np.repeat(order, 2), np.repeat(halves, 2), (0, 1) * 8)
+    left_sources = col_sources(col, order * 2, (1,) * 8 + (0,) * 8, halves * 2)
     blocks = np.array([(i % 2) * 8 + i // 2 for i in range(16)], np.int32)
     places = (((blocks & 1) ^ core) * 8 + (((blocks >> 1) - y) & 3) * 2 + ((blocks >> 3) ^ z)) * 64
     cores, sides = [core, core ^ 1], [z, z ^ 1]
@@ -345,10 +361,10 @@
     early, right_isometry = lax.optimization_barrier((early, right_isometry))
     other = row_permute(early, 1, 0, 0)
     nearest = [row_permute(early, 0, steps, 0) for steps in (1, 3, 2)]
-    values = (cotangent_offsets, isometry_offsets, sources, places)
+    values = (cotangent_offsets, isometry_offsets, edge_sources, left_sources, places)
     indices = (*cores, *sides, *ahead, first_row, at_low_z, at_low_core)
     other, values, indices = lax.optimization_barrier((other, values, indices))
-    cotangent_offsets, isometry_offsets, sources, places = values
+    cotangent_offsets, isometry_offsets, edge_sources, left_sources, places = values
     cores, sides, ahead, (first_row, at_low_z, at_low_core) = indices[:2], indices[2:4], indices[4:8], indices[8:]
     own = dense(right_isometry)
     pair = jnp.concatenate([own, row_permute(own, 1, 0, 0)], 0)
@@ -361,11 +377,15 @@
     back_split, swapped_split = rest[:2], rest[2:]
 
     pairs += [row_permute(piece, 0, 0, 1) for piece in pairs]
-    right_high, right_low, *edge_terms = edge_call(isometry_offsets, sources, pairs, back_split)
-    edge_gradient = col_reduce(*edge_terms)
+    right_high, right_low, *edge_terms = edge_call(isometry_offsets, edge_sources, pairs, back_split)
+    same, other = ring_sum(*(part.reshape(-1, 2, 64, 1024) for part in edge_terms))
+    other = col_permute(other, 1, 0)
+    edge_gradient = jnp.transpose(same + other, (1, 0, 2))
     *second_split, site_terms = first_call(edge_rows, (right_high, right_low), site_matrix, swapped_split)
-    left_terms = left_call(sources, second_split, (cotangent_high, cotangent_low))
-    left_gradient = col_reduce(*left_terms)
+    left_terms = left_call(left_sources, second_split, (cotangent_high, cotangent_low))
+    other = jnp.stack(ring_sum(*left_terms[:3]))
+    other = col_permute(other, 1, 0)
+    left_gradient = jnp.transpose(jnp.stack(ring_sum(*left_terms[3:])) + other, (1, 0, 2))
 
     right_own, right_other = right_call(places, back_split, edge_rows)
 

time: 244 us -> 277 us (1.14)
  the two profiles are of different devices: /device:TPU:26 before, /device:TPU:1 now
where the time goes in v3:
time: 277 us; the launch traced here: 276 us
  waiting for transfers between devices  105 us (38%)
  starting transfers between devices  72.7 us (26%)
  Pallas kernels  67.9 us (25%)
  local copies, waits for them, and re-layouts  19.7 us (7%)
  other arithmetic  9.64 us (3%)
    ppermute x39, waiting for transfers between devices, row_permute(): return lax.ppermute(value, 'row', pairs)  58.4 us
    ppermute x39, starting transfers between devices, row_permute(): return lax.ppermute(value, 'row', pairs)  52.2 us
    ppermute x18, waiting for transfers between devices, col_permute(): lax.ppermute(value, 'col', [(i, (i // 4 ^ z) * 4 + (i + x) % 4) for i in...  46.8 us
    ppermute x18, starting transfers between devices, col_permute(): lax.ppermute(value, 'col', [(i, (i // 4 ^ z) * 4 + (i + x) % 4) for i in...  20.5 us
    pallas_call x1, Pallas kernels, first_call(): pl.pallas_call(first_kernel, out_shape=(SQUARE, SQUARE, jax.ShapeDtypeStr...  14.9 us
    pallas_call x1, Pallas kernels, edge_call(): pl.pallas_call(functools.partial(edge_kernel, len(pieces)), out_shape=(SQ...  14.8 us
    pallas_call x1, Pallas kernels, back_call(): pl.pallas_call(functools.partial(back_kernel, len(pieces)), out_shape=(SQ...  14.3 us
    pallas_call x1, Pallas kernels, left_call(): pl.pallas_call(left_kernel, out_shape=LEFT_SHAPES, grid_spec=pltpu.Prefet...  12.3 us
  transfers between devices with their start and end apart: 57, of which 28 were waited for; matrix products, arithmetic and copies ran while one was open for 9% of the time, Pallas kernels for 14%

profile of v3, /device:TPU:1, one launch (start us, length us, event | category | flops | bytes accessed | tf_op | source)
XLA Modules:
  0.0 276.3 jit_solution(5273945418800478892)
XLA Ops:
  0.8 1.6 copy.29
  2.9 4.5 %collective-permute-start = (f32[64,1024]{1,0:T(8,128)S(1)}, f32[64,1024]{1,0:T(8,128)S(1)}, u32[]{:S(2)}, u32[]{:S(2)}) collective-permute-start(f32[64,1024]{1,0:T(8,128)S(1)} %reshape.101.refs_0_), channel_id=1, source_target_pairs={{0,64},{8,72},{16,80},{24,88},{32,96},{40,104},{48,112},{56,120},{... | collective-permute-start | bytes 786440 | tf_op jit(solution)/shard_map/ppermute | solution.py:304
  8.4 1.4 collective-permute-start.9
  9.8 1.5 collective-permute-start.10
  11.3 1.6 collective-permute-start.11
  13.3 2.1 collective-permute-start.15
  15.4 3.5 %collective-permute-done.1 = f32[64,1024]{1,0:T(8,128)S(1)} collective-permute-done((f32[64,1024]{1,0:T(8,128)S(1)}, f32[64,1024]{1,0:T(8,128)S(1)}, u32[]{:S(2)}, u32[]{:S(2)}) %collective-permute-start.1) | collective-permute-done | bytes 262176 | tf_op jit(solution)/shard_map/ppermute | solution.py:304
  19.0 1.3 collective-permute-start.12
  20.3 1.4 collective-permute-start.13
  21.7 1.6 collective-permute-start.14
  23.5 2.6 collective-permute-start.16
  26.0 3.2 %copy.31 = f32[16,16,16,16]{3,2,1,0:T(8,128)} copy(f32[16,16,16,16]{2,0,1,3:T(8,128)} %bitcast.111) | data formatting | bytes 524288 | tf_op jit(solution)/shard_map/transpose | solution.py:345
  29.2 2.4 reshape.104.refs_17_.site_matrix_ref
  31.8 1.6 collective-permute-start.2
  35.6 2.9 %collective-permute-start.18 = (f32[64,1024]{1,0:T(8,128)S(1)}, f32[64,1024]{1,0:T(8,128)S(1)}, u32[]{:S(2)}, u32[]{:S(2)}) collective-permute-start(f32[64,1024]{1,0:T(8,128)S(1)} %collective-permute-done.11.refs_3_), channel_id=1, source_target_pairs={{0,8},{8,0},{16,24},{24,16},{32,40},{40,32},{48,56},{56,48},{64,72... | collective-permute-start | bytes 786440 | tf_op jit(solution)/shard_map/ppermute | solution.py:304
  40.4 6.7 %collective-permute-done.2.refs_1_ = f32[128,1024]{1,0:T(8,128)S(1)} collective-permute-done((f32[128,1024]{1,0:T(8,128)S(1)}, f32[128,1024]{1,0:T(8,128)S(1)}, u32[]{:S(2)}, u32[]{:S(2)}) %collective-permute-start.2) | collective-permute-done | bytes 524320 | tf_op jit(solution)/shard_map/ppermute | solution.py:304
  47.0 1.3 collective-permute-start.5
  49.5 8.6 %collective-permute-done.4.refs_3_ = f32[128,1024]{1,0:T(8,128)S(1)} collective-permute-done((f32[128,1024]{1,0:T(8,128)S(1)}, f32[128,1024]{1,0:T(8,128)S(1)}, u32[]{:S(2)}, u32[]{:S(2)}) %collective-permute-start.4) | collective-permute-done | bytes 524320 | tf_op jit(solution)/shard_map/ppermute | solution.py:304
  59.6 2.1 collective-permute-done.22.refs_15_
  61.7 14.3 %back.1 = (bf16[1024,1024]{1,0:T(8,128)(2,1)S(1)}, bf16[1024,1024]{1,0:T(8,128)(2,1)S(1)}, bf16[1024,1024]{1,0:T(8,128)(2,1)S(1)}, bf16[1024,1024]{1,0:T(8,128)(...) custom-call(s32[16]{0:T(128)S(1)} %get-tuple-element.57.offsets_ref, ...), custom_call_target="tpu_custom_call" | custom-call | tf_op jit(solution)/shard_map/back/pallas_call | solution.py:209
  76.0 14.8 %edge.1 = (bf16[1024,1024]{1,0:T(8,128)(2,1)S(1)}, bf16[1024,1024]{1,0:T(8,128)(2,1)S(1)}, f32[4,64,1024]{2,1,0:T(8,128)}, f32[4,64,1024]{2,1,0:T(8,128)}, f32[8,64,1024]{2,1,0:T(8,128)S(1)}) custom-call(s32[16]{0:T(128)S(1)} %get-tuple-element.54.offsets_ref, s32[16]{0:T(128)S(1)} %get-tuple-element.55.sources_ref, ...), custom_call_target="tpu_custom_call" | custom-call | tf_op jit(solution)/shard_map/edge/pallas_call | solution.py:234
  90.8 1.3 copy-done.1
  92.1 14.9 %first.1 = (bf16[1024,1024]{1,0:T(8,128)(2,1)S(1)}, bf16[1024,1024]{1,0:T(8,128)(2,1)S(1)}, f32[256,256]{1,0:T(8,128)S(1)}) custom-call(f32[1024,1024]{1,0:T(8,128)S(1)} %bitcast.105, bf16[1024,1024]{1,0:T(8,128)(2,1)S(1)} %get-tuple-element.70.right_high_ref, bf16[1024,1024]{1,0:T(8,128)(2,1)S(1)} %get-tuple-element.71.right_low_ref, ...), custom_call_target="tpu_custom_call" | custom-call | tf_op jit(solution)/shard_map/first/pallas_call | solution.py:254
  107.0 3.3 %collective-permute-start.30 = (f32[64,256]{1,0:T(8,128)S(1)}, f32[64,256]{1,0:T(8,128)S(1)}, u32[]{:S(2)}, u32[]{:S(2)}) collective-permute-start(f32[64,256]{1,0:T(8,128)S(1)} %bitcast.123), channel_id=1, source_target_pairs={{0,72},{8,64},{16,88},{24,80},{32,104},{40,96},{48,120},{56,112},{... | collective-permute-start | bytes 196616 | tf_op jit(solution)/shard_map/ppermute | solution.py:304
  110.8 2.0 collective-permute-done.30
  112.8 2.6 collective-permute-done.28
  115.4 3.3 %collective-permute-start.33 = (f32[16,256]{1,0:T(8,128)S(1)}, f32[16,256]{1,0:T(8,128)S(1)}, u32[]{:S(2)}, u32[]{:S(2)}) collective-permute-start(f32[16,256]{1,0:T(8,128)S(1)} %get-tuple-element.131), channel_id=1, source_target_pairs={{0,48},{8,56},{16,0},{24,8},{32,16},{40,24},{48,32},{56,40},{64,11... | collective-permute-start | bytes 49160 | tf_op jit(solution)/shard_map/ppermute | solution.py:304
  118.7 1.3 collective-permute-start.32
  120.0 2.5 collective-permute-done.31
  123.6 1.9 collective-permute-done.34
  125.5 2.3 collective-permute-start.37
  127.8 1.7 collective-permute-start.36
  129.5 2.1 collective-permute-done.35
  131.9 1.7 collective-permute-start.38
  133.6 2.4 collective-permute-done.38
  136.1 2.7 collective-permute-start.39
  138.8 11.7 %right.1 = (f32[512,1024]{1,0:T(8,128)S(1)}, f32[512,1024]{1,0:T(8,128)}) custom-call(s32[16]{0:T(128)S(1)} %get-tuple-element.99.places_ref, bf16[1024,1024]{1,0:T(8,128)(2,1)S(1)} %get-tuple-element.61.refs_8_.back_high_ref, bf16[1024,1024]{1,0:T(8,128)(2,1)S(1)} %get-tuple-element.62.refs_9_.back_low_ref, f32[1024,1024]{1,0:T(8,128)S(1)} %bitcast.106), custom_call_target="tpu_custom_call" | custom-call | tf_op jit(solution)/shard_map/right/pallas_call | solution.py:284
  150.5 6.8 %collective-permute-start.52 = (f32[512,1024]{1,0:T(8,128)}, f32[512,1024]{1,0:T(8,128)}, u32[]{:S(2)}, u32[]{:S(2)}) collective-permute-start(f32[512,1024]{1,0:T(8,128)} %get-tuple-element.101), channel_id=1, source_target_pairs={{0,8},{8,0},{16,24},{24,16},{32,40},{40,32},{48,56},{56,48},{64,72... | collective-permute-start | bytes 6291464 | tf_op jit(solution)/shard_map/ppermute | solution.py:304
  157.2 12.3 %left.1 = (f32[2,64,1024]{2,1,0:T(8,128)S(1)}, f32[2,64,1024]{2,1,0:T(8,128)S(1)}, f32[4,64,1024]{2,1,0:T(8,128)S(1)}, f32[2,64,1024]{2,1,0:T(8,128)S(1)}, f32[2...) custom-call(s32[16]{0:T(128)S(1)} %get-tuple-element.84.sources_ref, ...), custom_call_target="tpu_custom_call" | custom-call | tf_op jit(solution)/shard_map/left/pallas_call | solution.py:267
  169.6 3.0 %collective-permute-start.47 = (f32[2,64,1024]{2,1,0:T(8,128)S(1)}, f32[2,64,1024]{2,1,0:T(8,128)S(1)}, u32[]{:S(2)}, u32[]{:S(2)}) collective-permute-start(f32[2,64,1024]{2,1,0:T(8,128)S(1)} %get-tuple-element.95), channel_id=1, source_target_pairs={{0,3},{1,0},{2,1},{3,2},{4,7},{5,4},{6,5},{7,6},{8,11},{9,8},{10,9... | collective-permute-start | bytes 1572872 | tf_op jit(solution)/shard_map/ppermute | solution.py:308
  172.9 4.1 %collective-permute-done.40 = f32[32,256]{1,0:T(8,128)S(1)} collective-permute-done((f32[32,256]{1,0:T(8,128)S(1)}, f32[32,256]{1,0:T(8,128)S(1)}, u32[]{:S(2)}, u32[]{:S(2)}) %collective-permute-start.40) | collective-permute-done | bytes 32800 | tf_op jit(solution)/shard_map/ppermute | solution.py:304
  177.4 1.2 collective-permute-start.42
  178.6 2.9 %collective-permute-start.43 = (f32[2,64,1024]{2,1,0:T(8,128)S(1)}, f32[2,64,1024]{2,1,0:T(8,128)S(1)}, u32[]{:S(2)}, u32[]{:S(2)}) collective-permute-start(f32[2,64,1024]{2,1,0:T(8,128)S(1)} %get-tuple-element.90), channel_id=1, source_target_pairs={{0,3},{1,0},{2,1},{3,2},{4,7},{5,4},{6,5},{7,6},{8,11},{9,8},{10,9... | collective-permute-start | bytes 1572872 | tf_op jit(solution)/shard_map/ppermute | solution.py:308
  181.5 2.4 collective-permute-done.47
  183.9 3.4 %collective-permute-start.23 = (f32[2,2,64,1024]{3,2,1,0:T(8,128)}, f32[2,2,64,1024]{3,2,1,0:T(8,128)}, u32[]{:S(2)}, u32[]{:S(2)}) collective-permute-start(f32[2,2,64,1024]{3,2,1,0:T(8,128)} %bitcast.6), channel_id=1, source_target_pairs={{0,3},{1,0},{2,1},{3,2},{4,7},{5,4},{6,5},{7,6},{8,11},{9,8},{10,9... | collective-permute-start | bytes 3145736 | tf_op jit(solution)/shard_map/ppermute | solution.py:308
  188.3 6.8 %collective-permute-done.43 = f32[2,64,1024]{2,1,0:T(8,128)S(1)} collective-permute-done((f32[2,64,1024]{2,1,0:T(8,128)S(1)}, f32[2,64,1024]{2,1,0:T(8,128)S(1)}, u32[]{:S(2)}, u32[]{:S(2)}) %collective-permute-start.43) | collective-permute-done | bytes 524320 | tf_op jit(solution)/shard_map/ppermute | solution.py:308
  195.1 3.1 %collective-permute-done.44 = f32[2,64,1024]{2,1,0:T(8,128)S(1)} collective-permute-done((f32[2,64,1024]{2,1,0:T(8,128)S(1)}, f32[2,64,1024]{2,1,0:T(8,128)S(1)}, u32[]{:S(2)}, u32[]{:S(2)}) %collective-permute-start.44) | collective-permute-done | bytes 524320 | tf_op jit(solution)/shard_map/ppermute | solution.py:308
  199.1 2.1 select_n.24
  201.1 3.7 %copy.33 = f32[16,16,16,16]{3,2,1,0:T(8,128)} copy(f32[16,16,16,16]{0,3,1,2:T(8,128)} %bitcast.108) | data formatting | bytes 524288
  206.0 20.4 %collective-permute-done.49 = f32[64,1024]{1,0:T(8,128)} collective-permute-done((f32[64,1024]{1,0:T(8,128)}, f32[64,1024]{1,0:T(8,128)}, u32[]{:S(2)}, u32[]{:S(2)}) %collective-permute-start.49) | collective-permute-done | bytes 262176 | tf_op jit(solution)/shard_map/ppermute | solution.py:308
  226.4 2.7 collective-permute-start.46
  229.1 1.4 fusion.17
  230.6 3.8 %collective-permute-done.45 = f32[64,1024]{1,0:T(8,128)S(1)} collective-permute-done((f32[64,1024]{1,0:T(8,128)S(1)}, f32[64,1024]{1,0:T(8,128)S(1)}, u32[]{:S(2)}, u32[]{:S(2)}) %collective-permute-start.45) | collective-permute-done | bytes 262176 | tf_op jit(solution)/shard_map/ppermute | solution.py:308
  235.2 1.4 fusion.2
  236.5 1.8 collective-permute-start.26
  238.3 1.9 slice_add_fusion.1
  240.6 5.2 %collective-permute-done.51 = f32[2,64,1024]{2,1,0:T(8,128)S(1)} collective-permute-done((f32[2,64,1024]{2,1,0:T(8,128)S(1)}, f32[2,64,1024]{2,1,0:T(8,128)S(1)}, u32[]{:S(2)}, u32[]{:S(2)}) %collective-permute-start.51) | collective-permute-done | bytes 524320 | tf_op jit(solution)/shard_map/ppermute | solution.py:308
  245.9 1.2 copy.34
  249.8 3.0 %collective-permute-done.55 = f32[2,64,1024]{2,1,0:T(8,128)S(1)} collective-permute-done((f32[2,64,1024]{2,1,0:T(8,128)S(1)}, f32[2,64,1024]{2,1,0:T(8,128)S(1)}, u32[]{:S(2)}, u32[]{:S(2)}) %collective-permute-start.55) | collective-permute-done | bytes 524320 | tf_op jit(solution)/shard_map/ppermute | solution.py:304
  252.8 13.7 %collective-permute-done.53 = f32[2,64,1024]{2,1,0:T(8,128)S(1)} collective-permute-done((f32[2,64,1024]{2,1,0:T(8,128)S(1)}, f32[2,64,1024]{2,1,0:T(8,128)S(1)}, u32[]{:S(2)}, u32[]{:S(2)}) %collective-permute-start.53) | collective-permute-done | bytes 524320 | tf_op jit(solution)/shard_map/ppermute | solution.py:304
  266.7 1.8 collective-permute-start.56
  268.5 1.2 fusion.7
  269.7 1.2 copy.32
  270.9 4.5 %collective-permute-done.56 = f32[64,1024]{1,0:T(8,128)S(1)} collective-permute-done((f32[64,1024]{1,0:T(8,128)S(1)}, f32[64,1024]{1,0:T(8,128)S(1)}, u32[]{:S(2)}, u32[]{:S(2)}) %collective-permute-start.56) | collective-permute-done | bytes 262176 | tf_op jit(solution)/shard_map/ppermute | solution.py:304
  (144 shorter events, 19.7 us)
Async XLA Ops:
  0.6 12.2 %copy-start.11 = (s32[16]{0:T(128)S(1)}, s32[16]{0:T(128)}, u32[]{:S(2)}) copy-start(s32[16]{0:T(128)} %constant.60.clone) | copy-start | bytes 196
  0.6 12.2 %copy-start.12 = (s32[16]{0:T(128)S(1)}, s32[16]{0:T(128)}, u32[]{:S(2)}) copy-start(s32[16]{0:T(128)} %constant.68.clone) | copy-start | bytes 196
  2.9 10.5 %collective-permute-start = (f32[64,1024]{1,0:T(8,128)S(1)}, f32[64,1024]{1,0:T(8,128)S(1)}, u32[]{:S(2)}, u32[]{:S(2)}) collective-permute-start(f32[64,1024]{1,0:T(8,128)S(1)} %reshape.101.refs_0_), channel_id=1, source_target_pairs={{0,64},{8,72},{16,80},{24,88},{32,96},{40,104},{48,112},{56,120},{... | collective-permute-start | bytes 786440 | tf_op jit(solution)/shard_map/ppermute | solution.py:304
  8.3 10.6 %collective-permute-start.1 = (f32[64,1024]{1,0:T(8,128)S(1)}, f32[64,1024]{1,0:T(8,128)S(1)}, u32[]{:S(2)}, u32[]{:S(2)}) collective-permute-start(f32[64,1024]{1,0:T(8,128)S(1)} %reshape.103), channel_id=1, source_target_pairs={{0,64},{8,72},{16,80},{24,88},{32,96},{40,104},{48,112},{56,120},{... | collective-permute-start | bytes 786440 | tf_op jit(solution)/shard_map/ppermute | solution.py:304
  8.4 11.9 %collective-permute-start.9 = (f32[64,1024]{1,0:T(8,128)S(1)}, f32[64,1024]{1,0:T(8,128)S(1)}, u32[]{:S(2)}, u32[]{:S(2)}) collective-permute-start(f32[64,1024]{1,0:T(8,128)S(1)} %reshape.101.refs_0_), channel_id=1, source_target_pairs={{0,16},{8,24},{16,32},{24,40},{32,48},{40,56},{48,0},{56,8},{64,80... | collective-permute-start | bytes 786440 | tf_op jit(solution)/shard_map/ppermute | solution.py:304
  9.8 11.9 %collective-permute-start.10 = (f32[64,1024]{1,0:T(8,128)S(1)}, f32[64,1024]{1,0:T(8,128)S(1)}, u32[]{:S(2)}, u32[]{:S(2)}) collective-permute-start(f32[64,1024]{1,0:T(8,128)S(1)} %reshape.101.refs_0_), channel_id=1, source_target_pairs={{0,48},{8,56},{16,0},{24,8},{32,16},{40,24},{48,32},{56,40},{64,11... | collective-permute-start | bytes 786440 | tf_op jit(solution)/shard_map/ppermute | solution.py:304
  11.3 12.2 %collective-permute-start.11 = (f32[64,1024]{1,0:T(8,128)S(1)}, f32[64,1024]{1,0:T(8,128)S(1)}, u32[]{:S(2)}, u32[]{:S(2)}) collective-permute-start(f32[64,1024]{1,0:T(8,128)S(1)} %reshape.101.refs_0_), channel_id=1, source_target_pairs={{0,32},{8,40},{16,48},{24,56},{32,0},{40,8},{48,16},{56,24},{64,96... | collective-permute-start | bytes 786440 | tf_op jit(solution)/shard_map/ppermute | solution.py:304
  13.3 18.3 %collective-permute-start.15 = (f32[64,1024]{1,0:T(8,128)S(1)}, f32[64,1024]{1,0:T(8,128)S(1)}, u32[]{:S(2)}, u32[]{:S(2)}) collective-permute-start(f32[64,1024]{1,0:T(8,128)S(1)} %reshape.101.refs_0_), channel_id=1, source_target_pairs={{0,8},{8,0},{16,24},{24,16},{32,40},{40,32},{48,56},{56,48},{64,72... | collective-permute-start | bytes 786440 | tf_op jit(solution)/shard_map/ppermute | solution.py:304
  19.0 12.8 %collective-permute-start.12 = (f32[64,1024]{1,0:T(8,128)S(1)}, f32[64,1024]{1,0:T(8,128)S(1)}, u32[]{:S(2)}, u32[]{:S(2)}) collective-permute-start(f32[64,1024]{1,0:T(8,128)S(1)} %collective-permute-done.refs_4_), channel_id=1, source_target_pairs={{0,16},{8,24},{16,32},{24,40},{32,48},{40,56},{48,0},{56,8},{64,80... | collective-permute-start | bytes 786440 | tf_op jit(solution)/shard_map/ppermute | solution.py:304
  20.3 13.1 %collective-permute-start.13 = (f32[64,1024]{1,0:T(8,128)S(1)}, f32[64,1024]{1,0:T(8,128)S(1)}, u32[]{:S(2)}, u32[]{:S(2)}) collective-permute-start(f32[64,1024]{1,0:T(8,128)S(1)} %collective-permute-done.refs_4_), channel_id=1, source_target_pairs={{0,48},{8,56},{16,0},{24,8},{32,16},{40,24},{48,32},{56,40},{64,11... | collective-permute-start | bytes 786440 | tf_op jit(solution)/shard_map/ppermute | solution.py:304
  21.7 13.4 %collective-permute-start.14 = (f32[64,1024]{1,0:T(8,128)S(1)}, f32[64,1024]{1,0:T(8,128)S(1)}, u32[]{:S(2)}, u32[]{:S(2)}) collective-permute-start(f32[64,1024]{1,0:T(8,128)S(1)} %collective-permute-done.refs_4_), channel_id=1, source_target_pairs={{0,32},{8,40},{16,48},{24,56},{32,0},{40,8},{48,16},{56,24},{64,96... | collective-permute-start | bytes 786440 | tf_op jit(solution)/shard_map/ppermute | solution.py:304
  23.5 12.1 %collective-permute-start.16 = (f32[64,1024]{1,0:T(8,128)S(1)}, f32[64,1024]{1,0:T(8,128)S(1)}, u32[]{:S(2)}, u32[]{:S(2)}) collective-permute-start(f32[64,1024]{1,0:T(8,128)S(1)} %collective-permute-done.9.refs_1_), channel_id=1, source_target_pairs={{0,8},{8,0},{16,24},{24,16},{32,40},{40,32},{48,56},{56,48},{64,72... | collective-permute-start | bytes 786440 | tf_op jit(solution)/shard_map/ppermute | solution.py:304
  31.7 6.8 %collective-permute-start.17 = (f32[64,1024]{1,0:T(8,128)S(1)}, f32[64,1024]{1,0:T(8,128)S(1)}, u32[]{:S(2)}, u32[]{:S(2)}) collective-permute-start(f32[64,1024]{1,0:T(8,128)S(1)} %collective-permute-done.10.refs_2_), channel_id=1, source_target_pairs={{0,8},{8,0},{16,24},{24,16},{32,40},{40,32},{48,56},{56,48},{64,72... | collective-permute-start | bytes 786440 | tf_op jit(solution)/shard_map/ppermute | solution.py:304
  31.8 15.2 %collective-permute-start.2 = (f32[128,1024]{1,0:T(8,128)S(1)}, f32[128,1024]{1,0:T(8,128)S(1)}, u32[]{:S(2)}, u32[]{:S(2)}) collective-permute-start(f32[128,1024]{1,0:T(8,128)S(1)} %constant_dynamic-update-slice_fusion.refs_0_), channel_id=1, source_target_pairs={{0,16},{8,24},{16,32},{24,40},{32,48},{40,56},{48,0},{56,8},{64,80... | collective-permute-start | bytes 1572872 | tf_op jit(solution)/shard_map/ppermute | solution.py:304
  33.4 14.9 %collective-permute-start.3 = (f32[128,1024]{1,0:T(8,128)S(1)}, f32[128,1024]{1,0:T(8,128)S(1)}, u32[]{:S(2)}, u32[]{:S(2)}) collective-permute-start(f32[128,1024]{1,0:T(8,128)S(1)} %constant_dynamic-update-slice_fusion.refs_0_), channel_id=1, source_target_pairs={{0,48},{8,56},{16,0},{24,8},{32,16},{40,24},{48,32},{56,40},{64,11... | collective-permute-start | bytes 1572872 | tf_op jit(solution)/shard_map/ppermute | solution.py:304
  35.1 23.0 %collective-permute-start.4 = (f32[128,1024]{1,0:T(8,128)S(1)}, f32[128,1024]{1,0:T(8,128)S(1)}, u32[]{:S(2)}, u32[]{:S(2)}) collective-permute-start(f32[128,1024]{1,0:T(8,128)S(1)} %constant_dynamic-update-slice_fusion.refs_0_), channel_id=1, source_target_pairs={{0,32},{8,40},{16,48},{24,56},{32,0},{40,8},{48,16},{56,24},{64,96... | collective-permute-start | bytes 1572872 | tf_op jit(solution)/shard_map/ppermute | solution.py:304
  35.6 4.0 %collective-permute-start.18 = (f32[64,1024]{1,0:T(8,128)S(1)}, f32[64,1024]{1,0:T(8,128)S(1)}, u32[]{:S(2)}, u32[]{:S(2)}) collective-permute-start(f32[64,1024]{1,0:T(8,128)S(1)} %collective-permute-done.11.refs_3_), channel_id=1, source_target_pairs={{0,8},{8,0},{16,24},{24,16},{32,40},{40,32},{48,56},{56,48},{64,72... | collective-permute-start | bytes 786440 | tf_op jit(solution)/shard_map/ppermute | solution.py:304
  38.5 1.5 collective-permute-start.19
  39.6 19.4 %collective-permute-start.20 = (f32[64,1024]{1,0:T(8,128)S(1)}, f32[64,1024]{1,0:T(8,128)S(1)}, u32[]{:S(2)}, u32[]{:S(2)}) collective-permute-start(f32[64,1024]{1,0:T(8,128)S(1)} %collective-permute-done.12.refs_5_), channel_id=1, source_target_pairs={{0,8},{8,0},{16,24},{24,16},{32,40},{40,32},{48,56},{56,48},{64,72... | collective-permute-start | bytes 786440 | tf_op jit(solution)/shard_map/ppermute | solution.py:304
  40.0 19.1 %collective-permute-start.21 = (f32[64,1024]{1,0:T(8,128)S(1)}, f32[64,1024]{1,0:T(8,128)S(1)}, u32[]{:S(2)}, u32[]{:S(2)}) collective-permute-start(f32[64,1024]{1,0:T(8,128)S(1)} %collective-permute-done.13.refs_6_), channel_id=1, source_target_pairs={{0,8},{8,0},{16,24},{24,16},{32,40},{40,32},{48,56},{56,48},{64,72... | collective-permute-start | bytes 786440 | tf_op jit(solution)/shard_map/ppermute | solution.py:304
  47.0 29.0 %collective-permute-start.5 = (f32[128,1024]{1,0:T(8,128)S(1)}, f32[128,1024]{1,0:T(8,128)S(1)}, u32[]{:S(2)}, u32[]{:S(2)}) collective-permute-start(f32[128,1024]{1,0:T(8,128)S(1)} %constant_dynamic-update-slice_fusion.refs_0_), channel_id=1, source_target_pairs={{0,8},{8,0},{16,24},{24,16},{32,40},{40,32},{48,56},{56,48},{64,72... | collective-permute-start | bytes 1572872 | tf_op jit(solution)/shard_map/ppermute | solution.py:304
  48.3 27.7 %collective-permute-start.6 = (f32[128,1024]{1,0:T(8,128)S(1)}, f32[128,1024]{1,0:T(8,128)S(1)}, u32[]{:S(2)}, u32[]{:S(2)}) collective-permute-start(f32[128,1024]{1,0:T(8,128)S(1)} %collective-permute-done.2.refs_1_), channel_id=1, source_target_pairs={{0,8},{8,0},{16,24},{24,16},{32,40},{40,32},{48,56},{56,48},{64,72... | collective-permute-start | bytes 1572872 | tf_op jit(solution)/shard_map/ppermute | solution.py:304
  58.1 17.9 %collective-permute-start.7 = (f32[128,1024]{1,0:T(8,128)S(1)}, f32[128,1024]{1,0:T(8,128)S(1)}, u32[]{:S(2)}, u32[]{:S(2)}) collective-permute-start(f32[128,1024]{1,0:T(8,128)S(1)} %collective-permute-done.3.refs_2_), channel_id=1, source_target_pairs={{0,8},{8,0},{16,24},{24,16},{32,40},{40,32},{48,56},{56,48},{64,72... | collective-permute-start | bytes 1572872 | tf_op jit(solution)/shard_map/ppermute | solution.py:304
  59.1 17.0 %collective-permute-start.8 = (f32[128,1024]{1,0:T(8,128)S(1)}, f32[128,1024]{1,0:T(8,128)S(1)}, u32[]{:S(2)}, u32[]{:S(2)}) collective-permute-start(f32[128,1024]{1,0:T(8,128)S(1)} %collective-permute-done.4.refs_3_), channel_id=1, source_target_pairs={{0,8},{8,0},{16,24},{24,16},{32,40},{40,32},{48,56},{56,48},{64,72... | collective-permute-start | bytes 1572872 | tf_op jit(solution)/shard_map/ppermute | solution.py:304
  59.1 2.6 collective-permute-start.22
  76.0 16.1 %copy-start = (f32[64,16,1024]{2,1,0:T(8,128)S(1)}, f32[64,16,1024]{2,1,0:T(8,128)}, u32[]{:S(2)}) copy-start(f32[64,16,1024]{2,1,0:T(8,128)} %param.20) | copy-start | bytes 12582916
  107.0 5.7 %collective-permute-start.30 = (f32[64,256]{1,0:T(8,128)S(1)}, f32[64,256]{1,0:T(8,128)S(1)}, u32[]{:S(2)}, u32[]{:S(2)}) collective-permute-start(f32[64,256]{1,0:T(8,128)S(1)} %bitcast.123), channel_id=1, source_target_pairs={{0,72},{8,64},{16,88},{24,80},{32,104},{40,96},{48,120},{56,112},{... | collective-permute-start | bytes 196616 | tf_op jit(solution)/shard_map/ppermute | solution.py:304
  110.3 5.1 %collective-permute-start.28 = (f32[64,256]{1,0:T(8,128)S(1)}, f32[64,256]{1,0:T(8,128)S(1)}, u32[]{:S(2)}, u32[]{:S(2)}) collective-permute-start(f32[64,256]{1,0:T(8,128)S(1)} %bitcast.122), channel_id=1, source_target_pairs={{0,64},{8,72},{16,80},{24,88},{32,96},{40,104},{48,112},{56,120},{... | collective-permute-start | bytes 196616 | tf_op jit(solution)/shard_map/ppermute | solution.py:304
  110.4 5.0 %collective-permute-start.29 = (f32[64,256]{1,0:T(8,128)S(1)}, f32[64,256]{1,0:T(8,128)S(1)}, u32[]{:S(2)}, u32[]{:S(2)}) collective-permute-start(f32[64,256]{1,0:T(8,128)S(1)} %bitcast.121), channel_id=1, source_target_pairs={{0,8},{8,0},{16,24},{24,16},{32,40},{40,32},{48,56},{56,48},{64,72... | collective-permute-start | bytes 196616 | tf_op jit(solution)/shard_map/ppermute | solution.py:304
  115.4 4.6 %collective-permute-start.33 = (f32[16,256]{1,0:T(8,128)S(1)}, f32[16,256]{1,0:T(8,128)S(1)}, u32[]{:S(2)}, u32[]{:S(2)}) collective-permute-start(f32[16,256]{1,0:T(8,128)S(1)} %get-tuple-element.131), channel_id=1, source_target_pairs={{0,48},{8,56},{16,0},{24,8},{32,16},{40,24},{48,32},{56,40},{64,11... | collective-permute-start | bytes 49160 | tf_op jit(solution)/shard_map/ppermute | solution.py:304
  118.7 3.8 %collective-permute-start.31 = (f32[16,256]{1,0:T(8,128)S(1)}, f32[16,256]{1,0:T(8,128)S(1)}, u32[]{:S(2)}, u32[]{:S(2)}) collective-permute-start(f32[16,256]{1,0:T(8,128)S(1)} %get-tuple-element.132), channel_id=1, source_target_pairs={{0,16},{8,24},{16,32},{24,40},{32,48},{40,56},{48,0},{56,8},{64,80... | collective-permute-start | bytes 49160 | tf_op jit(solution)/shard_map/ppermute | solution.py:304
  118.7 4.1 %collective-permute-start.32 = (f32[16,256]{1,0:T(8,128)S(1)}, f32[16,256]{1,0:T(8,128)S(1)}, u32[]{:S(2)}, u32[]{:S(2)}) collective-permute-start(f32[16,256]{1,0:T(8,128)S(1)} %get-tuple-element.130), channel_id=1, source_target_pairs={{0,32},{8,40},{16,48},{24,56},{32,0},{40,8},{48,16},{56,24},{64,96... | collective-permute-start | bytes 49160 | tf_op jit(solution)/shard_map/ppermute | solution.py:304
  122.8 2.7 collective-permute-start.34
  125.5 4.0 %collective-permute-start.37 = (f32[16,256]{1,0:T(8,128)S(1)}, f32[16,256]{1,0:T(8,128)S(1)}, u32[]{:S(2)}, u32[]{:S(2)}) collective-permute-start(f32[16,256]{1,0:T(8,128)S(1)} %add.228), channel_id=1, source_target_pairs={{0,3},{1,0},{2,1},{3,2},{4,7},{5,4},{6,5},{7,6},{8,11},{9,8},{10,9... | collective-permute-start | bytes 49160 | tf_op jit(solution)/shard_map/ppermute | solution.py:308
  127.8 3.8 %collective-permute-start.35 = (f32[16,256]{1,0:T(8,128)S(1)}, f32[16,256]{1,0:T(8,128)S(1)}, u32[]{:S(2)}, u32[]{:S(2)}) collective-permute-start(f32[16,256]{1,0:T(8,128)S(1)} %add.228), channel_id=1, source_target_pairs={{0,1},{1,2},{2,3},{3,0},{4,5},{5,6},{6,7},{7,4},{8,9},{9,10},{10,1... | collective-permute-start | bytes 49160 | tf_op jit(solution)/shard_map/ppermute | solution.py:308
  127.8 4.1 %collective-permute-start.36 = (f32[16,256]{1,0:T(8,128)S(1)}, f32[16,256]{1,0:T(8,128)S(1)}, u32[]{:S(2)}, u32[]{:S(2)}) collective-permute-start(f32[16,256]{1,0:T(8,128)S(1)} %add.228), channel_id=1, source_target_pairs={{0,2},{1,3},{2,0},{3,1},{4,6},{5,7},{6,4},{7,5},{8,10},{9,11},{10,... | collective-permute-start | bytes 49160 | tf_op jit(solution)/shard_map/ppermute | solution.py:308
  131.9 4.1 %collective-permute-start.38 = (f32[16,256]{1,0:T(8,128)S(1)}, f32[16,256]{1,0:T(8,128)S(1)}, u32[]{:S(2)}, u32[]{:S(2)}) collective-permute-start(f32[16,256]{1,0:T(8,128)S(1)} %add_add_fusion.1), channel_id=1, source_target_pairs={{0,64},{8,72},{16,80},{24,88},{32,96},{40,104},{48,112},{56,120},{... | collective-permute-start | bytes 49160 | tf_op jit(solution)/shard_map/ppermute | solution.py:304
  136.1 36.5 %collective-permute-start.39 = (f32[32,256]{1,0:T(8,128)S(1)}, f32[32,256]{1,0:T(8,128)S(1)}, u32[]{:S(2)}, u32[]{:S(2)}) collective-permute-start(f32[32,256]{1,0:T(8,128)S(1)} %get-tuple-element.111), channel_id=1, source_target_pairs={{0,48},{8,56},{16,0},{24,8},{32,16},{40,24},{48,32},{56,40},{64,11... | collective-permute-start | bytes 98312 | tf_op jit(solution)/shard_map/ppermute | solution.py:304
  150.5 87.9 %collective-permute-start.52 = (f32[512,1024]{1,0:T(8,128)}, f32[512,1024]{1,0:T(8,128)}, u32[]{:S(2)}, u32[]{:S(2)}) collective-permute-start(f32[512,1024]{1,0:T(8,128)} %get-tuple-element.101), channel_id=1, source_target_pairs={{0,8},{8,0},{16,24},{24,16},{32,40},{40,32},{48,56},{56,48},{64,72... | collective-permute-start | bytes 6291464 | tf_op jit(solution)/shard_map/ppermute | solution.py:304
  169.6 17.7 %copy-start.3 = (f32[4,64,1024]{2,1,0:T(8,128)}, f32[4,64,1024]{2,1,0:T(8,128)S(1)}, u32[]{:S(2)}) copy-start(f32[4,64,1024]{2,1,0:T(8,128)S(1)} %get-tuple-element.94) | copy-start | bytes 3145732
  169.6 14.3 %collective-permute-start.47 = (f32[2,64,1024]{2,1,0:T(8,128)S(1)}, f32[2,64,1024]{2,1,0:T(8,128)S(1)}, u32[]{:S(2)}, u32[]{:S(2)}) collective-permute-start(f32[2,64,1024]{2,1,0:T(8,128)S(1)} %get-tuple-element.95), channel_id=1, source_target_pairs={{0,3},{1,0},{2,1},{3,2},{4,7},{5,4},{6,5},{7,6},{8,11},{9,8},{10,9... | collective-permute-start | bytes 1572872 | tf_op jit(solution)/shard_map/ppermute | solution.py:308
  172.6 14.7 %collective-permute-start.48 = (f32[2,64,1024]{2,1,0:T(8,128)S(1)}, f32[2,64,1024]{2,1,0:T(8,128)S(1)}, u32[]{:S(2)}, u32[]{:S(2)}) collective-permute-start(f32[2,64,1024]{2,1,0:T(8,128)S(1)} %get-tuple-element.96), channel_id=1, source_target_pairs={{0,1},{1,2},{2,3},{3,0},{4,5},{5,6},{6,7},{7,4},{8,9},{9,10},{10,1... | collective-permute-start | bytes 1572872 | tf_op jit(solution)/shard_map/ppermute | solution.py:308
  172.6 4.4 %collective-permute-start.40 = (f32[32,256]{1,0:T(8,128)S(1)}, f32[32,256]{1,0:T(8,128)S(1)}, u32[]{:S(2)}, u32[]{:S(2)}) collective-permute-start(f32[32,256]{1,0:T(8,128)S(1)} %get-tuple-element.111), channel_id=1, source_target_pairs={{0,32},{8,40},{16,48},{24,56},{32,0},{40,8},{48,16},{56,24},{64,96... | collective-permute-start | bytes 98312 | tf_op jit(solution)/shard_map/ppermute | solution.py:304
  172.6 4.7 %collective-permute-start.41 = (f32[32,256]{1,0:T(8,128)S(1)}, f32[32,256]{1,0:T(8,128)S(1)}, u32[]{:S(2)}, u32[]{:S(2)}) collective-permute-start(f32[32,256]{1,0:T(8,128)S(1)} %get-tuple-element.111), channel_id=1, source_target_pairs={{0,16},{8,24},{16,32},{24,40},{32,48},{40,56},{48,0},{56,8},{64,80... | collective-permute-start | bytes 98312 | tf_op jit(solution)/shard_map/ppermute | solution.py:304
  177.4 4.1 %collective-permute-start.42 = (f32[128,256]{1,0:T(8,128)S(1)}, f32[128,256]{1,0:T(8,128)S(1)}, u32[]{:S(2)}, u32[]{:S(2)}) collective-permute-start(f32[128,256]{1,0:T(8,128)S(1)} %constant_dynamic-slice_fusion), channel_id=1, source_target_pairs={{0,8},{8,0},{16,24},{24,16},{32,40},{40,32},{48,56},{56,48},{64,72... | collective-permute-start | bytes 393224 | tf_op jit(solution)/shard_map/ppermute | solution.py:304
  178.6 16.5 %collective-permute-start.43 = (f32[2,64,1024]{2,1,0:T(8,128)S(1)}, f32[2,64,1024]{2,1,0:T(8,128)S(1)}, u32[]{:S(2)}, u32[]{:S(2)}) collective-permute-start(f32[2,64,1024]{2,1,0:T(8,128)S(1)} %get-tuple-element.90), channel_id=1, source_target_pairs={{0,3},{1,0},{2,1},{3,2},{4,7},{5,4},{6,5},{7,6},{8,11},{9,8},{10,9... | collective-permute-start | bytes 1572872 | tf_op jit(solution)/shard_map/ppermute | solution.py:308
  181.5 16.8 %collective-permute-start.44 = (f32[2,64,1024]{2,1,0:T(8,128)S(1)}, f32[2,64,1024]{2,1,0:T(8,128)S(1)}, u32[]{:S(2)}, u32[]{:S(2)}) collective-permute-start(f32[2,64,1024]{2,1,0:T(8,128)S(1)} %get-tuple-element.91), channel_id=1, source_target_pairs={{0,1},{1,2},{2,3},{3,0},{4,5},{5,6},{6,7},{7,4},{8,9},{9,10},{10,1... | collective-permute-start | bytes 1572872 | tf_op jit(solution)/shard_map/ppermute | solution.py:308
  183.9 14.4 %copy-start.5 = (f32[2,64,1024]{2,1,0:T(8,128)}, f32[2,64,1024]{2,1,0:T(8,128)S(1)}, u32[]{:S(2)}) copy-start(f32[2,64,1024]{2,1,0:T(8,128)S(1)} %collective-permute-done.47) | copy-start | bytes 1572868
  183.9 51.3 %collective-permute-start.23 = (f32[2,2,64,1024]{3,2,1,0:T(8,128)}, f32[2,2,64,1024]{3,2,1,0:T(8,128)}, u32[]{:S(2)}, u32[]{:S(2)}) collective-permute-start(f32[2,2,64,1024]{3,2,1,0:T(8,128)} %bitcast.6), channel_id=1, source_target_pairs={{0,3},{1,0},{2,1},{3,2},{4,7},{5,4},{6,5},{7,6},{8,11},{9,8},{10,9... | collective-permute-start | bytes 3145736 | tf_op jit(solution)/shard_map/ppermute | solution.py:308
  187.3 47.9 %collective-permute-start.24 = (f32[2,2,64,1024]{3,2,1,0:T(8,128)}, f32[2,2,64,1024]{3,2,1,0:T(8,128)}, u32[]{:S(2)}, u32[]{:S(2)}) collective-permute-start(f32[2,2,64,1024]{3,2,1,0:T(8,128)} %bitcast.8), channel_id=1, source_target_pairs={{0,1},{1,2},{2,3},{3,0},{4,5},{5,6},{6,7},{7,4},{8,9},{9,10},{10,1... | collective-permute-start | bytes 3145736 | tf_op jit(solution)/shard_map/ppermute | solution.py:308
  195.1 31.3 %collective-permute-start.49 = (f32[64,1024]{1,0:T(8,128)}, f32[64,1024]{1,0:T(8,128)}, u32[]{:S(2)}, u32[]{:S(2)}) collective-permute-start(f32[64,1024]{1,0:T(8,128)} %get-tuple-element.97), channel_id=1, source_target_pairs={{0,1},{1,2},{2,3},{3,0},{4,5},{5,6},{6,7},{7,4},{8,9},{9,10},{10,1... | collective-permute-start | bytes 786440 | tf_op jit(solution)/shard_map/ppermute | solution.py:308
  198.2 28.2 %collective-permute-start.50 = (f32[64,1024]{1,0:T(8,128)}, f32[64,1024]{1,0:T(8,128)}, u32[]{:S(2)}, u32[]{:S(2)}) collective-permute-start(f32[64,1024]{1,0:T(8,128)} %get-tuple-element.98), channel_id=1, source_target_pairs={{0,3},{1,0},{2,1},{3,2},{4,7},{5,4},{6,5},{7,6},{8,11},{9,8},{10,9... | collective-permute-start | bytes 786440 | tf_op jit(solution)/shard_map/ppermute | solution.py:308
  204.8 30.2 %copy-start.8 = (f32[2,64,1024]{2,1,0:T(8,128)S(1)}, f32[2,64,1024]{2,1,0:T(8,128)}, u32[]{:S(2)}) copy-start(f32[2,64,1024]{2,1,0:T(8,128)} %copy-done.7) | copy-start | bytes 1572868
  204.8 30.2 %copy-start.10 = (f32[2,64,1024]{2,1,0:T(8,128)S(1)}, f32[2,64,1024]{2,1,0:T(8,128)}, u32[]{:S(2)}) copy-start(f32[2,64,1024]{2,1,0:T(8,128)} %copy-done.9) | copy-start | bytes 1572868
  226.4 7.9 %collective-permute-start.45 = (f32[64,1024]{1,0:T(8,128)S(1)}, f32[64,1024]{1,0:T(8,128)S(1)}, u32[]{:S(2)}, u32[]{:S(2)}) collective-permute-start(f32[64,1024]{1,0:T(8,128)S(1)} %get-tuple-element.92), channel_id=1, source_target_pairs={{0,1},{1,2},{2,3},{3,0},{4,5},{5,6},{6,7},{7,4},{8,9},{9,10},{10,1... | collective-permute-start | bytes 786440 | tf_op jit(solution)/shard_map/ppermute | solution.py:308
  226.4 8.6 %collective-permute-start.46 = (f32[64,1024]{1,0:T(8,128)S(1)}, f32[64,1024]{1,0:T(8,128)S(1)}, u32[]{:S(2)}, u32[]{:S(2)}) collective-permute-start(f32[64,1024]{1,0:T(8,128)S(1)} %get-tuple-element.93), channel_id=1, source_target_pairs={{0,3},{1,0},{2,1},{3,2},{4,7},{5,4},{6,5},{7,6},{8,11},{9,8},{10,9... | collective-permute-start | bytes 786440 | tf_op jit(solution)/shard_map/ppermute | solution.py:308
  234.4 11.5 %collective-permute-start.51 = (f32[2,64,1024]{2,1,0:T(8,128)S(1)}, f32[2,64,1024]{2,1,0:T(8,128)S(1)}, u32[]{:S(2)}, u32[]{:S(2)}) collective-permute-start(f32[2,64,1024]{2,1,0:T(8,128)S(1)} %pad_maximum_fusion), channel_id=1, source_target_pairs={{0,4},{1,5},{2,6},{3,7},{4,0},{5,1},{6,2},{7,3},{8,12},{9,13},{10,... | collective-permute-start | bytes 1572872 | tf_op jit(solution)/shard_map/ppermute | solution.py:308
  236.5 11.3 %collective-permute-start.26 = (f32[2,64,1024]{2,1,0:T(8,128)S(1)}, f32[2,64,1024]{2,1,0:T(8,128)S(1)}, u32[]{:S(2)}, u32[]{:S(2)}) collective-permute-start(f32[2,64,1024]{2,1,0:T(8,128)S(1)} %get-tuple-element.67), channel_id=1, source_target_pairs={{0,3},{1,0},{2,1},{3,2},{4,7},{5,4},{6,5},{7,6},{8,11},{9,8},{10,9... | collective-permute-start | bytes 1572872 | tf_op jit(solution)/shard_map/ppermute | solution.py:308
  238.3 30.2 %collective-permute-start.25 = (f32[2,64,1024]{2,1,0:T(8,128)S(1)}, f32[2,64,1024]{2,1,0:T(8,128)S(1)}, u32[]{:S(2)}, u32[]{:S(2)}) collective-permute-start(f32[2,64,1024]{2,1,0:T(8,128)S(1)} %get-tuple-element.66), channel_id=1, source_target_pairs={{0,1},{1,2},{2,3},{3,0},{4,5},{5,6},{6,7},{7,4},{8,9},{9,10},{10,1... | collective-permute-start | bytes 1572872 | tf_op jit(solution)/shard_map/ppermute | solution.py:308
  240.2 12.6 %collective-permute-start.55 = (f32[2,64,1024]{2,1,0:T(8,128)S(1)}, f32[2,64,1024]{2,1,0:T(8,128)S(1)}, u32[]{:S(2)}, u32[]{:S(2)}) collective-permute-start(f32[2,64,1024]{2,1,0:T(8,128)S(1)} %bitcast.116), channel_id=1, source_target_pairs={{0,32},{8,40},{16,48},{24,56},{32,0},{40,8},{48,16},{56,24},{64,96... | collective-permute-start | bytes 1572872 | tf_op jit(solution)/shard_map/ppermute | solution.py:304
  240.3 26.1 %collective-permute-start.53 = (f32[2,64,1024]{2,1,0:T(8,128)S(1)}, f32[2,64,1024]{2,1,0:T(8,128)S(1)}, u32[]{:S(2)}, u32[]{:S(2)}) collective-permute-start(f32[2,64,1024]{2,1,0:T(8,128)S(1)} %bitcast.115), channel_id=1, source_target_pairs={{0,16},{8,24},{16,32},{24,40},{32,48},{40,56},{48,0},{56,8},{64,80... | collective-permute-start | bytes 1572872 | tf_op jit(solution)/shard_map/ppermute | solution.py:304
  245.9 20.6 %collective-permute-start.54 = (f32[2,64,1024]{2,1,0:T(8,128)S(1)}, f32[2,64,1024]{2,1,0:T(8,128)S(1)}, u32[]{:S(2)}, u32[]{:S(2)}) collective-permute-start(f32[2,64,1024]{2,1,0:T(8,128)S(1)} %bitcast.114), channel_id=1, source_target_pairs={{0,48},{8,56},{16,0},{24,8},{32,16},{40,24},{48,32},{56,40},{64,11... | collective-permute-start | bytes 1572872 | tf_op jit(solution)/shard_map/ppermute | solution.py:304
  249.0 19.5 %collective-permute-start.27 = (f32[2,64,1024]{2,1,0:T(8,128)S(1)}, f32[2,64,1024]{2,1,0:T(8,128)S(1)}, u32[]{:S(2)}, u32[]{:S(2)}) collective-permute-start(f32[2,64,1024]{2,1,0:T(8,128)S(1)} %fusion.1), channel_id=1, source_target_pairs={{0,4},{1,5},{2,6},{3,7},{4,0},{5,1},{6,2},{7,3},{8,12},{9,13},{10,... | collective-permute-start | bytes 1572872 | tf_op jit(solution)/shard_map/ppermute | solution.py:308
  266.7 8.7 %collective-permute-start.56 = (f32[64,1024]{1,0:T(8,128)S(1)}, f32[64,1024]{1,0:T(8,128)S(1)}, u32[]{:S(2)}, u32[]{:S(2)}) collective-permute-start(f32[64,1024]{1,0:T(8,128)S(1)} %slice_bitcast_fusion.4), channel_id=1, source_target_pairs={{0,64},{8,72},{16,80},{24,88},{32,96},{40,104},{48,112},{56,120},{... | collective-permute-start | bytes 786440 | tf_op jit(solution)/shard_map/ppermute | solution.py:304
  (16 other events, 149.9 us)

commit v4 on v2

--- a/solution.py
+++ b/solution.py
@@ -304,7 +304,8 @@
     far_ahead = col_permute(sums[1], 0, 3)
     other = kept[3] + from_behind[1] + far_ahead
     same = kept[2] + from_ahead[1] + far_behind
-    return jnp.transpose(same + col_permute(other, 1, 0), (1, 0, 2))
+    last = col_permute(other, 1, 0)
+    return jnp.transpose(same + last, (1, 0, 2))
 
 
 def dense(value):
@@ -377,7 +378,8 @@
 
     part = corner(0) + sum(row_permute(corner(k), k & 1, 0, k >> 1) for k in (1, 2, 3))
     part = part.reshape(4, 16, 256)
-    part = take(part, ahead[0]) + sum(row_permute(take(part, ahead[k]), 0, k, 0) for k in (1, 2, 3))
+    sends = [row_permute(take(part, ahead[k]), 0, k, 0) for k in (1, 2, 3)]
+    part = take(part, ahead[0]) + sum(sends)
     part = part + col_permute(part, 1, 0)
     part = part + sum(col_permute(part, 0, k) for k in (1, 2, 3))
     other = row_permute(part, 1, 0, 0)

time: 244 us -> 244 us (level)
  no operation moved by 1% of the time
where the time goes in v4:
time: 244 us
  waiting for transfers between devices  96.3 us (39%)
  Pallas kernels  62.2 us (25%)
  starting transfers between devices  57.5 us (24%)
  local copies, waits for them, and re-layouts  17.9 us (7%)
  other arithmetic  8.66 us (4%)
    ppermute x39, waiting for transfers between devices, row_permute(): return lax.ppermute(value, 'row', pairs)  65.3 us
    ppermute x39, starting transfers between devices, row_permute(): return lax.ppermute(value, 'row', pairs)  38.6 us
    ppermute x14, waiting for transfers between devices, col_permute(): lax.ppermute(value, 'col', [(i, (i // 4 ^ z) * 4 + (i + x) % 4) for i in...  31 us
    ppermute x14, starting transfers between devices, col_permute(): lax.ppermute(value, 'col', [(i, (i // 4 ^ z) * 4 + (i + x) % 4) for i in...  19 us
    pallas_call x1, Pallas kernels, first_call(): pl.pallas_call(first_kernel, out_shape=(SQUARE, SQUARE, jax.ShapeDtypeStr...  15.1 us
    pallas_call x1, Pallas kernels, back_call(): pl.pallas_call(functools.partial(back_kernel, len(pieces)), out_shape=(SQ...  14.2 us
    pallas_call x1, Pallas kernels, edge_call(): pl.pallas_call(functools.partial(edge_kernel, len(pieces)), out_shape=(SQ...  11.6 us
    pallas_call x1, Pallas kernels, right_call(): pl.pallas_call(right_kernel, out_shape=(jax.ShapeDtypeStruct((512, 1024),...  10.8 us
  transfers between devices with their start and end apart: 53, of which 26 were waited for; matrix products, arithmetic and copies ran while one was open for 10% of the time, Pallas kernels for 15%

profile of v4, /device:TPU:26, one launch (start us, length us, event | category | flops | bytes accessed | tf_op | source)
XLA Modules:
  0.0 243.7 jit_solution(8193111440179025720)
XLA Ops:
  0.8 1.6 copy.25
  2.8 3.9 %collective-permute-start = (f32[64,1024]{1,0:T(8,128)S(1)}, f32[64,1024]{1,0:T(8,128)S(1)}, u32[]{:S(2)}, u32[]{:S(2)}) collective-permute-start(f32[64,1024]{1,0:T(8,128)S(1)} %reshape.86.refs_0_), channel_id=1, source_target_pairs={{0,64},{8,72},{16,80},{24,88},{32,96},{40,104},{48,112},{56,120},{... | collective-permute-start | bytes 786440 | tf_op jit(solution)/shard_map/ppermute | solution.py:292
  7.0 1.8 collective-permute-start.10
  8.8 1.2 collective-permute-start.11
  11.3 2.2 collective-permute-done.refs_4_
  13.5 6.0 %collective-permute-done.1 = f32[64,1024]{1,0:T(8,128)S(1)} collective-permute-done((f32[64,1024]{1,0:T(8,128)S(1)}, f32[64,1024]{1,0:T(8,128)S(1)}, u32[]{:S(2)}, u32[]{:S(2)}) %collective-permute-start.1) | collective-permute-done | bytes 262176 | tf_op jit(solution)/shard_map/ppermute | solution.py:292
  19.5 2.2 collective-permute-start.12
  21.7 2.1 collective-permute-start.14
  23.8 3.2 %copy.27 = f32[16,16,16,16]{3,2,1,0:T(8,128)} copy(f32[16,16,16,16]{2,0,1,3:T(8,128)} %bitcast.77) | data formatting | bytes 524288 | tf_op jit(solution)/shard_map/transpose | solution.py:331
  27.0 2.4 %reshape.89.refs_17_.site_matrix_ref = f32[256,256]{1,0:T(8,128)S(1)} reshape(f32[16,16,16,16]{3,2,1,0:T(8,128)} %copy.27) | data formatting | bytes 524288 | tf_op jit(solution)/shard_map/reshape | solution.py:331
  31.2 3.7 %collective-permute-start.2 = (f32[128,1024]{1,0:T(8,128)S(1)}, f32[128,1024]{1,0:T(8,128)S(1)}, u32[]{:S(2)}, u32[]{:S(2)}) collective-permute-start(f32[128,1024]{1,0:T(8,128)S(1)} %constant_dynamic-update-slice_fusion.refs_0_), channel_id=1, source_target_pairs={{0,16},{8,24},{16,32},{24,40},{32,48},{40,56},{48,0},{56,8},{64,80... | collective-permute-start | bytes 1572872 | tf_op jit(solution)/shard_map/ppermute | solution.py:292
  34.8 1.5 collective-permute-start.4
  38.3 7.6 %collective-permute-done.2.refs_1_ = f32[128,1024]{1,0:T(8,128)S(1)} collective-permute-done((f32[128,1024]{1,0:T(8,128)S(1)}, f32[128,1024]{1,0:T(8,128)S(1)}, u32[]{:S(2)}, u32[]{:S(2)}) %collective-permute-start.2) | collective-permute-done | bytes 524320 | tf_op jit(solution)/shard_map/ppermute | solution.py:292
  46.0 11.7 %collective-permute-done.3.refs_2_ = f32[128,1024]{1,0:T(8,128)S(1)} collective-permute-done((f32[128,1024]{1,0:T(8,128)S(1)}, f32[128,1024]{1,0:T(8,128)S(1)}, u32[]{:S(2)}, u32[]{:S(2)}) %collective-permute-start.3) | collective-permute-done | bytes 524320 | tf_op jit(solution)/shard_map/ppermute | solution.py:292
  58.7 2.8 %collective-permute-done.22.refs_15_ = f32[64,1024]{1,0:T(8,128)S(1)} collective-permute-done((f32[64,1024]{1,0:T(8,128)S(1)}, f32[64,1024]{1,0:T(8,128)S(1)}, u32[]{:S(2)}, u32[]{:S(2)}) %collective-permute-start.22) | collective-permute-done | bytes 262176 | tf_op jit(solution)/shard_map/ppermute | solution.py:292
  61.5 14.2 %back.1 = (bf16[1024,1024]{1,0:T(8,128)(2,1)S(1)}, bf16[1024,1024]{1,0:T(8,128)(2,1)S(1)}, bf16[1024,1024]{1,0:T(8,128)(2,1)S(1)}, bf16[1024,1024]{1,0:T(8,128)(...) custom-call(s32[16]{0:T(128)S(1)} %get-tuple-element.47.offsets_ref, ...), custom_call_target="tpu_custom_call" | custom-call | tf_op jit(solution)/shard_map/back/pallas_call | solution.py:202
  75.7 11.6 %edge.1 = (bf16[1024,1024]{1,0:T(8,128)(2,1)S(1)}, bf16[1024,1024]{1,0:T(8,128)(2,1)S(1)}, f32[2,2,64,1024]{3,2,1,0:T(8,128)S(1)}, f32[2,2,64,1024]{3,2,1,0:T(8,128)S(1)}, f32[4,2,64,1024]{3,2,1,0:T(8,128)S(1)}) custom-call(s32[16]{0:T(128)S(1)} %get-tuple-element.44.offsets_ref, s32[8]{0:T(128)S(1)} %and_add_fusion.sources_ref, ...), custom_call_target="tpu_custom_call" | custom-call | tf_op jit(solution)/shard_map/edge/pallas_call | solution.py:222
  87.3 15.1 %first.1 = (bf16[1024,1024]{1,0:T(8,128)(2,1)S(1)}, bf16[1024,1024]{1,0:T(8,128)(2,1)S(1)}, f32[256,256]{1,0:T(8,128)S(1)}) custom-call(f32[1024,1024]{1,0:T(8,128)S(1)} %bitcast.71, bf16[1024,1024]{1,0:T(8,128)(2,1)S(1)} %get-tuple-element.58.right_high_ref, bf16[1024,1024]{1,0:T(8,128)(2,1)S(1)} %get-tuple-element.59.right_low_ref, ...), custom_call_target="tpu_custom_call" | custom-call | tf_op jit(solution)/shard_map/first/pallas_call | solution.py:242
  102.4 1.9 collective-permute-start.30
  104.3 1.5 collective-permute-start.28
  105.9 2.2 collective-permute-done.30
  108.1 2.2 collective-permute-done.28
  110.4 3.2 %collective-permute-start.31 = (f32[16,256]{1,0:T(8,128)S(1)}, f32[16,256]{1,0:T(8,128)S(1)}, u32[]{:S(2)}, u32[]{:S(2)}) collective-permute-start(f32[16,256]{1,0:T(8,128)S(1)} %get-tuple-element.106), channel_id=1, source_target_pairs={{0,16},{8,24},{16,32},{24,40},{32,48},{40,56},{48,0},{56,8},{64,80... | collective-permute-start | bytes 49160 | tf_op jit(solution)/shard_map/ppermute | solution.py:292
  113.6 1.7 collective-permute-done.33
  115.3 3.5 %collective-permute-done.32 = f32[16,256]{1,0:T(8,128)S(1)} collective-permute-done((f32[16,256]{1,0:T(8,128)S(1)}, f32[16,256]{1,0:T(8,128)S(1)}, u32[]{:S(2)}, u32[]{:S(2)}) %collective-permute-start.32) | collective-permute-done | bytes 16416 | tf_op jit(solution)/shard_map/ppermute | solution.py:292
  118.8 1.1 collective-permute-start.34
  120.0 2.7 %collective-permute-done.34 = f32[16,256]{1,0:T(8,128)S(1)} collective-permute-done((f32[16,256]{1,0:T(8,128)S(1)}, f32[16,256]{1,0:T(8,128)S(1)}, u32[]{:S(2)}, u32[]{:S(2)}) %collective-permute-start.34) | collective-permute-done | bytes 16416 | tf_op jit(solution)/shard_map/ppermute | solution.py:296
  123.2 1.5 collective-permute-start.35
  124.7 3.3 %collective-permute-start.36 = (f32[16,256]{1,0:T(8,128)S(1)}, f32[16,256]{1,0:T(8,128)S(1)}, u32[]{:S(2)}, u32[]{:S(2)}) collective-permute-start(f32[16,256]{1,0:T(8,128)S(1)} %add.197), channel_id=1, source_target_pairs={{0,2},{1,3},{2,0},{3,1},{4,6},{5,7},{6,4},{7,5},{8,10},{9,11},{10,... | collective-permute-start | bytes 49160 | tf_op jit(solution)/shard_map/ppermute | solution.py:296
  128.0 1.9 collective-permute-done.36
  129.9 1.7 collective-permute-start.38
  131.6 10.8 %right.1 = (f32[512,1024]{1,0:T(8,128)S(1)}, f32[512,1024]{1,0:T(8,128)}) custom-call(s32[16]{0:T(128)S(1)} %get-tuple-element.79.places_ref, bf16[1024,1024]{1,0:T(8,128)(2,1)S(1)} %get-tuple-element.51.refs_8_.back_high_ref, bf16[1024,1024]{1,0:T(8,128)(2,1)S(1)} %get-tuple-element.52.refs_9_.back_low_ref, f32[1024,1024]{1,0:T(8,128)S(1)} %bitcast.72), custom_call_target="tpu_custom_call" | custom-call | tf_op jit(solution)/shard_map/right/pallas_call | solution.py:272
  142.4 1.5 collective-permute-start.24
  144.5 10.6 %left.1 = (f32[2,2,64,1024]{3,2,1,0:T(8,128)}, f32[2,2,64,1024]{3,2,1,0:T(8,128)}, f32[4,2,64,1024]{3,2,1,0:T(8,128)S(1)}) custom-call(s32[8]{0:T(128)S(1)} %and_add_fusion.sources_ref, bf16[1024,1024]{1,0:T(8,128)(2,1)S(1)} %get-tuple-element.72.second_high_ref, bf16[1024,1024]{1,0:T(8,128)(2,1)S(1)} %get-tuple-element.73.second_low_ref, ...), custom_call_target="tpu_custom_call" | custom-call | tf_op jit(solution)/shard_map/left/pallas_call | solution.py:255
  155.1 1.9 collective-permute-start.44
  157.0 1.5 collective-permute-start.40
  158.4 4.0 %collective-permute-done.40 = f32[32,256]{1,0:T(8,128)S(1)} collective-permute-done((f32[32,256]{1,0:T(8,128)S(1)}, f32[32,256]{1,0:T(8,128)S(1)}, u32[]{:S(2)}, u32[]{:S(2)}) %collective-permute-start.40) | collective-permute-done | bytes 32800 | tf_op jit(solution)/shard_map/ppermute | solution.py:292
  162.4 3.2 %collective-permute-start.41 = (f32[32,256]{1,0:T(8,128)S(1)}, f32[32,256]{1,0:T(8,128)S(1)}, u32[]{:S(2)}, u32[]{:S(2)}) collective-permute-start(f32[32,256]{1,0:T(8,128)S(1)} %get-tuple-element.91), channel_id=1, source_target_pairs={{0,16},{8,24},{16,32},{24,40},{32,48},{40,56},{48,0},{56,8},{64,80... | collective-permute-start | bytes 98312 | tf_op jit(solution)/shard_map/ppermute | solution.py:292
  165.6 1.6 collective-permute-done.41
  168.4 1.9 collective-permute-done.23
  170.3 1.1 fusion.11
  171.4 1.2 collective-permute-start.26
  172.7 2.0 select_n.24
  174.7 3.7 %copy.29 = f32[16,16,16,16]{3,2,1,0:T(8,128)} copy(f32[16,16,16,16]{0,3,1,2:T(8,128)} %bitcast.74) | data formatting | bytes 524288
  179.2 11.8 %collective-permute-done.44 = f32[2,2,64,1024]{3,2,1,0:T(8,128)} collective-permute-done((f32[2,2,64,1024]{3,2,1,0:T(8,128)}, f32[2,2,64,1024]{3,2,1,0:T(8,128)}, u32[]{:S(2)}, u32[]{:S(2)}) %collective-permute-start.44) | collective-permute-done | bytes 1048608 | tf_op jit(solution)/shard_map/ppermute | solution.py:296
  191.0 2.6 %collective-permute-done.43 = f32[2,2,64,1024]{3,2,1,0:T(8,128)} collective-permute-done((f32[2,2,64,1024]{3,2,1,0:T(8,128)}, f32[2,2,64,1024]{3,2,1,0:T(8,128)}, u32[]{:S(2)}, u32[]{:S(2)}) %collective-permute-start.43) | collective-permute-done | bytes 1048608 | tf_op jit(solution)/shard_map/ppermute | solution.py:296
  193.6 1.7 fusion.3
  195.2 1.6 collective-permute-start.46
  196.9 7.9 %collective-permute-done.26 = f32[2,64,1024]{2,1,0:T(8,128)} collective-permute-done((f32[2,64,1024]{2,1,0:T(8,128)}, f32[2,64,1024]{2,1,0:T(8,128)}, u32[]{:S(2)}, u32[]{:S(2)}) %collective-permute-start.26) | collective-permute-done | bytes 524320 | tf_op jit(solution)/shard_map/ppermute | solution.py:296
  204.8 1.2 fusion.10
  206.0 1.1 collective-permute-start.27
  207.1 2.0 slice_add_fusion.1
  209.1 1.8 collective-permute-start.51
  210.9 1.9 collective-permute-start.49
  212.8 2.0 collective-permute-done.46
  215.9 1.8 collective-permute-start.45
  218.9 1.2 copy.28
  220.1 5.3 %collective-permute-done.51 = f32[2,64,1024]{2,1,0:T(8,128)S(1)} collective-permute-done((f32[2,64,1024]{2,1,0:T(8,128)S(1)}, f32[2,64,1024]{2,1,0:T(8,128)S(1)}, u32[]{:S(2)}, u32[]{:S(2)}) %collective-permute-start.51) | collective-permute-done | bytes 524320 | tf_op jit(solution)/shard_map/ppermute | solution.py:292
  225.5 3.8 %collective-permute-done.49 = f32[2,64,1024]{2,1,0:T(8,128)S(1)} collective-permute-done((f32[2,64,1024]{2,1,0:T(8,128)S(1)}, f32[2,64,1024]{2,1,0:T(8,128)S(1)}, u32[]{:S(2)}, u32[]{:S(2)}) %collective-permute-start.49) | collective-permute-done | bytes 524320 | tf_op jit(solution)/shard_map/ppermute | solution.py:292
  229.3 3.9 %collective-permute-done.50 = f32[2,64,1024]{2,1,0:T(8,128)S(1)} collective-permute-done((f32[2,64,1024]{2,1,0:T(8,128)S(1)}, f32[2,64,1024]{2,1,0:T(8,128)S(1)}, u32[]{:S(2)}, u32[]{:S(2)}) %collective-permute-start.50) | collective-permute-done | bytes 524320 | tf_op jit(solution)/shard_map/ppermute | solution.py:292
  233.4 2.5 %collective-permute-start.52 = (f32[64,1024]{1,0:T(8,128)S(1)}, f32[64,1024]{1,0:T(8,128)S(1)}, u32[]{:S(2)}, u32[]{:S(2)}) collective-permute-start(f32[64,1024]{1,0:T(8,128)S(1)} %slice_bitcast_fusion), channel_id=1, source_target_pairs={{0,64},{8,72},{16,80},{24,88},{32,96},{40,104},{48,112},{56,120},{... | collective-permute-start | bytes 786440 | tf_op jit(solution)/shard_map/ppermute | solution.py:292
  235.9 1.2 fusion.7
  237.1 1.2 copy.30
  238.3 4.4 %collective-permute-done.52 = f32[64,1024]{1,0:T(8,128)S(1)} collective-permute-done((f32[64,1024]{1,0:T(8,128)S(1)}, f32[64,1024]{1,0:T(8,128)S(1)}, u32[]{:S(2)}, u32[]{:S(2)}) %collective-permute-start.52) | collective-permute-done | bytes 262176 | tf_op jit(solution)/shard_map/ppermute | solution.py:292
  (122 shorter events, 13.5 us)
Async XLA Ops:
  0.6 10.5 %copy-start.8 = (s32[8]{0:T(128)S(1)}, s32[8]{0:T(128)}, u32[]{:S(2)}) copy-start(s32[8]{0:T(128)} %constant.58.clone) | copy-start | bytes 100
  0.7 10.5 %copy-start.10 = (s32[16]{0:T(128)S(1)}, s32[16]{0:T(128)}, u32[]{:S(2)}) copy-start(s32[16]{0:T(128)} %constant.55.clone) | copy-start | bytes 196
  0.7 10.5 %copy-start.11 = (s32[16]{0:T(128)S(1)}, s32[16]{0:T(128)}, u32[]{:S(2)}) copy-start(s32[16]{0:T(128)} %constant.60.clone) | copy-start | bytes 196
  0.7 10.5 %copy-start.12 = (s32[16]{0:T(128)S(1)}, s32[16]{0:T(128)}, u32[]{:S(2)}) copy-start(s32[16]{0:T(128)} %constant.59.clone) | copy-start | bytes 196
  0.7 10.5 %copy-start.13 = (s32[16]{0:T(128)S(1)}, s32[16]{0:T(128)}, u32[]{:S(2)}) copy-start(s32[16]{0:T(128)} %constant.54.clone) | copy-start | bytes 196
  0.7 10.5 %copy-start.14 = (s32[16]{0:T(128)S(1)}, s32[16]{0:T(128)}, u32[]{:S(2)}) copy-start(s32[16]{0:T(128)} %constant.62) | copy-start | bytes 196
  2.8 10.6 %collective-permute-start = (f32[64,1024]{1,0:T(8,128)S(1)}, f32[64,1024]{1,0:T(8,128)S(1)}, u32[]{:S(2)}, u32[]{:S(2)}) collective-permute-start(f32[64,1024]{1,0:T(8,128)S(1)} %reshape.86.refs_0_), channel_id=1, source_target_pairs={{0,64},{8,72},{16,80},{24,88},{32,96},{40,104},{48,112},{56,120},{... | collective-permute-start | bytes 786440 | tf_op jit(solution)/shard_map/ppermute | solution.py:292
  6.8 14.9 %collective-permute-start.9 = (f32[64,1024]{1,0:T(8,128)S(1)}, f32[64,1024]{1,0:T(8,128)S(1)}, u32[]{:S(2)}, u32[]{:S(2)}) collective-permute-start(f32[64,1024]{1,0:T(8,128)S(1)} %reshape.86.refs_0_), channel_id=1, source_target_pairs={{0,16},{8,24},{16,32},{24,40},{32,48},{40,56},{48,0},{56,8},{64,80... | collective-permute-start | bytes 786440 | tf_op jit(solution)/shard_map/ppermute | solution.py:292
  7.0 14.7 %collective-permute-start.10 = (f32[64,1024]{1,0:T(8,128)S(1)}, f32[64,1024]{1,0:T(8,128)S(1)}, u32[]{:S(2)}, u32[]{:S(2)}) collective-permute-start(f32[64,1024]{1,0:T(8,128)S(1)} %reshape.86.refs_0_), channel_id=1, source_target_pairs={{0,48},{8,56},{16,0},{24,8},{32,16},{40,24},{48,32},{56,40},{64,11... | collective-permute-start | bytes 786440 | tf_op jit(solution)/shard_map/ppermute | solution.py:292
  8.8 15.0 %collective-permute-start.11 = (f32[64,1024]{1,0:T(8,128)S(1)}, f32[64,1024]{1,0:T(8,128)S(1)}, u32[]{:S(2)}, u32[]{:S(2)}) collective-permute-start(f32[64,1024]{1,0:T(8,128)S(1)} %reshape.86.refs_0_), channel_id=1, source_target_pairs={{0,32},{8,40},{16,48},{24,56},{32,0},{40,8},{48,16},{56,24},{64,96... | collective-permute-start | bytes 786440 | tf_op jit(solution)/shard_map/ppermute | solution.py:292
  11.0 8.5 %collective-permute-start.1 = (f32[64,1024]{1,0:T(8,128)S(1)}, f32[64,1024]{1,0:T(8,128)S(1)}, u32[]{:S(2)}, u32[]{:S(2)}) collective-permute-start(f32[64,1024]{1,0:T(8,128)S(1)} %reshape.88), channel_id=1, source_target_pairs={{0,64},{8,72},{16,80},{24,88},{32,96},{40,104},{48,112},{56,120},{... | collective-permute-start | bytes 786440 | tf_op jit(solution)/shard_map/ppermute | solution.py:292
  13.4 16.1 %collective-permute-start.15 = (f32[64,1024]{1,0:T(8,128)S(1)}, f32[64,1024]{1,0:T(8,128)S(1)}, u32[]{:S(2)}, u32[]{:S(2)}) collective-permute-start(f32[64,1024]{1,0:T(8,128)S(1)} %reshape.86.refs_0_), channel_id=1, source_target_pairs={{0,8},{8,0},{16,24},{24,16},{32,40},{40,32},{48,56},{56,48},{64,72... | collective-permute-start | bytes 786440 | tf_op jit(solution)/shard_map/ppermute | solution.py:292
  19.5 11.7 %collective-permute-start.12 = (f32[64,1024]{1,0:T(8,128)S(1)}, f32[64,1024]{1,0:T(8,128)S(1)}, u32[]{:S(2)}, u32[]{:S(2)}) collective-permute-start(f32[64,1024]{1,0:T(8,128)S(1)} %collective-permute-done.refs_4_), channel_id=1, source_target_pairs={{0,16},{8,24},{16,32},{24,40},{32,48},{40,56},{48,0},{56,8},{64,80... | collective-permute-start | bytes 786440 | tf_op jit(solution)/shard_map/ppermute | solution.py:292
  21.7 13.1 %collective-permute-start.13 = (f32[64,1024]{1,0:T(8,128)S(1)}, f32[64,1024]{1,0:T(8,128)S(1)}, u32[]{:S(2)}, u32[]{:S(2)}) collective-permute-start(f32[64,1024]{1,0:T(8,128)S(1)} %collective-permute-done.refs_4_), channel_id=1, source_target_pairs={{0,48},{8,56},{16,0},{24,8},{32,16},{40,24},{48,32},{56,40},{64,11... | collective-permute-start | bytes 786440 | tf_op jit(solution)/shard_map/ppermute | solution.py:292
  21.7 13.1 %collective-permute-start.14 = (f32[64,1024]{1,0:T(8,128)S(1)}, f32[64,1024]{1,0:T(8,128)S(1)}, u32[]{:S(2)}, u32[]{:S(2)}) collective-permute-start(f32[64,1024]{1,0:T(8,128)S(1)} %collective-permute-done.refs_4_), channel_id=1, source_target_pairs={{0,32},{8,40},{16,48},{24,56},{32,0},{40,8},{48,16},{56,24},{64,96... | collective-permute-start | bytes 786440 | tf_op jit(solution)/shard_map/ppermute | solution.py:292
  23.8 12.5 %collective-permute-start.16 = (f32[64,1024]{1,0:T(8,128)S(1)}, f32[64,1024]{1,0:T(8,128)S(1)}, u32[]{:S(2)}, u32[]{:S(2)}) collective-permute-start(f32[64,1024]{1,0:T(8,128)S(1)} %collective-permute-done.9.refs_1_), channel_id=1, source_target_pairs={{0,8},{8,0},{16,24},{24,16},{32,40},{40,32},{48,56},{56,48},{64,72... | collective-permute-start | bytes 786440 | tf_op jit(solution)/shard_map/ppermute | solution.py:292
  29.5 6.8 %collective-permute-start.17 = (f32[64,1024]{1,0:T(8,128)S(1)}, f32[64,1024]{1,0:T(8,128)S(1)}, u32[]{:S(2)}, u32[]{:S(2)}) collective-permute-start(f32[64,1024]{1,0:T(8,128)S(1)} %collective-permute-done.10.refs_2_), channel_id=1, source_target_pairs={{0,8},{8,0},{16,24},{24,16},{32,40},{40,32},{48,56},{56,48},{64,72... | collective-permute-start | bytes 786440 | tf_op jit(solution)/shard_map/ppermute | solution.py:292
  31.2 14.8 %collective-permute-start.2 = (f32[128,1024]{1,0:T(8,128)S(1)}, f32[128,1024]{1,0:T(8,128)S(1)}, u32[]{:S(2)}, u32[]{:S(2)}) collective-permute-start(f32[128,1024]{1,0:T(8,128)S(1)} %constant_dynamic-update-slice_fusion.refs_0_), channel_id=1, source_target_pairs={{0,16},{8,24},{16,32},{24,40},{32,48},{40,56},{48,0},{56,8},{64,80... | collective-permute-start | bytes 1572872 | tf_op jit(solution)/shard_map/ppermute | solution.py:292
  34.8 22.9 %collective-permute-start.3 = (f32[128,1024]{1,0:T(8,128)S(1)}, f32[128,1024]{1,0:T(8,128)S(1)}, u32[]{:S(2)}, u32[]{:S(2)}) collective-permute-start(f32[128,1024]{1,0:T(8,128)S(1)} %constant_dynamic-update-slice_fusion.refs_0_), channel_id=1, source_target_pairs={{0,48},{8,56},{16,0},{24,8},{32,16},{40,24},{48,32},{56,40},{64,11... | collective-permute-start | bytes 1572872 | tf_op jit(solution)/shard_map/ppermute | solution.py:292
  34.8 22.9 %collective-permute-start.4 = (f32[128,1024]{1,0:T(8,128)S(1)}, f32[128,1024]{1,0:T(8,128)S(1)}, u32[]{:S(2)}, u32[]{:S(2)}) collective-permute-start(f32[128,1024]{1,0:T(8,128)S(1)} %constant_dynamic-update-slice_fusion.refs_0_), channel_id=1, source_target_pairs={{0,32},{8,40},{16,48},{24,56},{32,0},{40,8},{48,16},{56,24},{64,96... | collective-permute-start | bytes 1572872 | tf_op jit(solution)/shard_map/ppermute | solution.py:292
  36.3 1.5 collective-permute-start.18
  36.3 1.9 collective-permute-start.19
  37.8 20.4 %collective-permute-start.20 = (f32[64,1024]{1,0:T(8,128)S(1)}, f32[64,1024]{1,0:T(8,128)S(1)}, u32[]{:S(2)}, u32[]{:S(2)}) collective-permute-start(f32[64,1024]{1,0:T(8,128)S(1)} %collective-permute-done.12.refs_5_), channel_id=1, source_target_pairs={{0,8},{8,0},{16,24},{24,16},{32,40},{40,32},{48,56},{56,48},{64,72... | collective-permute-start | bytes 786440 | tf_op jit(solution)/shard_map/ppermute | solution.py:292
  38.2 20.1 %collective-permute-start.21 = (f32[64,1024]{1,0:T(8,128)S(1)}, f32[64,1024]{1,0:T(8,128)S(1)}, u32[]{:S(2)}, u32[]{:S(2)}) collective-permute-start(f32[64,1024]{1,0:T(8,128)S(1)} %collective-permute-done.13.refs_6_), channel_id=1, source_target_pairs={{0,8},{8,0},{16,24},{24,16},{32,40},{40,32},{48,56},{56,48},{64,72... | collective-permute-start | bytes 786440 | tf_op jit(solution)/shard_map/ppermute | solution.py:292
  46.0 29.7 %collective-permute-start.5 = (f32[128,1024]{1,0:T(8,128)S(1)}, f32[128,1024]{1,0:T(8,128)S(1)}, u32[]{:S(2)}, u32[]{:S(2)}) collective-permute-start(f32[128,1024]{1,0:T(8,128)S(1)} %constant_dynamic-update-slice_fusion.refs_0_), channel_id=1, source_target_pairs={{0,8},{8,0},{16,24},{24,16},{32,40},{40,32},{48,56},{56,48},{64,72... | collective-permute-start | bytes 1572872 | tf_op jit(solution)/shard_map/ppermute | solution.py:292
  57.7 18.0 %collective-permute-start.6 = (f32[128,1024]{1,0:T(8,128)S(1)}, f32[128,1024]{1,0:T(8,128)S(1)}, u32[]{:S(2)}, u32[]{:S(2)}) collective-permute-start(f32[128,1024]{1,0:T(8,128)S(1)} %collective-permute-done.2.refs_1_), channel_id=1, source_target_pairs={{0,8},{8,0},{16,24},{24,16},{32,40},{40,32},{48,56},{56,48},{64,72... | collective-permute-start | bytes 1572872 | tf_op jit(solution)/shard_map/ppermute | solution.py:292
  57.7 18.0 %collective-permute-start.7 = (f32[128,1024]{1,0:T(8,128)S(1)}, f32[128,1024]{1,0:T(8,128)S(1)}, u32[]{:S(2)}, u32[]{:S(2)}) collective-permute-start(f32[128,1024]{1,0:T(8,128)S(1)} %collective-permute-done.3.refs_2_), channel_id=1, source_target_pairs={{0,8},{8,0},{16,24},{24,16},{32,40},{40,32},{48,56},{56,48},{64,72... | collective-permute-start | bytes 1572872 | tf_op jit(solution)/shard_map/ppermute | solution.py:292
  58.2 17.5 %collective-permute-start.8 = (f32[128,1024]{1,0:T(8,128)S(1)}, f32[128,1024]{1,0:T(8,128)S(1)}, u32[]{:S(2)}, u32[]{:S(2)}) collective-permute-start(f32[128,1024]{1,0:T(8,128)S(1)} %collective-permute-done.4.refs_3_), channel_id=1, source_target_pairs={{0,8},{8,0},{16,24},{24,16},{32,40},{40,32},{48,56},{56,48},{64,72... | collective-permute-start | bytes 1572872 | tf_op jit(solution)/shard_map/ppermute | solution.py:292
  58.3 3.2 %collective-permute-start.22 = (f32[64,1024]{1,0:T(8,128)S(1)}, f32[64,1024]{1,0:T(8,128)S(1)}, u32[]{:S(2)}, u32[]{:S(2)}) collective-permute-start(f32[64,1024]{1,0:T(8,128)S(1)} %collective-permute-done.14.refs_7_), channel_id=1, source_target_pairs={{0,8},{8,0},{16,24},{24,16},{32,40},{40,32},{48,56},{56,48},{64,72... | collective-permute-start | bytes 786440 | tf_op jit(solution)/shard_map/ppermute | solution.py:292
  75.7 11.6 %copy-start = (f32[64,16,1024]{2,1,0:T(8,128)S(1)}, f32[64,16,1024]{2,1,0:T(8,128)}, u32[]{:S(2)}) copy-start(f32[64,16,1024]{2,1,0:T(8,128)} %param.16) | copy-start | bytes 12582916
  87.3 83.0 %copy-start.1 = (f32[4,2,64,1024]{3,2,1,0:T(8,128)}, f32[4,2,64,1024]{3,2,1,0:T(8,128)S(1)}, u32[]{:S(2)}) copy-start(f32[4,2,64,1024]{3,2,1,0:T(8,128)S(1)} %get-tuple-element.53) | copy-start | bytes 6291460
  102.4 5.6 %collective-permute-start.30 = (f32[64,256]{1,0:T(8,128)S(1)}, f32[64,256]{1,0:T(8,128)S(1)}, u32[]{:S(2)}, u32[]{:S(2)}) collective-permute-start(f32[64,256]{1,0:T(8,128)S(1)} %bitcast.89), channel_id=1, source_target_pairs={{0,72},{8,64},{16,88},{24,80},{32,104},{40,96},{48,120},{56,112},{... | collective-permute-start | bytes 196616 | tf_op jit(solution)/shard_map/ppermute | solution.py:292
  104.3 5.9 %collective-permute-start.28 = (f32[64,256]{1,0:T(8,128)S(1)}, f32[64,256]{1,0:T(8,128)S(1)}, u32[]{:S(2)}, u32[]{:S(2)}) collective-permute-start(f32[64,256]{1,0:T(8,128)S(1)} %bitcast.88), channel_id=1, source_target_pairs={{0,64},{8,72},{16,80},{24,88},{32,96},{40,104},{48,112},{56,120},{... | collective-permute-start | bytes 196616 | tf_op jit(solution)/shard_map/ppermute | solution.py:292
  105.8 4.4 %collective-permute-start.29 = (f32[64,256]{1,0:T(8,128)S(1)}, f32[64,256]{1,0:T(8,128)S(1)}, u32[]{:S(2)}, u32[]{:S(2)}) collective-permute-start(f32[64,256]{1,0:T(8,128)S(1)} %bitcast.87), channel_id=1, source_target_pairs={{0,8},{8,0},{16,24},{24,16},{32,40},{40,32},{48,56},{56,48},{64,72... | collective-permute-start | bytes 196616 | tf_op jit(solution)/shard_map/ppermute | solution.py:292
  110.3 5.0 %collective-permute-start.33 = (f32[16,256]{1,0:T(8,128)S(1)}, f32[16,256]{1,0:T(8,128)S(1)}, u32[]{:S(2)}, u32[]{:S(2)}) collective-permute-start(f32[16,256]{1,0:T(8,128)S(1)} %get-tuple-element.105), channel_id=1, source_target_pairs={{0,48},{8,56},{16,0},{24,8},{32,16},{40,24},{48,32},{56,40},{64,11... | collective-permute-start | bytes 49160 | tf_op jit(solution)/shard_map/ppermute | solution.py:292
  110.4 4.9 %collective-permute-start.31 = (f32[16,256]{1,0:T(8,128)S(1)}, f32[16,256]{1,0:T(8,128)S(1)}, u32[]{:S(2)}, u32[]{:S(2)}) collective-permute-start(f32[16,256]{1,0:T(8,128)S(1)} %get-tuple-element.106), channel_id=1, source_target_pairs={{0,16},{8,24},{16,32},{24,40},{32,48},{40,56},{48,0},{56,8},{64,80... | collective-permute-start | bytes 49160 | tf_op jit(solution)/shard_map/ppermute | solution.py:292
  113.6 5.2 %collective-permute-start.32 = (f32[16,256]{1,0:T(8,128)S(1)}, f32[16,256]{1,0:T(8,128)S(1)}, u32[]{:S(2)}, u32[]{:S(2)}) collective-permute-start(f32[16,256]{1,0:T(8,128)S(1)} %get-tuple-element.104), channel_id=1, source_target_pairs={{0,32},{8,40},{16,48},{24,56},{32,0},{40,8},{48,16},{56,24},{64,96... | collective-permute-start | bytes 49160 | tf_op jit(solution)/shard_map/ppermute | solution.py:292
  118.8 3.8 %collective-permute-start.34 = (f32[16,256]{1,0:T(8,128)S(1)}, f32[16,256]{1,0:T(8,128)S(1)}, u32[]{:S(2)}, u32[]{:S(2)}) collective-permute-start(f32[16,256]{1,0:T(8,128)S(1)} %bitcast_add_fusion.1), channel_id=1, source_target_pairs={{0,4},{1,5},{2,6},{3,7},{4,0},{5,1},{6,2},{7,3},{8,12},{9,13},{10,... | collective-permute-start | bytes 49160 | tf_op jit(solution)/shard_map/ppermute | solution.py:296
  122.7 5.4 %collective-permute-start.37 = (f32[16,256]{1,0:T(8,128)S(1)}, f32[16,256]{1,0:T(8,128)S(1)}, u32[]{:S(2)}, u32[]{:S(2)}) collective-permute-start(f32[16,256]{1,0:T(8,128)S(1)} %add.197), channel_id=1, source_target_pairs={{0,3},{1,0},{2,1},{3,2},{4,7},{5,4},{6,5},{7,6},{8,11},{9,8},{10,9... | collective-permute-start | bytes 49160 | tf_op jit(solution)/shard_map/ppermute | solution.py:296
  123.2 4.9 %collective-permute-start.35 = (f32[16,256]{1,0:T(8,128)S(1)}, f32[16,256]{1,0:T(8,128)S(1)}, u32[]{:S(2)}, u32[]{:S(2)}) collective-permute-start(f32[16,256]{1,0:T(8,128)S(1)} %add.197), channel_id=1, source_target_pairs={{0,1},{1,2},{2,3},{3,0},{4,5},{5,6},{6,7},{7,4},{8,9},{9,10},{10,1... | collective-permute-start | bytes 49160 | tf_op jit(solution)/shard_map/ppermute | solution.py:296
  124.7 5.2 %collective-permute-start.36 = (f32[16,256]{1,0:T(8,128)S(1)}, f32[16,256]{1,0:T(8,128)S(1)}, u32[]{:S(2)}, u32[]{:S(2)}) collective-permute-start(f32[16,256]{1,0:T(8,128)S(1)} %add.197), channel_id=1, source_target_pairs={{0,2},{1,3},{2,0},{3,1},{4,6},{5,7},{6,4},{7,5},{8,10},{9,11},{10,... | collective-permute-start | bytes 49160 | tf_op jit(solution)/shard_map/ppermute | solution.py:296
  129.9 14.5 %collective-permute-start.38 = (f32[16,256]{1,0:T(8,128)S(1)}, f32[16,256]{1,0:T(8,128)S(1)}, u32[]{:S(2)}, u32[]{:S(2)}) collective-permute-start(f32[16,256]{1,0:T(8,128)S(1)} %add_add_fusion.1), channel_id=1, source_target_pairs={{0,64},{8,72},{16,80},{24,88},{32,96},{40,104},{48,112},{56,120},{... | collective-permute-start | bytes 49160 | tf_op jit(solution)/shard_map/ppermute | solution.py:292
  142.4 64.7 %collective-permute-start.48 = (f32[512,1024]{1,0:T(8,128)}, f32[512,1024]{1,0:T(8,128)}, u32[]{:S(2)}, u32[]{:S(2)}) collective-permute-start(f32[512,1024]{1,0:T(8,128)} %get-tuple-element.81), channel_id=1, source_target_pairs={{0,8},{8,0},{16,24},{24,16},{32,40},{40,32},{48,56},{56,48},{64,72... | collective-permute-start | bytes 6291464 | tf_op jit(solution)/shard_map/ppermute | solution.py:292
  142.4 26.0 %collective-permute-start.24 = (f32[2,2,64,1024]{3,2,1,0:T(8,128)S(1)}, f32[2,2,64,1024]{3,2,1,0:T(8,128)S(1)}, u32[]{:S(2)}, u32[]{:S(2)}) collective-permute-start(f32[2,2,64,1024]{3,2,1,0:T(8,128)S(1)} %get-tuple-element.55), channel_id=1, source_target_pairs={{0,1},{1,2},{2,3},{3,0},{4,5},{5,6},{6,7},{7,4},{8,9},{9,10},{10,1... | collective-permute-start | bytes 3145736 | tf_op jit(solution)/shard_map/ppermute | solution.py:296
  143.9 26.4 %collective-permute-start.23 = (f32[2,2,64,1024]{3,2,1,0:T(8,128)S(1)}, f32[2,2,64,1024]{3,2,1,0:T(8,128)S(1)}, u32[]{:S(2)}, u32[]{:S(2)}) collective-permute-start(f32[2,2,64,1024]{3,2,1,0:T(8,128)S(1)} %get-tuple-element.54), channel_id=1, source_target_pairs={{0,3},{1,0},{2,1},{3,2},{4,7},{5,4},{6,5},{7,6},{8,11},{9,8},{10,9... | collective-permute-start | bytes 3145736 | tf_op jit(solution)/shard_map/ppermute | solution.py:296
  144.4 12.6 %collective-permute-start.39 = (f32[32,256]{1,0:T(8,128)S(1)}, f32[32,256]{1,0:T(8,128)S(1)}, u32[]{:S(2)}, u32[]{:S(2)}) collective-permute-start(f32[32,256]{1,0:T(8,128)S(1)} %get-tuple-element.91), channel_id=1, source_target_pairs={{0,48},{8,56},{16,0},{24,8},{32,16},{40,24},{48,32},{56,40},{64,11... | collective-permute-start | bytes 98312 | tf_op jit(solution)/shard_map/ppermute | solution.py:292
  155.1 16.3 %copy-start.3 = (f32[4,2,64,1024]{3,2,1,0:T(8,128)}, f32[4,2,64,1024]{3,2,1,0:T(8,128)S(1)}, u32[]{:S(2)}) copy-start(f32[4,2,64,1024]{3,2,1,0:T(8,128)S(1)} %get-tuple-element.76) | copy-start | bytes 6291460
  155.1 35.9 %collective-permute-start.44 = (f32[2,2,64,1024]{3,2,1,0:T(8,128)}, f32[2,2,64,1024]{3,2,1,0:T(8,128)}, u32[]{:S(2)}, u32[]{:S(2)}) collective-permute-start(f32[2,2,64,1024]{3,2,1,0:T(8,128)} %get-tuple-element.78), channel_id=1, source_target_pairs={{0,1},{1,2},{2,3},{3,0},{4,5},{5,6},{6,7},{7,4},{8,9},{9,10},{10,1... | collective-permute-start | bytes 3145736 | tf_op jit(solution)/shard_map/ppermute | solution.py:296
  157.0 5.4 %collective-permute-start.40 = (f32[32,256]{1,0:T(8,128)S(1)}, f32[32,256]{1,0:T(8,128)S(1)}, u32[]{:S(2)}, u32[]{:S(2)}) collective-permute-start(f32[32,256]{1,0:T(8,128)S(1)} %get-tuple-element.91), channel_id=1, source_target_pairs={{0,32},{8,40},{16,48},{24,56},{32,0},{40,8},{48,16},{56,24},{64,96... | collective-permute-start | bytes 98312 | tf_op jit(solution)/shard_map/ppermute | solution.py:292
  162.4 4.8 %collective-permute-start.41 = (f32[32,256]{1,0:T(8,128)S(1)}, f32[32,256]{1,0:T(8,128)S(1)}, u32[]{:S(2)}, u32[]{:S(2)}) collective-permute-start(f32[32,256]{1,0:T(8,128)S(1)} %get-tuple-element.91), channel_id=1, source_target_pairs={{0,16},{8,24},{16,32},{24,40},{32,48},{40,56},{48,0},{56,8},{64,80... | collective-permute-start | bytes 98312 | tf_op jit(solution)/shard_map/ppermute | solution.py:292
  167.2 26.3 %collective-permute-start.43 = (f32[2,2,64,1024]{3,2,1,0:T(8,128)}, f32[2,2,64,1024]{3,2,1,0:T(8,128)}, u32[]{:S(2)}, u32[]{:S(2)}) collective-permute-start(f32[2,2,64,1024]{3,2,1,0:T(8,128)} %get-tuple-element.77), channel_id=1, source_target_pairs={{0,3},{1,0},{2,1},{3,2},{4,7},{5,4},{6,5},{7,6},{8,11},{9,8},{10,9... | collective-permute-start | bytes 3145736 | tf_op jit(solution)/shard_map/ppermute | solution.py:296
  168.4 4.3 %collective-permute-start.42 = (f32[128,256]{1,0:T(8,128)S(1)}, f32[128,256]{1,0:T(8,128)S(1)}, u32[]{:S(2)}, u32[]{:S(2)}) collective-permute-start(f32[128,256]{1,0:T(8,128)S(1)} %constant_dynamic-slice_fusion), channel_id=1, source_target_pairs={{0,8},{8,0},{16,24},{24,16},{32,40},{40,32},{48,56},{56,48},{64,72... | collective-permute-start | bytes 393224 | tf_op jit(solution)/shard_map/ppermute | solution.py:292
  171.4 33.4 %collective-permute-start.26 = (f32[2,64,1024]{2,1,0:T(8,128)}, f32[2,64,1024]{2,1,0:T(8,128)}, u32[]{:S(2)}, u32[]{:S(2)}) collective-permute-start(f32[2,64,1024]{2,1,0:T(8,128)} %get-tuple-element.99), channel_id=1, source_target_pairs={{0,3},{1,0},{2,1},{3,2},{4,7},{5,4},{6,5},{7,6},{8,11},{9,8},{10,9... | collective-permute-start | bytes 1572872 | tf_op jit(solution)/shard_map/ppermute | solution.py:296
  178.4 26.4 %copy-start.2 = (f32[4,2,64,1024]{3,2,1,0:T(8,128)S(1)}, f32[4,2,64,1024]{3,2,1,0:T(8,128)}, u32[]{:S(2)}) copy-start(f32[4,2,64,1024]{3,2,1,0:T(8,128)} %copy-done.1) | copy-start | bytes 6291460
  178.4 26.4 %copy-start.6 = (f32[2,2,64,1024]{3,2,1,0:T(8,128)S(1)}, f32[2,2,64,1024]{3,2,1,0:T(8,128)}, u32[]{:S(2)}) copy-start(f32[2,2,64,1024]{3,2,1,0:T(8,128)} %copy-done.5) | copy-start | bytes 3145732
  178.4 37.5 %collective-permute-start.25 = (f32[2,64,1024]{2,1,0:T(8,128)}, f32[2,64,1024]{2,1,0:T(8,128)S(1)}, u32[]{:S(2)}, u32[]{:S(2)}) collective-permute-start(f32[2,64,1024]{2,1,0:T(8,128)} %get-tuple-element.98), channel_id=1, source_target_pairs={{0,1},{1,2},{2,3},{3,0},{4,5},{5,6},{6,7},{7,4},{8,9},{9,10},{10,1... | collective-permute-start | bytes 1572872 | tf_op jit(solution)/shard_map/ppermute | solution.py:296
  195.2 19.5 %collective-permute-start.46 = (f32[2,64,1024]{2,1,0:T(8,128)S(1)}, f32[2,64,1024]{2,1,0:T(8,128)S(1)}, u32[]{:S(2)}, u32[]{:S(2)}) collective-permute-start(f32[2,64,1024]{2,1,0:T(8,128)S(1)} %get-tuple-element.97), channel_id=1, source_target_pairs={{0,3},{1,0},{2,1},{3,2},{4,7},{5,4},{6,5},{7,6},{8,11},{9,8},{10,9... | collective-permute-start | bytes 1572872 | tf_op jit(solution)/shard_map/ppermute | solution.py:296
  206.0 11.8 %collective-permute-start.27 = (f32[2,64,1024]{2,1,0:T(8,128)S(1)}, f32[2,64,1024]{2,1,0:T(8,128)S(1)}, u32[]{:S(2)}, u32[]{:S(2)}) collective-permute-start(f32[2,64,1024]{2,1,0:T(8,128)S(1)} %fusion.10), channel_id=1, source_target_pairs={{0,4},{1,5},{2,6},{3,7},{4,0},{5,1},{6,2},{7,3},{8,12},{9,13},{10,... | collective-permute-start | bytes 1572872 | tf_op jit(solution)/shard_map/ppermute | solution.py:296
  209.1 16.4 %collective-permute-start.51 = (f32[2,64,1024]{2,1,0:T(8,128)S(1)}, f32[2,64,1024]{2,1,0:T(8,128)S(1)}, u32[]{:S(2)}, u32[]{:S(2)}) collective-permute-start(f32[2,64,1024]{2,1,0:T(8,128)S(1)} %bitcast.82), channel_id=1, source_target_pairs={{0,32},{8,40},{16,48},{24,56},{32,0},{40,8},{48,16},{56,24},{64,96... | collective-permute-start | bytes 1572872 | tf_op jit(solution)/shard_map/ppermute | solution.py:292
  210.9 18.4 %collective-permute-start.49 = (f32[2,64,1024]{2,1,0:T(8,128)S(1)}, f32[2,64,1024]{2,1,0:T(8,128)S(1)}, u32[]{:S(2)}, u32[]{:S(2)}) collective-permute-start(f32[2,64,1024]{2,1,0:T(8,128)S(1)} %bitcast.81), channel_id=1, source_target_pairs={{0,16},{8,24},{16,32},{24,40},{32,48},{40,56},{48,0},{56,8},{64,80... | collective-permute-start | bytes 1572872 | tf_op jit(solution)/shard_map/ppermute | solution.py:292
  214.8 18.4 %collective-permute-start.50 = (f32[2,64,1024]{2,1,0:T(8,128)S(1)}, f32[2,64,1024]{2,1,0:T(8,128)S(1)}, u32[]{:S(2)}, u32[]{:S(2)}) collective-permute-start(f32[2,64,1024]{2,1,0:T(8,128)S(1)} %bitcast.80), channel_id=1, source_target_pairs={{0,48},{8,56},{16,0},{24,8},{32,16},{40,24},{48,32},{56,40},{64,11... | collective-permute-start | bytes 1572872 | tf_op jit(solution)/shard_map/ppermute | solution.py:292
  215.9 20.0 %collective-permute-start.45 = (f32[2,64,1024]{2,1,0:T(8,128)S(1)}, f32[2,64,1024]{2,1,0:T(8,128)S(1)}, u32[]{:S(2)}, u32[]{:S(2)}) collective-permute-start(f32[2,64,1024]{2,1,0:T(8,128)S(1)} %get-tuple-element.96), channel_id=1, source_target_pairs={{0,1},{1,2},{2,3},{3,0},{4,5},{5,6},{6,7},{7,4},{8,9},{9,10},{10,1... | collective-permute-start | bytes 1572872 | tf_op jit(solution)/shard_map/ppermute | solution.py:296
  217.7 18.2 %collective-permute-start.47 = (f32[2,64,1024]{2,1,0:T(8,128)S(1)}, f32[2,64,1024]{2,1,0:T(8,128)S(1)}, u32[]{:S(2)}, u32[]{:S(2)}) collective-permute-start(f32[2,64,1024]{2,1,0:T(8,128)S(1)} %fusion.2), channel_id=1, source_target_pairs={{0,4},{1,5},{2,6},{3,7},{4,0},{5,1},{6,2},{7,3},{8,12},{9,13},{10,... | collective-permute-start | bytes 1572872 | tf_op jit(solution)/shard_map/ppermute | solution.py:296
  233.4 9.4 %collective-permute-start.52 = (f32[64,1024]{1,0:T(8,128)S(1)}, f32[64,1024]{1,0:T(8,128)S(1)}, u32[]{:S(2)}, u32[]{:S(2)}) collective-permute-start(f32[64,1024]{1,0:T(8,128)S(1)} %slice_bitcast_fusion), channel_id=1, source_target_pairs={{0,64},{8,72},{16,80},{24,88},{32,96},{40,104},{48,112},{56,120},{... | collective-permute-start | bytes 786440 | tf_op jit(solution)/shard_map/ppermute | solution.py:292
  (6 other events, 52.8 us)
